TPU v7x, 32 devices: a whole 2x2x4 slice. The times are simulated.
32 devices in a mesh: dp: 16 (over z, x, core), seq: 2 (over y).
Axes of the slice: x: 2, y: 2, z: 4, core: 2. Of those that a mesh axis runs over, the one named last changes fastest.
Arguments:
- tokens: bfloat16 [32, 512, 768], P('dp', 'seq'), may hold values from -6 to 6
- cotangent: bfloat16 [32, 512, 768], P('dp', 'seq'), may hold values from -6 to 6
- lengths: int32 [32], P('dp'), may hold values from 1 to 512, 12288 in all
- query_weight: bfloat16 [768, 768], replicated, may hold values from -0.21875 to 0.21875
- query_bias: float32 [768], replicated, may hold values from -1.2 to 1.2
- key_weight: bfloat16 [768, 768], replicated, may hold values from -0.21875 to 0.21875
- value_weight: bfloat16 [768, 768], replicated, may hold values from -0.21875 to 0.21875
- value_bias: float32 [768], replicated, may hold values from -0.3 to 0.3
- mixer_weight: bfloat16 [768, 768], replicated, may hold values from -3.5 to 3.5
- mixer_bias: float32 [768], replicated, may hold values from -1.2 to 1.2
- first_gain: float32 [768], replicated, may hold values from 0.25 to 1.75
- first_bias: float32 [768], replicated, may hold values from -1.2 to 1.2
- inner_weight: bfloat16 [768, 3072], replicated, may hold values from -0.21875 to 0.21875
- inner_bias: float32 [3072], replicated, may hold values from -1.2 to 1.2
- outer_weight: bfloat16 [3072, 768], replicated, may hold values from -0.109375 to 0.109375
- outer_bias: float32 [768], replicated, may hold values from -1.2 to 1.2
- second_gain: float32 [768], replicated, may hold values from 0.25 to 1.75
- second_bias: float32 [768], replicated, may hold values from -1.2 to 1.2
Outputs:
- layer_output: float32 [32, 512, 768], P('dp', 'seq')
- input_gradient: float32 [32, 512, 768], P('dp', 'seq')
- weight_query: float32 [768, 768], P('dp', 'seq')
- weight_key: float32 [768, 768], P('dp', 'seq')
- weight_value: float32 [768, 768], P('dp', 'seq')
- weight_mixer: float32 [768, 768], P('dp', 'seq')
- weight_inner: float32 [768, 3072], P('dp', 'seq')
- weight_outer: float32 [3072, 768], P('dp', 'seq')
- bias_query: float32 [768], replicated
- bias_value: float32 [768], replicated
- bias_mixer: float32 [768], replicated
- bias_inner: float32 [3072], replicated
- bias_outer: float32 [768], replicated
- gain_first: float32 [768], replicated
- bias_first: float32 [768], replicated
- gain_second: float32 [768], replicated
- bias_second: float32 [768], replicated
Inputs may be any that keep to these rules, and one draw needn't show every extreme that they name: `lengths`: positions from a slot's length to 511 are padding; some slot has exactly 512 tokens.
All inputs are finite; a program needn't handle non-finite values. No bound on the sum of `lengths` on one device may be relied on, other than what follows from the above.
Results may differ from a plain program's by a relative error of at most 0.017.
Values may be sent and summed in bfloat16 or wider, within the bound.
No kernel may reach another device: no remote copies, remote signals or barrier semaphores. Data moves between devices by JAX's collectives and lax.ppermute only.
A program may use at most 192 MiB of HBM per device.

v0:
```python
import math

import jax
import jax.numpy as jnp
from jax import lax
from jax.sharding import PartitionSpec as P

HEADS = 12


gelu_scale = math.sqrt(2.0 / math.pi)


def normalize(residue, gain, shift):
    average = jnp.mean(residue, -1, keepdims=True)
    centred = residue - average
    variance = jnp.mean(centred * centred, -1, keepdims=True)
    return centred * lax.rsqrt(variance + 1e-05) * gain + shift


def smooth(pre_act):
    return (
        0.5
        * pre_act
        * (1.0 + jnp.tanh(gelu_scale * (pre_act + 0.044715 * pre_act * pre_act * pre_act)))
    )


def product(left, right):
    return jnp.dot(left, right, preferred_element_type=jnp.float32)


def across(left, right):
    return lax.dot_general(
        left, right, (((0,), (0,)), ((), ())), preferred_element_type=jnp.float32
    )


def against(left, right):
    return lax.dot_general(
        left, right, (((1,), (1,)), ((), ())), preferred_element_type=jnp.float32
    )


def column_sums(matrix):
    return jnp.sum(matrix.astype(jnp.float32), 0)


def local(
    tokens,
    cotangent,
    lengths,
    query_weight,
    query_bias,
    key_weight,
    value_weight,
    value_bias,
    mixer_weight,
    mixer_bias,
    first_gain,
    first_bias,
    inner_weight,
    inner_bias,
    outer_weight,
    outer_bias,
    second_gain,
    second_bias,
):
    slots, own_length, breadth = tokens.shape
    head_count = HEADS
    head_width = breadth // head_count
    token_rows = tokens.reshape(slots * own_length, breadth)
    queries = (product(token_rows, query_weight) + query_bias).astype(jnp.bfloat16)
    own_keys = (
        product(token_rows, key_weight).astype(jnp.bfloat16).reshape(slots, own_length, breadth)
    )
    own_values = (
        (product(token_rows, value_weight) + value_bias)
        .astype(jnp.bfloat16)
        .reshape(slots, own_length, breadth)
    )
    all_keys, all_values = (
        lax.all_gather(own_keys, "seq", axis=1, tiled=True),
        lax.all_gather(own_values, "seq", axis=1, tiled=True),
    )
    length = all_keys.shape[1]
    usable = jnp.arange(length, dtype=jnp.int32)[None, :] < lengths[:, None]
    query_heads = queries.reshape(slots, own_length, head_count, head_width)
    key_heads = all_keys.reshape(slots, length, head_count, head_width)
    value_heads = all_values.reshape(slots, length, head_count, head_width)

    def scores_of():
        raw_scores = (
            jnp.einsum(
                "sqhd,skhd->shqk", query_heads, key_heads, preferred_element_type=jnp.float32
            )
            * 0.125
        )
        return jnp.where(usable[:, None, None, :], raw_scores, -1000000000.0)

    masked = scores_of()
    row_top = jnp.max(masked, -1, keepdims=True)
    raised = jnp.exp(masked - row_top)
    totals = jnp.sum(raised, -1, keepdims=True)
    logsum = row_top + jnp.log(totals)
    shares_low = (raised / totals).astype(jnp.bfloat16)
    context = jnp.einsum(
        "shqk,skhd->sqhd", shares_low, value_heads, preferred_element_type=jnp.float32
    )
    context = context.reshape(slots * own_length, breadth).astype(jnp.bfloat16)
    mixed = product(context, mixer_weight) + mixer_bias
    normed_one, first_back = jax.vjp(
        normalize, token_rows.astype(jnp.float32) + mixed, first_gain, first_bias
    )
    normed_low = normed_one.astype(jnp.bfloat16)
    inner_pre = product(normed_low, inner_weight) + inner_bias
    active_f, active_back = jax.vjp(smooth, inner_pre)
    active = active_f.astype(jnp.bfloat16)
    outer_out = product(active, outer_weight) + outer_bias
    layer_output, second_back = jax.vjp(normalize, normed_one + outer_out, second_gain, second_bias)
    tangent = cotangent.reshape(slots * own_length, breadth).astype(jnp.float32)
    slope_second, gain_second, bias_second = second_back(tangent)
    second_low = slope_second.astype(jnp.bfloat16)
    weight_outer = across(active, second_low)
    bias_outer = column_sums(second_low)
    (slope_active,) = active_back(against(second_low, outer_weight))
    slope_inner = slope_active.astype(jnp.bfloat16)
    weight_inner = across(normed_low, slope_inner)
    bias_inner = column_sums(slope_inner)
    slope_first = slope_second + against(slope_inner, inner_weight)
    slope_mixed, gain_first, bias_first = first_back(slope_first)
    mixed_low = slope_mixed.astype(jnp.bfloat16)
    weight_mixer = across(context, mixed_low)
    bias_mixer = column_sums(mixed_low)
    slope_context = against(mixed_low, mixer_weight).astype(jnp.bfloat16)
    slope_context = slope_context.reshape(slots, own_length, head_count, head_width)
    shares = jnp.exp(scores_of() - logsum)
    slope_shares = jnp.einsum(
        "sqhd,skhd->shqk", slope_context, value_heads, preferred_element_type=jnp.float32
    )
    row_inner = jnp.sum(slope_shares * shares, -1, keepdims=True)
    slope_scores = (shares * (slope_shares - row_inner)).astype(jnp.bfloat16)
    slope_queries = (
        jnp.einsum("shqk,skhd->sqhd", slope_scores, key_heads, preferred_element_type=jnp.float32)
        * 0.125
    )
    slope_queries = slope_queries.reshape(slots * own_length, breadth).astype(jnp.bfloat16)
    key_terms = (
        jnp.einsum("shqk,sqhd->skhd", slope_scores, query_heads, preferred_element_type=jnp.float32)
        * 0.125
    )
    value_terms = jnp.einsum(
        "shqk,sqhd->skhd",
        shares.astype(jnp.bfloat16),
        slope_context,
        preferred_element_type=jnp.float32,
    )
    key_terms = key_terms.reshape(slots, length, breadth)
    value_terms = value_terms.reshape(slots, length, breadth)
    slope_keys, slope_values = (
        lax.psum_scatter(
            key_terms.astype(jnp.bfloat16), "seq", scatter_dimension=1, tiled=True
        ).astype(jnp.float32),
        lax.psum_scatter(
            value_terms.astype(jnp.bfloat16), "seq", scatter_dimension=1, tiled=True
        ).astype(jnp.float32),
    )
    keys_low = slope_keys.reshape(slots * own_length, breadth).astype(jnp.bfloat16)
    values_low = slope_values.reshape(slots * own_length, breadth).astype(jnp.bfloat16)
    weight_query = across(token_rows, slope_queries)
    bias_query = column_sums(slope_queries)
    weight_key = across(token_rows, keys_low)
    weight_value = across(token_rows, values_low)
    bias_value = column_sums(values_low)
    input_gradient = (
        slope_mixed
        + against(slope_queries, query_weight)
        + against(keys_low, key_weight)
        + against(values_low, value_weight)
    )
    part_query, part_key, part_value, part_mixer, part_inner, part_outer = (
        lax.psum_scatter(
            weight_query.astype(jnp.bfloat16), "seq", scatter_dimension=1, tiled=True
        ).astype(jnp.float32),
        lax.psum_scatter(
            weight_key.astype(jnp.bfloat16), "seq", scatter_dimension=1, tiled=True
        ).astype(jnp.float32),
        lax.psum_scatter(
            weight_value.astype(jnp.bfloat16), "seq", scatter_dimension=1, tiled=True
        ).astype(jnp.float32),
        lax.psum_scatter(
            weight_mixer.astype(jnp.bfloat16), "seq", scatter_dimension=1, tiled=True
        ).astype(jnp.float32),
        lax.psum_scatter(
            weight_inner.astype(jnp.bfloat16), "seq", scatter_dimension=1, tiled=True
        ).astype(jnp.float32),
        lax.psum_scatter(
            weight_outer.astype(jnp.bfloat16), "seq", scatter_dimension=1, tiled=True
        ).astype(jnp.float32),
    )
    summed = (
        lax.psum_scatter(part_query, "dp", scatter_dimension=0, tiled=True),
        lax.psum_scatter(part_key, "dp", scatter_dimension=0, tiled=True),
        lax.psum_scatter(part_value, "dp", scatter_dimension=0, tiled=True),
        lax.psum_scatter(part_mixer, "dp", scatter_dimension=0, tiled=True),
        lax.psum_scatter(part_inner, "dp", scatter_dimension=0, tiled=True),
        lax.psum_scatter(part_outer, "dp", scatter_dimension=0, tiled=True),
    )
    vectors = lax.psum(
        (
            bias_query,
            bias_value,
            bias_mixer,
            bias_inner,
            bias_outer,
            gain_first,
            bias_first,
            gain_second,
            bias_second,
        ),
        ("dp", "seq"),
    )
    return (
        layer_output.reshape(slots, own_length, breadth),
        input_gradient.reshape(slots, own_length, breadth),
        summed[0],
        summed[1],
        summed[2],
        summed[3],
        summed[4],
        summed[5],
        vectors[0],
        vectors[1],
        vectors[2],
        vectors[3],
        vectors[4],
        vectors[5],
        vectors[6],
        vectors[7],
        vectors[8],
    )


def solution(mesh):
    placed = (
        P("dp", "seq", None),
        P("dp", "seq", None),
        P("dp"),
        P(),
        P(),
        P(),
        P(),
        P(),
        P(),
        P(),
        P(),
        P(),
        P(),
        P(),
        P(),
        P(),
        P(),
        P(),
    )
    return jax.shard_map(
        local,
        mesh=mesh,
        in_specs=placed,
        out_specs=(
            P("dp", "seq", None),
            P("dp", "seq", None),
            P("dp", "seq"),
            P("dp", "seq"),
            P("dp", "seq"),
            P("dp", "seq"),
            P("dp", "seq"),
            P("dp", "seq"),
            P(),
            P(),
            P(),
            P(),
            P(),
            P(),
            P(),
            P(),
            P(),
        ),
        check_vma=False,
    )
```

profile of v0, /device:TPU:0, one launch (start us, length us, event | category | flops | bytes accessed | tf_op | source)
XLA Modules:
  0.0 814.7 jit_solution(2650582798111291371)
XLA Ops:
  7.3 3.3 convolution_convert_fusion.5
  15.1 25.6 %all-gather.5.cloned.1.call-done = bf16[2,512,768]{2,1,0:T(8,128)(2,1)} async-done(((bf16[2,256,768]{2,1,0:T(8,128)(2,1)}), bf16[2,512,768]{2,1,0:T(8,128)(2,1)}) %all-gather.5.cloned.1.call-update) | async-done | bytes 1572880 | tf_op jit(solution)/shard_map/all_gather | solution.py:83
  50.1 19.9 %all-gather.3.cloned.1.call-done = bf16[2,512,768]{2,1,0:T(8,128)(2,1)} async-done(((bf16[2,256,768]{2,1,0:T(8,128)(2,1)}), bf16[2,512,768]{2,1,0:T(8,128)(2,1)}) %all-gather.3.cloned.1.call-update) | async-done | bytes 1572880 | tf_op jit(solution)/shard_map/all_gather | solution.py:84
  71.8 7.5 fusion.25
  82.2 5.7 fusion.40
  87.9 4.2 fusion.46
  96.7 8.2 %convert_reduce_fusion = (f32[3072]{0:T(1024)}, bf16[512,3072]{1,0:T(8,128)(2,1)S(1)}) fusion(f32[512,3072]{1,0:T(8,128)S(1)} %fusion.40, f32[3072]{0:T(1024)S(1)} %copy-done.38, bf16[512,768]{1,0:T(8,128)(2,1)S(1)} %get-tuple-element.83, bf16[3072,768]{1,0:T(8,128)(2,1)S(1)} %bitcast.128), kind=kOutput, calls=%fused_computation.19 | convolution fusion | flops 2458383360 | bytes 14966784 | tf_op jit(solution)/shard_map/dot_general | solution.py:40
  104.9 3.7 multiply_reduce_fusion.1
  117.6 7.4 fusion.13
  127.7 8.0 multiply_reduce_fusion
  135.8 6.8 multiply_convert_fusion
  152.9 5.4 convert_reduce_fusion.5
  164.9 17.4 %reduce-scatter.25.cloned.1.call-done = bf16[2,256,768]{2,1,0:T(8,128)(2,1)} async-done(((bf16[2,512,768]{2,1,0:T(8,128)(2,1)}), bf16[2,256,768]{2,1,0:T(8,128)(2,1)}) %reduce-scatter.25.cloned.1.call-update) | async-done | bytes 786448 | tf_op jit(solution)/shard_map/reduce_scatter | solution.py:161
  185.3 7.4 convolution_convert_fusion.1
  193.9 8.7 %convolution_convert_fusion = bf16[3072,768]{1,0:T(8,128)(2,1)} fusion(bf16[512,768]{1,0:T(8,128)(2,1)S(1)} %copy-done.17, f32[512,3072]{1,0:T(8,128)} %copy-done.46, f32[3072]{0:T(1024)S(1)} %copy-done.39), kind=kOutput, calls=%fused_computation.24 | convolution fusion | flops 2434007040 | bytes 11808768 | tf_op jit(solution)/shard_map/dot_general | solution.py:34
  202.6 6.7 copy.88
  211.9 18.8 %reduce-scatter.29.cloned.1.call-done = bf16[768,384]{0,1:T(8,128)(2,1)} async-done(((bf16[768,768]{0,1:T(8,128)(2,1)}), bf16[768,384]{0,1:T(8,128)(2,1)}) %reduce-scatter.29.cloned.1.call-update) | async-done | bytes 589840 | tf_op jit(solution)/shard_map/reduce_scatter | solution.py:182
  233.2 21.7 %reduce-scatter.33.cloned.1.call-done = bf16[768,384]{0,1:T(8,128)(2,1)} async-done(((bf16[768,768]{0,1:T(8,128)(2,1)}), bf16[768,384]{0,1:T(8,128)(2,1)}) %reduce-scatter.33.cloned.1.call-update) | async-done | bytes 589840 | tf_op jit(solution)/shard_map/reduce_scatter | solution.py:188
  257.3 21.7 %reduce-scatter.31.cloned.1.call-done = bf16[768,384]{0,1:T(8,128)(2,1)} async-done(((bf16[768,768]{0,1:T(8,128)(2,1)}), bf16[768,384]{0,1:T(8,128)(2,1)}) %reduce-scatter.31.cloned.1.call-update) | async-done | bytes 589840 | tf_op jit(solution)/shard_map/reduce_scatter | solution.py:185
  281.4 60.0 %reduce-scatter.37.cloned.1.call-done = bf16[768,1536]{1,0:T(8,128)(2,1)} async-done(((bf16[768,3072]{1,0:T(8,128)(2,1)}), bf16[768,1536]{1,0:T(8,128)(2,1)}) %reduce-scatter.37.cloned.1.call-update) | async-done | bytes 2359312 | tf_op jit(solution)/shard_map/reduce_scatter | solution.py:194
  341.4 4.4 convert_element_type.203
  345.9 57.8 %reduce-scatter.51.cloned.1.call-done = bf16[384,3072]{1,0:T(8,128)(2,1)} async-done(((bf16[768,3072]{1,0:T(8,128)(2,1)}), bf16[384,3072]{1,0:T(8,128)(2,1)}) %reduce-scatter.51.cloned.1.call-update) | async-done | bytes 2359312
  403.6 4.3 copy.89
  407.9 4.2 convert_element_type.205
  413.5 3.6 fusion.47
  417.3 41.1 %all-reduce = (f32[768]{0:T(1024)}, f32[768]{0:T(1024)}, f32[768]{0:T(1024)}, f32[3072]{0:T(1024)}, f32[768]{0:T(1024)}, /*index=5*/f32[768]{0:T(1024)}, f32[768]{0:T(1024)}, f32[768]{0:T(1024)}, f32[768]{0:T(1024)}) all-reduce(f32[768]{0:T(1024)S(1)} %reduce_sum.216, ...), channel_id=1, replica_groups=mesh['dp'=16,'seq'=2] {'dp','seq'}, use_global_device_ids=true, to_apply=%region_26.27 | all-reduce | flops 9216 | bytes 73728 | tf_op jit(solution)/shard_map/psum | solution.py:209
  462.7 3.3 reduce-scatter.35.cloned.1.call-done
  466.1 61.3 %reduce-scatter.43.cloned.1.call-done = f32[48,384]{1,0:T(8,128)} async-done(((f32[768,384]{1,0:T(8,128)}), f32[48,384]{1,0:T(8,128)}) %reduce-scatter.43.cloned.1.call-update) | async-done | bytes 73744
  527.3 61.4 %reduce-scatter.47.cloned.1.call-done = f32[48,384]{1,0:T(8,128)} async-done(((f32[768,384]{1,0:T(8,128)}), f32[48,384]{1,0:T(8,128)}) %reduce-scatter.47.cloned.1.call-update) | async-done | bytes 73744
  588.7 61.2 %reduce-scatter.45.cloned.1.call-done = f32[48,384]{1,0:T(8,128)} async-done(((f32[768,384]{1,0:T(8,128)}), f32[48,384]{1,0:T(8,128)}) %reduce-scatter.45.cloned.1.call-update) | async-done | bytes 73744
  649.9 78.9 %reduce-scatter.39.cloned.1.call-done = f32[48,1536]{1,0:T(8,128)} async-done(((f32[768,1536]{1,0:T(8,128)}), f32[48,1536]{1,0:T(8,128)}) %reduce-scatter.39.cloned.1.call-update) | async-done | bytes 294928 | tf_op jit(solution)/shard_map/reduce_scatter | solution.py:206
  728.8 79.1 %reduce-scatter.41.cloned.1.call-done = f32[192,384]{1,0:T(8,128)} async-done(((f32[3072,384]{1,0:T(8,128)}), f32[192,384]{1,0:T(8,128)}) %reduce-scatter.41.cloned.1.call-update) | async-done | bytes 294928 | tf_op jit(solution)/shard_map/reduce_scatter | solution.py:207
  (191 shorter events, 71.1 us)
Async XLA Ops:
  7.2 73.1 %copy-start = (bf16[768,768]{1,0:T(8,128)(2,1)S(1)}, bf16[768,768]{1,0:T(8,128)(2,1)}, u32[]{:S(2)}) copy-start(bf16[768,768]{1,0:T(8,128)(2,1)} %param.26) | copy-start | bytes 3538948
  7.2 33.5 %all-gather.5.cloned.1.call-start = ((), (), s32[]{:S(2)}) async-start(), calls=%async_computation.15 | async-start | bytes 2359296 | tf_op jit(solution)/shard_map/all_gather | solution.py:83
  10.7 59.4 %all-gather.3.cloned.1.call-start = ((), (), s32[]{:S(2)}) async-start(), calls=%async_computation.14 | async-start | bytes 2359296 | tf_op jit(solution)/shard_map/all_gather | solution.py:84
  12.4 149.1 %reduce-scatter.27.cloned.1.call-start = ((), (), s32[]{:S(2)}) async-start(), calls=%async_computation.17 | async-start | bytes 2359296 | tf_op jit(solution)/shard_map/reduce_scatter | solution.py:164
  71.7 7.5 copy-start.7
  81.4 27.2 %copy-start.8 = (f32[512,768]{1,0:T(8,128)}, f32[512,768]{1,0:T(8,128)S(1)}, u32[]{:S(2)}) copy-start(f32[512,768]{1,0:T(8,128)S(1)} %get-tuple-element.96) | copy-start | bytes 4718596
  81.4 6.5 slice-start
  82.2 26.5 %copy-start.26 = (f32[512]{0:T(512)}, f32[512]{0:T(512)S(1)}, u32[]{:S(2)}) copy-start(f32[512]{0:T(512)S(1)} %fusion.33) | copy-start | bytes 6148
  82.2 5.7 copy-start.38
  82.2 5.7 copy-start.43
  87.9 8.7 %copy-start.46 = (f32[512,3072]{1,0:T(8,128)}, f32[512,3072]{1,0:T(8,128)S(1)}, u32[]{:S(2)}) copy-start(f32[512,3072]{1,0:T(8,128)S(1)} %fusion.40) | copy-start | bytes 18874372
  95.9 9.0 %slice-start.2 = ((s8[4718592]{0:T(1024)(128)(4,1)}), s8[4194304]{0:T(1024)(128)(4,1)S(1)}, s32[]{:S(2)}) async-start(s8[4718592]{0:T(1024)(128)(4,1)} %bitcast.129), calls=%async_computation.32 | async-start | bytes 8388608
  96.7 8.2 %copy-start.16 = (bf16[512,768]{1,0:T(8,128)(2,1)}, bf16[512,768]{1,0:T(8,128)(2,1)S(1)}, u32[]{:S(2)}) copy-start(bf16[512,768]{1,0:T(8,128)(2,1)S(1)} %get-tuple-element.83) | copy-start | bytes 2359300
  96.7 8.2 %slice-start.3 = ((s8[4718592]{0:T(1024)(128)(4,1)}), s8[524288]{0:T(1024)(128)(4,1)S(1)}, s32[]{:S(2)}) async-start(s8[4718592]{0:T(1024)(128)(4,1)} %bitcast.129), calls=%async_computation.33 | async-start | bytes 1048576
  127.7 54.6 %reduce-scatter.25.cloned.1.call-start = ((), (), s32[]{:S(2)}) async-start(), calls=%async_computation.16 | async-start | bytes 2359296 | tf_op jit(solution)/shard_map/reduce_scatter | solution.py:161
  148.4 61.0 %reduce-scatter.49.cloned.1.call-start = ((), (), s32[]{:S(2)}) async-start(), calls=%async_computation.28 | async-start | bytes 1769472
  152.9 77.9 %reduce-scatter.29.cloned.1.call-start = ((), (), s32[]{:S(2)}) async-start(), calls=%async_computation.18 | async-start | bytes 1769472 | tf_op jit(solution)/shard_map/reduce_scatter | solution.py:182
  161.3 93.5 %reduce-scatter.33.cloned.1.call-start = ((), (), s32[]{:S(2)}) async-start(), calls=%async_computation.20 | async-start | bytes 1769472 | tf_op jit(solution)/shard_map/reduce_scatter | solution.py:188
  164.8 20.5 %copy-start.27 = (f32[512]{0:T(512)S(1)}, f32[512]{0:T(512)}, u32[]{:S(2)}) copy-start(f32[512]{0:T(512)} %copy-done.26) | copy-start | bytes 6148
  164.8 20.5 %copy-start.32 = (f32[768]{0:T(1024)S(1)}, f32[768]{0:T(1024)}, u32[]{:S(2)}) copy-start(f32[768]{0:T(1024)} %param.28) | copy-start | bytes 9220
  164.8 20.5 %copy-start.45 = (f32[768]{0:T(1024)S(1)}, f32[768]{0:T(1024)}, u32[]{:S(2)}) copy-start(f32[768]{0:T(1024)} %param.29) | copy-start | bytes 9220
  164.8 114.2 %reduce-scatter.31.cloned.1.call-start = ((), (), s32[]{:S(2)}) async-start(), calls=%async_computation.19 | async-start | bytes 1769472 | tf_op jit(solution)/shard_map/reduce_scatter | solution.py:185
  185.2 156.2 %reduce-scatter.37.cloned.1.call-start = ((), (), s32[]{:S(2)}) async-start(), calls=%async_computation.22 | async-start | bytes 7077888 | tf_op jit(solution)/shard_map/reduce_scatter | solution.py:194
  192.8 210.8 %reduce-scatter.51.cloned.1.call-start = ((), (), s32[]{:S(2)}) async-start(), calls=%async_computation.29 | async-start | bytes 7077888
  209.3 256.8 %reduce-scatter.35.cloned.1.call-start = ((), (), s32[]{:S(2)}) async-start(), calls=%async_computation.21 | async-start | bytes 1253376 | tf_op jit(solution)/shard_map/reduce_scatter | solution.py:205
  211.9 315.4 %reduce-scatter.43.cloned.1.call-start = ((), (), s32[]{:S(2)}) async-start(), calls=%async_computation.25 | async-start | bytes 1253376
  233.1 355.6 %reduce-scatter.47.cloned.1.call-start = ((), (), s32[]{:S(2)}) async-start(), calls=%async_computation.27 | async-start | bytes 1253376
  257.2 392.7 %reduce-scatter.45.cloned.1.call-start = ((), (), s32[]{:S(2)}) async-start(), calls=%async_computation.26 | async-start | bytes 1253376
  281.3 447.5 %reduce-scatter.39.cloned.1.call-start = ((), (), s32[]{:S(2)}) async-start(), calls=%async_computation.23 | async-start | bytes 5013504 | tf_op jit(solution)/shard_map/reduce_scatter | solution.py:206
  345.8 462.1 %reduce-scatter.41.cloned.1.call-start = ((), (), s32[]{:S(2)}) async-start(), calls=%async_computation.24 | async-start | bytes 5013504 | tf_op jit(solution)/shard_map/reduce_scatter | solution.py:207
  413.4 45.0 %copy-start.37 = (bf16[2,256,768]{2,1,0:T(8,128)(2,1)S(1)}, bf16[2,256,768]{2,1,0:T(8,128)(2,1)}, u32[]{:S(2)}) copy-start(bf16[2,256,768]{2,1,0:T(8,128)(2,1)} %reduce-scatter.25.cloned.1.call-done) | copy-start | bytes 2359300
  460.7 347.3 %copy-start.1 = (bf16[768,768]{1,0:T(8,128)(2,1)S(1)}, bf16[768,768]{1,0:T(8,128)(2,1)}, u32[]{:S(2)}) copy-start(bf16[768,768]{1,0:T(8,128)(2,1)} %param.26) | copy-start | bytes 3538948
  (36 other events, 88.3 us)
Sparse Core Ops, SparseCore 0:
  10.7 29.9 all-gather.4
  42.8 27.1 all-gather.2
  127.8 26.1 reduce-scatter.26
  156.1 26.1 reduce-scatter.24
  184.3 21.8 reduce-scatter.48
  208.9 21.8 reduce-scatter.28
  233.0 21.8 reduce-scatter.32
  257.1 21.8 reduce-scatter.30
  281.3 60.0 reduce-scatter.36
  343.5 60.0 reduce-scatter.50
  407.8 58.2 reduce-scatter.34
  470.1 57.1 reduce-scatter.42
  531.5 57.1 reduce-scatter.46
  592.8 57.1 reduce-scatter.44
  654.2 74.5 reduce-scatter.38
  733.1 74.7 reduce-scatter.40
where the time goes:
time: 824 us; the launch traced here: 815 us
  waiting for transfers between devices  588 us (71%)
  matrix products  98.7 us (12%)
  local copies, waits for them, and re-layouts  44.5 us (5%)
  blocking collectives  41.1 us (5%)
  other arithmetic  26.3 us (3%)
  between operations  14.8 us (2%)
    unnamed x21, waiting for transfers between devices  242 us
    reduce_scatter x1, waiting for transfers between devices, local(): lax.psum_scatter(part_outer, 'dp', scatter_dimension=0, tiled=True)  79.1 us
    reduce_scatter x1, waiting for transfers between devices, local(): lax.psum_scatter(part_inner, 'dp', scatter_dimension=0, tiled=True)  78.9 us
    reduce_scatter x1, waiting for transfers between devices, local(): lax.psum_scatter(weight_inner.astype(jnp.bfloat16), 'seq', scatter_dimens...  60 us
    psum x1, blocking collectives, local(): lax.psum((bias_query, bias_value, bias_mixer, bias_inner, bias_outer, gai...  41.1 us
    unnamed x113, local copies, waits for them, and re-layouts  28.8 us
    dot_general x6, matrix products, across(): lax.dot_general(left, right, (((0,), (0,)), ((), ())), preferred_element_...  26 us
    all_gather x1, waiting for transfers between devices, local(): lax.all_gather(own_keys, 'seq', axis=1, tiled=True)  25.6 us
  transfers between devices with their start and end apart: 16, of which 14 were waited for; matrix products, arithmetic and copies ran while one was open for 13% of the time, Pallas kernels for 0%

commit v1 on v0

v1 whole, which is shorter than its diff:
```python
import math

import jax
import jax.numpy as jnp
from jax import lax
from jax.experimental import pallas as pl
from jax.experimental.pallas import tpu as pltpu
from jax.sharding import PartitionSpec as P

HEADS = 12
F32, BF = jnp.float32, jnp.bfloat16
NEG = -1000000000.0
GELU = math.sqrt(2.0 / math.pi)
VMEM_LIMIT = 40 << 20


def nn(a, b):
    return lax.dot_general(a, b, (((1,), (0,)), ((), ())), preferred_element_type=F32)


def nt(a, b):
    return lax.dot_general(a, b, (((1,), (1,)), ((), ())), preferred_element_type=F32)


def tn(a, b):
    return lax.dot_general(a, b, (((0,), (0,)), ((), ())), preferred_element_type=F32)


def shape(dims, dtype):
    return jax.ShapeDtypeStruct(dims, dtype)


def full(dims):
    return pl.BlockSpec(dims, lambda g, s: (0,) * len(dims))


def cols(rows, width):
    return pl.BlockSpec((rows, width), lambda g, s: (0, g))


def rows_of(height, width):
    return pl.BlockSpec((height, width), lambda g, s: (g, 0))


def own_slot(rows, width):
    return pl.BlockSpec((1, rows, width), lambda g, s: (s[0], 0, 0))


def call(body, grid, in_specs, out_specs, out_shape, scratch, name, flops, nbytes, trans=0, aliases=None):
    return pl.pallas_call(
        body,
        grid_spec=pltpu.PrefetchScalarGridSpec(
            num_scalar_prefetch=1,
            grid=grid,
            in_specs=in_specs,
            out_specs=out_specs,
            scratch_shapes=scratch,
        ),
        out_shape=out_shape,
        input_output_aliases=aliases or {},
        compiler_params=pltpu.CompilerParams(vmem_limit_bytes=VMEM_LIMIT),
        cost_estimate=pl.CostEstimate(flops=flops, bytes_accessed=nbytes, transcendentals=trans),
        name=name,
    )


def attn_fwd_body(s, own, rem, wq, wk, wv, bq, bv, wm, mb, g1, b1,
                  q_o, kt_o, v_o, e_o, il_o, ctx_o, n1_o, rs_o, nl_o, xs, mask, acc):
    g = pl.program_id(0)
    half = own.shape[1]
    length = 2 * half

    @pl.when(g == 0)
    def _():
        xs[:half] = own[0]
        xs[half:] = rem[...]
        at = lax.broadcasted_iota(jnp.int32, (length, 128), 0) + s[0] * half
        at = jnp.where(at >= length, at - length, at)
        mask[...] = jnp.where(at < s[1], 0.0, NEG)

    x = xs[...]
    q = (nn(x, wq[...]) + bq[...]).astype(BF) * BF(0.125)
    k = nn(x, wk[...]).astype(BF)
    v = (nn(x, wv[...]) + bv[...]).astype(BF)
    q_o[...] = q
    v_o[...] = v
    qt = q.T
    kt_o[...] = k.T
    vt = v.T
    zero = jnp.zeros((64, length), BF)
    outs = []
    for h in range(4):
        pair = (h // 2) * 128
        qh = qt[h * 64 : h * 64 + 64]
        qa = jnp.concatenate([qh, zero] if h % 2 == 0 else [zero, qh], 0)
        sc = nn(k[:, pair : pair + 128], qa) + mask[:, :1]
        e = jnp.exp(sc - jnp.max(sc, 0, keepdims=True))
        il = 1.0 / jnp.sum(e, 0, keepdims=True)
        low = e.astype(BF)
        e_o[h] = low
        il_o[h] = il
        outs.append(nn(vt[h * 64 : h * 64 + 64], low) * il)
    ctx = jnp.concatenate(outs, 0).astype(BF).T
    ctx_o[...] = ctx
    part = nn(ctx, wm[...])

    @pl.when(g == 0)
    def _():
        acc[...] = part

    @pl.when(g > 0)
    def _():
        acc[...] += part

    @pl.when(g == pl.num_programs(0) - 1)
    def _():
        for i in range(4):
            at = pl.ds(i * 128, 128)
            r = acc[at] + mb[...] + xs[at].astype(F32)
            c = r - jnp.mean(r, -1, keepdims=True)
            rs = lax.rsqrt(jnp.mean(c * c, -1, keepdims=True) + 1e-05)
            n = c * rs
            n1_o[at] = n
            rs_o[at] = rs
            nl_o[at] = (n * g1[...] + b1[...]).astype(BF)


def attn_fwd(s, tokens, rem, wq, wk, wv, bq, bv, wm, mb, g1, b1):
    half, d = rem.shape
    t = 2 * half
    return call(
        attn_fwd_body,
        (d // 256,),
        [own_slot(half, d), full((half, d))]
        + [cols(d, 256)] * 3
        + [cols(1, 256)] * 2
        + [rows_of(256, d)]
        + [full((1, d))] * 3,
        [
            cols(t, 256),
            rows_of(256, t),
            cols(t, 256),
            pl.BlockSpec((4, t, t), lambda g, s: (g, 0, 0)),
            pl.BlockSpec((4, 1, t), lambda g, s: (g, 0, 0)),
            cols(t, 256),
            full((t, d)),
            full((t, 1)),
            full((t, d)),
        ],
        [
            shape((t, d), BF),
            shape((d, t), BF),
            shape((t, d), BF),
            shape((HEADS, t, t), BF),
            shape((HEADS, 1, t), F32),
            shape((t, d), BF),
            shape((t, d), F32),
            shape((t, 1), F32),
            shape((t, d), BF),
        ],
        [pltpu.VMEM((t, d), BF), pltpu.VMEM((t, 128), F32), pltpu.VMEM((t, d), F32)],
        "attn_fwd",
        3_200_000_000,
        18 << 20,
        3 << 20,
    )(s, tokens, rem, wq, wk, wv, bq, bv, wm, mb, g1, b1)


def gelu_both(u):
    u2 = u * u
    a = 0.5 + 0.5 * jnp.tanh(u * (GELU + (GELU * 0.044715) * u2))
    return u * a, a + (2.0 * u) * (a * (1.0 - a)) * (GELU + (3.0 * GELU * 0.044715) * u2)


def norm_back(c, n, rs):
    return rs * (c - jnp.mean(c, -1, keepdims=True) - n * jnp.mean(c * n, -1, keepdims=True))


def mlp_fwd_body(s, nl, wi, bi, wo, bo, n1, g1, b1, g2, b2, cot_own, cot_rem,
                 act_o, dg_o, out_own, out_rem, ss_o, sl_o, vec_o, acc):
    j = pl.program_id(0)
    half = cot_rem.shape[0]
    u = nn(nl[...], wi[...]) + bi[...]
    act, slope = gelu_both(u)
    act = act.astype(BF)
    act_o[...] = act
    dg_o[...] = slope.astype(BF)
    part = nn(act, wo[...])

    @pl.when(j == 0)
    def _():
        acc[...] = part

    @pl.when(j > 0)
    def _():
        acc[...] += part

    @pl.when(j == pl.num_programs(0) - 1)
    def _():
        gain = jnp.zeros((1, nl.shape[1]), F32)
        bias, outer = gain, gain
        for i in range(4):
            at = pl.ds(i * 128, 128)
            r = acc[at] + bo[...] + (n1[at] * g1[...] + b1[...])
            c = r - jnp.mean(r, -1, keepdims=True)
            rs = lax.rsqrt(jnp.mean(c * c, -1, keepdims=True) + 1e-05)
            n = c * rs
            o = n * g2[...] + b2[...]
            if i * 128 < half:
                out_own[0, at] = o
                ct = cot_own[0, at].astype(F32)
            else:
                back = pl.ds(i * 128 - half, 128)
                out_rem[back] = o.astype(BF)
                ct = cot_rem[back].astype(F32)
            gain += jnp.sum(ct * n, 0, keepdims=True)
            bias += jnp.sum(ct, 0, keepdims=True)
            slope2 = norm_back(ct * g2[...], n, rs)
            ss_o[at] = slope2
            low = slope2.astype(BF)
            sl_o[at] = low
            outer += jnp.sum(low.astype(F32), 0, keepdims=True)
        vec_o[0:1] = gain
        vec_o[1:2] = bias
        vec_o[2:3] = outer


def mlp_fwd(s, nl, wi, bi, wo, bo, n1, g1, b1, g2, b2, cot, cot_rem):
    t, d = nl.shape
    ff = wi.shape[1]
    half = t // 2
    w = 512
    return call(
        mlp_fwd_body,
        (ff // w,),
        [full((t, d)), cols(d, w), cols(1, w), rows_of(w, d), full((1, d)), full((t, d))]
        + [full((1, d))] * 4
        + [own_slot(half, d), full((half, d))],
        [cols(t, w), cols(t, w), own_slot(half, d), full((half, d)), full((t, d)), full((t, d)), full((3, d))],
        [
            shape((t, ff), BF),
            shape((t, ff), BF),
            shape((2, half, d), F32),
            shape((half, d), BF),
            shape((t, d), F32),
            shape((t, d), BF),
            shape((3, d), F32),
        ],
        [pltpu.VMEM((t, d), F32)],
        "mlp_fwd",
        4_800_000_000,
        24 << 20,
        2 << 20,
    )(s, nl, wi, bi, wo, bo, n1, g1, b1, g2, b2, cot, cot_rem)


def mlp_bwd_body(s, sl, wo, dg, wi, ss, n1, rs, g1, si_o, sm_o, ml_o, vec_o, bi_o, acc):
    j = pl.program_id(0)
    si = (nt(sl[...], wo[...]) * dg[...].astype(F32)).astype(BF)
    si_o[...] = si
    bi_o[...] = jnp.sum(si.astype(F32), 0, keepdims=True)
    part = nt(si, wi[...])

    @pl.when(j == 0)
    def _():
        acc[...] = part

    @pl.when(j > 0)
    def _():
        acc[...] += part

    @pl.when(j == pl.num_programs(0) - 1)
    def _():
        gain = jnp.zeros((1, sl.shape[1]), F32)
        bias, mixer = gain, gain
        for i in range(4):
            at = pl.ds(i * 128, 128)
            sf = acc[at] + ss[at]
            n = n1[at]
            gain += jnp.sum(sf * n, 0, keepdims=True)
            bias += jnp.sum(sf, 0, keepdims=True)
            sm = norm_back(sf * g1[...], n, rs[at])
            sm_o[at] = sm
            low = sm.astype(BF)
            ml_o[at] = low
            mixer += jnp.sum(low.astype(F32), 0, keepdims=True)
        vec_o[0:1] = gain
        vec_o[1:2] = bias
        vec_o[2:3] = mixer


def mlp_bwd(s, sl, wo, dg, wi, ss, n1, rs, g1):
    t, d = sl.shape
    ff = wi.shape[1]
    w = 512
    return call(
        mlp_bwd_body,
        (ff // w,),
        [full((t, d)), rows_of(w, d), cols(t, w), cols(d, w), full((t, d)), full((t, d)), full((t, 1)), full((1, d))],
        [cols(t, w), full((t, d)), full((t, d)), full((3, d)), cols(1, w)],
        [shape((t, ff), BF), shape((t, d), F32), shape((t, d), BF), shape((3, d), F32), shape((1, ff), F32)],
        [pltpu.VMEM((t, d), F32)],
        "mlp_bwd",
        4_800_000_000,
        20 << 20,
    )(s, sl, wo, dg, wi, ss, n1, rs, g1)


def attn_bwd_body(s, ml, wm, q, kt, v, e, il, ctx, wq, wk, wv, sm, v2, v1, bi,
                  dq_o, dk_o, dv_o, vec_o, own_o, rem_o, acc):
    g = pl.program_id(0)
    t, d = ml.shape
    half = t // 2
    dct = nt(wm[...], ml[...]).astype(BF)
    ctxt = ctx[...].T
    zero = jnp.zeros((64, t), BF)
    lane = lax.broadcasted_iota(jnp.int32, (t, 128), 1)
    dqs, dks, dvs = [], [], []
    for pair in range(2):
        dkp = jnp.zeros((t, 128), F32)
        dvp = dkp
        at = slice(pair * 128, pair * 128 + 128)
        vp, qp = v[:, at], q[:, at]
        for one in range(2):
            h = pair * 2 + one
            sub = slice(h * 64, h * 64 + 64)
            dc = (dct[sub].astype(F32) * il[h]).astype(BF)
            da = jnp.concatenate([dc, zero] if one == 0 else [zero, dc], 0)
            delta = jnp.sum(dc.astype(F32) * ctxt[sub].astype(F32), 0, keepdims=True)
            low = e[h]
            ds = (low.astype(F32) * (nn(vp, da) - delta)).astype(BF)
            keep = (lane < 64) if one == 0 else (lane >= 64)
            dkp += nn(ds, jnp.where(keep, qp, BF(0)))
            dvp += nn(low, da.T)
            dqs.append(nn(kt[sub], ds) * 0.125)
        dks.append(dkp)
        dvs.append(dvp)
    dq = jnp.concatenate(dqs, 0).astype(BF).T
    dk = jnp.concatenate(dks, 1).astype(BF)
    dv = jnp.concatenate(dvs, 1).astype(BF)
    dq_o[...] = dq
    dk_o[...] = dk
    dv_o[...] = dv
    here = pl.ds(pl.multiple_of(g * 256, 256), 256)
    vec_o[0:1, here] = jnp.sum(dq.astype(F32), 0, keepdims=True)
    vec_o[1:2, here] = jnp.sum(dv.astype(F32), 0, keepdims=True)
    part = nt(dq, wq[...]) + nt(dk, wk[...]) + nt(dv, wv[...])

    @pl.when(g == 0)
    def _():
        acc[...] = part + sm[...]
        vec_o[2:5] = v2[...]
        vec_o[5:8] = v1[...]
        for i in range(4):
            vec_o[8 + i : 9 + i] = bi[:, i * d : i * d + d]

    @pl.when(g == 1)
    def _():
        acc[...] += part

    @pl.when(g == 2)
    def _():
        own_o[0] = acc[:half] + part[:half]
        rem_o[...] = (acc[half:] + part[half:]).astype(BF)


def attn_bwd(s, ml, wm, q, kt, v, e, il, ctx, wq, wk, wv, sm, v2, v1, bi):
    t, d = ml.shape
    half = t // 2
    return call(
        attn_bwd_body,
        (d // 256,),
        [
            full((t, d)),
            rows_of(256, d),
            cols(t, 256),
            rows_of(256, t),
            cols(t, 256),
            pl.BlockSpec((4, t, t), lambda g, s: (g, 0, 0)),
            pl.BlockSpec((4, 1, t), lambda g, s: (g, 0, 0)),
            cols(t, 256),
        ]
        + [cols(d, 256)] * 3
        + [full((t, d)), full((3, d)), full((3, d)), full((1, 4 * d))],
        [cols(t, 256)] * 3 + [full((12, d)), own_slot(half, d), full((half, d))],
        [shape((t, d), BF)] * 3 + [shape((12, d), F32), shape((2, half, d), F32), shape((half, d), BF)],
        [pltpu.VMEM((t, d), F32)],
        "attn_bwd",
        5_400_000_000,
        20 << 20,
    )(s, ml, wm, q, kt, v, e, il, ctx, wq, wk, wv, sm, v2, v1, bi)


def place(s, core, rx, ry, z1, z2):
    first = jnp.where(core == 0, rx, ry)
    second = jnp.where(core == 0, ry, rx)
    return first, second, z1 ^ s[4], z2 ^ s[5]


def flush(s, j, tile, outs, sems, jobs):
    copies = []
    for rc, out in enumerate(outs):
        core = s[2] ^ rc
        for n, (row_of, height, col, x, y, z1, z2, at) in enumerate(jobs):
            a, b, c, e = place(s, core, x ^ s[3], y ^ s[0], z1, z2)
            copies.append(
                pltpu.make_async_copy(
                    tile.at[pl.ds(pl.multiple_of(row_of(core), 16), height), pl.ds(col, 384)],
                    out.at[a, b, c, e, pl.ds(at, height)],
                    sems.at[rc * len(jobs) + n],
                )
            )
    return copies


def outer_jobs(j):
    return [
        ((lambda core, x=x: (2 * x + core) * 192), 192, 384 * y, x, y, j & 1, j >> 1, 0)
        for x in range(2)
        for y in range(2)
    ]


def thin_jobs(ys, ats):
    return [
        ((lambda core, r=r: (2 * r + core) * 48), 48, 384 * p, r & 1, ys[p], (r >> 1) & 1, r >> 2, ats[p])
        for r in range(8)
        for p in range(2)
    ]


def run_tiles(s, steps, tiles, sems, outs, compute, jobs_of):
    j = pl.program_id(0)

    def go(step, slot, wait):
        for copy in flush(s, step, tiles.at[slot], outs, sems.at[slot], jobs_of(step)):
            copy.wait() if wait else copy.start()

    slot = lax.rem(j, 2)

    @pl.when(j >= 2)
    def _():
        go(j - 2, slot, True)

    tiles[slot] = compute(j).astype(BF)
    go(j, slot, False)

    @pl.when(j == steps - 1)
    def _():
        if steps > 1:
            go(j - 1, 1 - slot, True)
        go(j, slot, True)


def outer_body(s, act, sl, keep, send, tiles, sems):
    run_tiles(s, 4, tiles, sems, (keep, send), lambda j: tn(act[...], sl[...]), outer_jobs)


def inner_body(s, nl, si, ctx, ml, keep, send, tiles, sems):
    j = pl.program_id(0)

    def jobs_of(step):
        mixer = step == 4
        base = jnp.where(mixer, 4, (step & 1) * 2) * 48
        ys = (jnp.where(mixer, 0, step >> 1), jnp.where(mixer, 1, step >> 1))
        return thin_jobs(ys, (pl.multiple_of(base, 16), pl.multiple_of(jnp.where(mixer, base, base + 48), 16)))

    def compute(_):
        return lax.cond(j == 4, lambda: tn(ctx[...], ml[...]), lambda: tn(nl[...], si[...]))

    run_tiles(s, 5, tiles, sems, (keep, send), compute, jobs_of)


def qkv_body(s, own, rem, dq, dk, dv, keep, send, tiles, sems, xs):
    j = pl.program_id(0)
    half = rem.shape[0]

    @pl.when(j == 0)
    def _():
        xs[:half] = own[0]
        xs[half:] = rem[...]

    def jobs_of(step):
        at = pl.multiple_of(step * 48, 16)
        return thin_jobs((0, 1), (at, at))

    def compute(_):
        b = jnp.where(j == 0, dq[...], jnp.where(j == 1, dk[...], dv[...]))
        return tn(xs[...], b)

    run_tiles(s, 3, tiles, sems, (keep, send), compute, jobs_of)


def weight_call(body, steps, in_specs, height, jobs, name, flops, scratch=()):
    block = (2, 2, 2, 2, height, 384)
    hbm = pl.BlockSpec(memory_space=pl.ANY)
    return call(
        body,
        (steps,),
        in_specs,
        [hbm, hbm],
        [shape(block, BF)] * 2,
        [pltpu.VMEM((2, 768, 768), BF), pltpu.SemaphoreType.DMA((2, 2 * jobs))] + list(scratch),
        name,
        flops,
        10 << 20,
    )


def finish_body(s, recv, whole, out):
    out[0] = recv[...].astype(F32)


def finish(s, recv, whole):
    half, d = recv.shape
    return call(
        finish_body,
        (1,),
        [full((half, d)), pl.BlockSpec(memory_space=pl.ANY)],
        pl.BlockSpec((1, half, d), lambda g, s: (1 - s[0], 0, 0)),
        shape(whole.shape, F32),
        [],
        "finish",
        0,
        1 << 20,
        aliases={2: 0},
    )(s, recv, whole)


def local(n, tokens, cotangent, lengths, query_weight, query_bias, key_weight, value_weight, value_bias,
          mixer_weight, mixer_bias, first_gain, first_bias, inner_weight, inner_bias, outer_weight,
          outer_bias, second_gain, second_bias):
    d = tokens.shape[2]
    low_n = n // 16
    y = lax.axis_index("seq")
    dp = lax.axis_index("dp")
    hi = dp // low_n
    mine = lax.dynamic_index_in_dim(lengths, y, 0, keepdims=False)
    s = jnp.stack([y, mine, hi & 1, (hi >> 1) & 1, (hi >> 2) & 1, (hi >> 3) & 1]).astype(jnp.int32)

    def trade(value, bit):
        if bit == "y":
            return lax.ppermute(value, "seq", [(0, 1), (1, 0)])
        return lax.ppermute(value, "dp", [(i, i ^ (bit * low_n)) for i in range(n)])

    def trade_mixed(value, first):
        pairs = []
        for i in range(n):
            for r in range(2):
                over_x = ((i // low_n) % 2 == 0) == first
                pairs.append((2 * i + r, 2 * (i ^ (2 * low_n)) + r if over_x else 2 * i + 1 - r))
        return lax.ppermute(value, ("dp", "seq"), pairs)

    rem = trade(lax.dynamic_index_in_dim(tokens, 1 - y, 0, keepdims=False), "y")
    cot_rem = trade(lax.dynamic_index_in_dim(cotangent, 1 - y, 0, keepdims=False), "y")

    def row(v):
        return v.reshape(1, -1)

    g1, b1, g2, b2 = row(first_gain), row(first_bias), row(second_gain), row(second_bias)
    q, kt, v, e, il, ctx, n1, rs, nl = attn_fwd(
        s, tokens, rem, query_weight, key_weight, value_weight, row(query_bias), row(value_bias),
        mixer_weight, row(mixer_bias), g1, b1)
    act, dg, out, out_rem, ss, sl, v2 = mlp_fwd(
        s, nl, inner_weight, row(inner_bias), outer_weight, row(outer_bias), n1, g1, b1, g2, b2,
        cotangent, cot_rem)
    t = sl.shape[0]
    half = t // 2
    piece = cols(t, 768)
    hold = full((t, d))

    def reduce(pair, height):
        keep, send = pair
        got = [keep, trade(send, 1)]

        def total(index):
            return sum(a[index[i:]].astype(F32) for a, i in zip(got, (0, 0, 1, 2, 3, 4)))

        for stage in range(4):
            out_going = total((0,) * stage + (1,)).astype(BF)
            got.append((
                lambda u: trade_mixed(u, True),
                lambda u: trade_mixed(u, False),
                lambda u: trade(u, 4),
                lambda u: trade(u, 8),
            )[stage](out_going))
        return total((0, 0, 0, 0))

    outer = reduce(
        weight_call(outer_body, 4, [piece, hold], 192, 4, "weight_outer", 2_400_000_000)(s, act, sl), 192)
    out = finish(s, trade(out_rem, "y"), out)
    si, sm, ml, v1, bi = mlp_bwd(s, sl, outer_weight, dg, inner_weight, ss, n1, rs, g1)
    inner_piece = pl.BlockSpec((t, 768), lambda g, s: (0, jnp.minimum(g, 3)))
    inner = reduce(
        weight_call(inner_body, 5, [hold, inner_piece, hold, hold], 240, 16, "weight_inner", 3_000_000_000)(
            s, nl, si, ctx, ml), 240)
    dq, dk, dv, vec, grad, grad_rem = attn_bwd(
        s, ml, mixer_weight, q, kt, v, e, il, ctx, query_weight, key_weight, value_weight, sm, v2, v1, bi)
    qkv = reduce(
        weight_call(qkv_body, 3, [own_slot(half, d), full((half, d)), hold, hold, hold], 144, 16,
                    "weight_qkv", 1_800_000_000, [pltpu.VMEM((t, d), BF)])(s, tokens, rem, dq, dk, dv), 144)
    grad = finish(s, trade(grad_rem, "y"), grad)
    for swap in (
        lambda u: trade(u, 1),
        lambda u: trade_mixed(u, True),
        lambda u: trade_mixed(u, False),
        lambda u: trade(u, 4),
        lambda u: trade(u, 8),
    ):
        vec = vec + swap(vec)

    inner_own = jnp.concatenate([inner[i * 48 : i * 48 + 48] for i in range(4)], 1)
    weights = [qkv[:48], qkv[48:96], qkv[96:], inner[192:], inner_own, outer]
    step = low_n // 2
    while step >= 1:
        bit = (dp // step) % 2
        rest = []
        for w in weights:
            two = w.reshape(2, w.shape[0] // 2, w.shape[1])
            away = lax.dynamic_index_in_dim(two, 1 - bit, 0, keepdims=False)
            near = lax.dynamic_index_in_dim(two, bit, 0, keepdims=False)
            rest.append(near + lax.ppermute(away, "dp", [(i, i ^ step) for i in range(n)]))
        weights = rest
        vec = vec + lax.ppermute(vec, "dp", [(i, i ^ step) for i in range(n)])
        step //= 2
    return (out, grad, *weights, vec[0], vec[1], vec[7], vec[8:].reshape(-1), vec[4], vec[5], vec[6], vec[2], vec[3])


def solution(mesh):
    split = P("dp", "seq", None)
    block = P("dp", "seq")
    n = mesh.shape["dp"]

    def run(*args):
        return local(n, *args)

    return jax.shard_map(
        run,
        mesh=mesh,
        in_specs=(split, split, P("dp")) + (P(),) * 15,
        out_specs=(split, split) + (block,) * 6 + (P(),) * 9,
        check_vma=False,
    )
```

time: 824 us -> 216 us (0.26)
  waiting for transfers between devices: 588 us -> 53.6 us
  matrix products: 98.7 us -> 0 us
  Pallas kernels: 0 us -> 80.3 us
  blocking collectives: 41.1 us -> 0 us
  starting transfers between devices: 0.84 us -> 35.7 us
  local copies, waits for them, and re-layouts: 44.5 us -> 22.5 us
  between operations: 14.8 us -> 1.03 us
    reduce_scatter x9 -> x0, waiting for transfers between devices: 301 us -> none  [the longest x1 79.1 us: local(): lax.psum_scatter(part_outer, 'dp', scatter_dimension=0, tiled=True)]
    unnamed x21 -> x0, waiting for transfers between devices: 242 us -> none
    dot_general x24 -> x0, matrix products: 98.7 us -> none  [the longest x6 26 us: across(): lax.dot_general(left, right, (((0,), (0,)), ((), ())), preferred_element_...]
    pallas_call x0 -> x9, Pallas kernels: none -> 80.3 us  [the longest x1 15 us: mlp_fwd(): call(mlp_fwd_body, (ff // w,), [full((t, d)), cols(d, w), cols(1, w), row...]
    ppermute x0 -> x24, waiting for transfers between devices: none -> 53.6 us  [the longest x8 39.2 us: trade_mixed(): return lax.ppermute(value, ('dp', 'seq'), pairs)]
    all_gather x2 -> x0, waiting for transfers between devices: 45.5 us -> none  [the longest x1 25.6 us: local(): lax.all_gather(own_keys, 'seq', axis=1, tiled=True)]
    psum x1 -> x0, blocking collectives: 41.1 us -> none  [local(): lax.psum((bias_query, bias_value, bias_mixer, bias_inner, bias_outer, gai...]
    ppermute x0 -> x24, starting transfers between devices: none -> 35.7 us  [the longest x12 17.4 us: trade(): return lax.ppermute(value, 'dp', [(i, i ^ bit * low_n) for i in range(n)])]
  transfers between devices with their start and end apart: 16 -> 24, of which waited for: 14 -> 12; matrix products, arithmetic and copies ran while one was open for 13% -> 14% of each run, Pallas kernels for 0% -> 20%
where the time goes in v1:
time: 216 us; the launch traced here: 215 us
  Pallas kernels  80.3 us (37%)
  waiting for transfers between devices  53.6 us (25%)
  starting transfers between devices  35.7 us (17%)
  local copies, waits for them, and re-layouts  22.5 us (10%)
  other arithmetic  21.3 us (10%)
    ppermute x8, waiting for transfers between devices, trade_mixed(): return lax.ppermute(value, ('dp', 'seq'), pairs)  39.2 us
    ppermute x12, starting transfers between devices, trade(): return lax.ppermute(value, 'dp', [(i, i ^ bit * low_n) for i in range(n)])  17.4 us
    convert_element_type x12, other arithmetic, reduce(): out_going = total((0,) * stage + (1,)).astype(BF)  16.4 us
    pallas_call x1, Pallas kernels, mlp_fwd(): call(mlp_fwd_body, (ff // w,), [full((t, d)), cols(d, w), cols(1, w), row...  15 us
    pallas_call x1, Pallas kernels, attn_bwd(): call(attn_bwd_body, (d // 256,), [full((t, d)), rows_of(256, d), cols(t,...  14.3 us
    pallas_call x1, Pallas kernels, attn_fwd(): call(attn_fwd_body, (d // 256,), [own_slot(half, d), full((half, d))] + [...  13.3 us
    ppermute x12, waiting for transfers between devices, trade(): return lax.ppermute(value, 'dp', [(i, i ^ bit * low_n) for i in range(n)])  13 us
    pallas_call x1, Pallas kernels, local(): weight_call(inner_body, 5, [hold, inner_piece, hold, hold], 240, 16, 'wei...  12.1 us
  transfers between devices with their start and end apart: 24, of which 12 were waited for; matrix products, arithmetic and copies ran while one was open for 14% of the time, Pallas kernels for 20%

profile of v1, /device:TPU:0, one launch (start us, length us, event | category | flops | bytes accessed | tf_op | source)
XLA Modules:
  0.0 214.5 jit_solution(13929943824215201010)
XLA Ops:
  1.7 3.1 %collective-permute-start = (bf16[256,768]{1,0:T(8,128)(2,1)S(1)}, bf16[256,768]{1,0:T(8,128)(2,1)S(1)}, u32[]{:S(2)}, u32[]{:S(2)}) collective-permute-start(bf16[256,768]{1,0:T(8,128)(2,1)S(1)} %dynamic-slice_bitcast_fusion.1), channel_id=1, source_target_pairs={{0,1},{1,0},{2,3},{3,2},{4,5},{5,4},{6,7},{7,6},{8,9},{9,8},{10,11... | collective-permute-start | bytes 1179656 | tf_op jit(solution)/shard_map/ppermute | solution.py:543
  20.9 13.3 %attn_fwd.1 = (bf16[512,768]{1,0:T(8,128)(2,1)S(1)}, bf16[768,512]{1,0:T(8,128)(2,1)S(1)}, bf16[512,768]{1,0:T(8,128)(2,1)S(1)}, bf16[12,512,512]{2,1,0:T(8,128)...) custom-call(s32[6]{0:T(128)S(1)} %stack.24.s, ...), custom_call_target="tpu_custom_call" | custom-call | flops 3200000000 | bytes 18874368 | tf_op jit(solution)/shard_map/attn_fwd/pallas_call | solution.py:131
  35.3 15.0 %mlp_fwd.1 = (bf16[512,3072]{1,0:T(8,128)(2,1)S(1)}, bf16[512,3072]{1,0:T(8,128)(2,1)S(1)}, f32[2,256,768]{2,1,0:T(8,128)}, bf16[256,768]{1,0:T(8,128)(2,1)}, f3...) custom-call(s32[6]{0:T(128)S(1)} %stack.24.s, ...), custom_call_target="tpu_custom_call" | custom-call | flops 4800000000 | bytes 25165824 | tf_op jit(solution)/shard_map/mlp_fwd/pallas_call | solution.py:233
  50.3 1.7 copy-done.16
  52.0 11.2 %mlp_bwd.1 = (bf16[512,3072]{1,0:T(8,128)(2,1)S(1)}, f32[512,768]{1,0:T(8,128)S(1)}, bf16[512,768]{1,0:T(8,128)(2,1)S(1)}, f32[3,768]{1,0:T(4,128)S(1)}, f32[1,3072]{1,0:T(1,128)S(1)}) custom-call(s32[6]{0:T(128)S(1)} %stack.24.s, bf16[512,768]{1,0:T(8,128)(2,1)S(1)} %get-tuple-element.54.sl, bf16[3072,768]{1,0:T(8,128)(2,1)} %wo.3, ...), custom_call_target="tpu_custom_call" | custom-call | flops 4800000000 | bytes 20971520 | tf_op jit(solution)/shard_map/mlp_bwd/pallas_call | solution.py:296
  63.3 12.1 %weight_inner.1 = (bf16[2,2,2,2,240,384]{5,4,3,2,1,0:T(8,128)(2,1)S(1)}, bf16[2,2,2,2,240,384]{5,4,3,2,1,0:T(8,128)(2,1)S(1)}) custom-call(s32[6]{0:T(128)S(1)} %stack.24.s, bf16[512,768]{1,0:T(8,128)(2,1)S(1)} %copy-done.28, bf16[512,3072]{1,0:T(8,128)(2,1)S(1)} %get-tuple-element.76.si, bf16[512,768]{1,0:T(8,128)(2,1)S(1)} %copy-done.25, ...), custom_call_target="tpu_custom_call" | custom-call | flops 3000000000 | bytes 10485760 | tf_op jit(solution)/shard_map/weight_inner/pallas_call | solution.py:595
  76.7 14.3 %attn_bwd.1 = (bf16[512,768]{1,0:T(8,128)(2,1)S(1)}, bf16[512,768]{1,0:T(8,128)(2,1)S(1)}, bf16[512,768]{1,0:T(8,128)(2,1)S(1)}, f32[12,768]{1,0:T(8,128)S(1)}, ...) custom-call(s32[6]{0:T(128)S(1)} %stack.24.s, bf16[512,768]{1,0:T(8,128)(2,1)S(1)} %copy-done.15, ...), custom_call_target="tpu_custom_call" | custom-call | flops 5400000000 | bytes 20971520 | tf_op jit(solution)/shard_map/attn_bwd/pallas_call | solution.py:370
  91.0 5.2 %weight_qkv.1 = (bf16[2,2,2,2,144,384]{5,4,3,2,1,0:T(8,128)(2,1)S(1)}, bf16[2,2,2,2,144,384]{5,4,3,2,1,0:T(8,128)(2,1)S(1)}) custom-call(s32[6]{0:T(128)S(1)} %stack.24.s, bf16[2,256,768]{2,1,0:T(8,128)(2,1)S(1)} %copy-done.4, bf16[256,768]{1,0:T(8,128)(2,1)S(1)} %collective-permute-done.rem, bf16[512,768]{1,0:T(8,128)(2,1)S(1)} %get-tuple-element.71.dq, ...), custom_call_target="tpu_custom_call" | custom-call | flops 1800000000 | bytes 10485760 | tf_op jit(solution)/shard_map/weight_qkv/pallas_call | solution.py:600
  96.8 5.3 %weight_outer.1 = (bf16[2,2,2,2,192,384]{5,4,3,2,1,0:T(8,128)(2,1)S(1)}, bf16[2,2,2,2,192,384]{5,4,3,2,1,0:T(8,128)(2,1)S(1)}) custom-call(s32[6]{0:T(128)S(1)} %stack.24.s, bf16[512,3072]{1,0:T(8,128)(2,1)S(1)} %copy-done.17, bf16[512,768]{1,0:T(8,128)(2,1)S(1)} %get-tuple-element.54.sl), custom_call_target="tpu_custom_call" | custom-call | flops 2400000000 | bytes 10485760 | tf_op jit(solution)/shard_map/weight_outer/pallas_call | solution.py:590
  102.4 2.1 collective-permute-start.5
  104.5 2.9 %fusion = bf16[2,2,2,240,384]{4,3,2,1,0:T(8,128)(2,1)} fusion(bf16[2,2,2,2,240,384]{5,4,3,2,1,0:T(8,128)(2,1)} %collective-permute-done.9, bf16[2,2,2,2,240,384]{5,4,3,2,1,0:T(8,128)(2,1)S(1)} %get-tuple-element.77), kind=kLoop, calls=%fused_computation.3 | loop fusion | flops 2949120 | bytes 4423680 | tf_op jit(solution)/shard_map/convert_element_type | solution.py:580
  111.3 4.3 %collective-permute-done.5 = bf16[2,2,2,144,384]{4,3,2,1,0:T(8,128)(2,1)S(1)} collective-permute-done((bf16[2,2,2,144,384]{4,3,2,1,0:T(8,128)(2,1)S(1)}, bf16[2,2,2,144,384]{4,3,2,1,0:T(8,128)(2,1)S(1)}, u32[]{:S(2)}, u32[]{:S(2)}) %collective-permute-start.5) | collective-permute-done | bytes 884768 | tf_op jit(solution)/shard_map/ppermute | solution.py:552
  116.6 2.0 collective-permute-start.6
  121.4 27.8 %collective-permute-done.20 = f32[12,768]{1,0:T(8,128)S(1)} collective-permute-done((f32[12,768]{1,0:T(8,128)S(1)}, f32[12,768]{1,0:T(8,128)S(1)}, u32[]{:S(2)}, u32[]{:S(2)}) %collective-permute-start.20) | collective-permute-done | bytes 36896 | tf_op jit(solution)/shard_map/ppermute | solution.py:552
  149.3 2.1 collective-permute-start.21
  151.3 2.1 collective-permute-done.21
  153.4 2.1 collective-permute-start.22
  155.5 2.1 collective-permute-done.22
  157.6 3.2 %collective-permute-start.23 = (f32[12,768]{1,0:T(8,128)S(1)}, f32[12,768]{1,0:T(8,128)S(1)}, u32[]{:S(2)}, u32[]{:S(2)}) collective-permute-start(f32[12,768]{1,0:T(8,128)S(1)} %add.262), channel_id=1, source_target_pairs={{0,16},{2,18},{4,20},{6,22},{8,24},{10,26},{12,28},{14,30},{16,0},... | collective-permute-start | bytes 110600 | tf_op jit(solution)/shard_map/ppermute | solution.py:544
  162.9 1.8 collective-permute-start.3
  166.7 1.6 collective-permute-start.7
  168.3 1.6 fusion.3
  170.5 1.6 fusion.1
  174.9 3.1 %collective-permute-start.8 = (bf16[144,384]{1,0:T(8,128)(2,1)S(1)}, bf16[144,384]{1,0:T(8,128)(2,1)S(1)}, u32[]{:S(2)}, u32[]{:S(2)}) collective-permute-start(bf16[144,384]{1,0:T(8,128)(2,1)S(1)} %fusion.13), channel_id=1, source_target_pairs={{0,16},{2,18},{4,20},{6,22},{8,24},{10,26},{12,28},{14,30},{16,0},... | collective-permute-start | bytes 331784 | tf_op jit(solution)/shard_map/ppermute | solution.py:544
  178.6 2.5 %finish.2 = f32[2,256,768]{2,1,0:T(8,128)} custom-call(s32[6]{0:T(128)S(1)} %stack.24.s, bf16[256,768]{1,0:T(8,128)(2,1)} %collective-permute-done.2.recv, f32[2,256,768]{2,1,0:T(8,128)} %get-tuple-element.53.whole), custom_call_target="tpu_custom_call", output_to_operand_aliasing={{}: (2, {})} | custom-call | bytes 1048576 | tf_op jit(solution)/shard_map/finish/pallas_call | solution.py:516
  185.1 1.6 collective-permute-start.17
  186.7 5.0 %collective-permute-done.11 = bf16[2,2,240,384]{3,2,1,0:T(8,128)(2,1)S(1)} collective-permute-done((bf16[2,2,240,384]{3,2,1,0:T(8,128)(2,1)S(1)}, bf16[2,2,240,384]{3,2,1,0:T(8,128)(2,1)S(1)}, u32[]{:S(2)}, u32[]{:S(2)}) %collective-permute-start.11) | collective-permute-done | bytes 737312 | tf_op jit(solution)/shard_map/ppermute | solution.py:552
  193.0 1.6 collective-permute-start.12
  198.0 4.4 %collective-permute-done.12 = bf16[2,240,384]{2,1,0:T(8,128)(2,1)S(1)} collective-permute-done((bf16[2,240,384]{2,1,0:T(8,128)(2,1)S(1)}, bf16[2,240,384]{2,1,0:T(8,128)(2,1)S(1)}, u32[]{:S(2)}, u32[]{:S(2)}) %collective-permute-start.12) | collective-permute-done | bytes 368672 | tf_op jit(solution)/shard_map/ppermute | solution.py:544
  203.5 1.9 collective-permute-start.13
  206.0 1.9 fusion.12
  207.9 4.1 %collective-permute-done.13 = bf16[240,384]{1,0:T(8,128)(2,1)S(1)} collective-permute-done((bf16[240,384]{1,0:T(8,128)(2,1)S(1)}, bf16[240,384]{1,0:T(8,128)(2,1)S(1)}, u32[]{:S(2)}, u32[]{:S(2)}) %collective-permute-start.13) | collective-permute-done | bytes 184352 | tf_op jit(solution)/shard_map/ppermute | solution.py:544
  (127 shorter events, 49.0 us)
Async XLA Ops:
  1.7 13.0 %collective-permute-start = (bf16[256,768]{1,0:T(8,128)(2,1)S(1)}, bf16[256,768]{1,0:T(8,128)(2,1)S(1)}, u32[]{:S(2)}, u32[]{:S(2)}) collective-permute-start(bf16[256,768]{1,0:T(8,128)(2,1)S(1)} %dynamic-slice_bitcast_fusion.1), channel_id=1, source_target_pairs={{0,1},{1,0},{2,3},{3,2},{4,5},{5,4},{6,7},{7,6},{8,9},{9,8},{10,11... | collective-permute-start | bytes 1179656 | tf_op jit(solution)/shard_map/ppermute | solution.py:543
  5.8 29.5 %collective-permute-start.1 = (bf16[256,768]{1,0:T(8,128)(2,1)S(1)}, bf16[256,768]{1,0:T(8,128)(2,1)S(1)}, u32[]{:S(2)}, u32[]{:S(2)}) collective-permute-start(bf16[256,768]{1,0:T(8,128)(2,1)S(1)} %dynamic-slice_bitcast_fusion), channel_id=1, source_target_pairs={{0,1},{1,0},{2,3},{3,2},{4,5},{5,4},{6,7},{7,6},{8,9},{9,8},{10,11... | collective-permute-start | bytes 1179656 | tf_op jit(solution)/shard_map/ppermute | solution.py:543
  13.3 21.9 %copy-start.2 = (bf16[2,256,768]{2,1,0:T(8,128)(2,1)S(1)}, bf16[2,256,768]{2,1,0:T(8,128)(2,1)}, u32[]{:S(2)}) copy-start(bf16[2,256,768]{2,1,0:T(8,128)(2,1)} %cot_own.1) | copy-start | bytes 2359300
  20.9 14.3 %copy-start.13 = (f32[3072]{0:T(1024)S(1)}, f32[3072]{0:T(1024)}, u32[]{:S(2)}) copy-start(f32[3072]{0:T(1024)} %param.31) | copy-start | bytes 36868
  35.2 15.0 %copy-start.18 = (bf16[512,768]{1,0:T(8,128)(2,1)}, bf16[512,768]{1,0:T(8,128)(2,1)S(1)}, u32[]{:S(2)}) copy-start(bf16[512,768]{1,0:T(8,128)(2,1)S(1)} %get-tuple-element.59.q) | copy-start | bytes 2359300
  35.2 15.0 %copy-start.20 = (bf16[768,512]{1,0:T(8,128)(2,1)}, bf16[768,512]{1,0:T(8,128)(2,1)S(1)}, u32[]{:S(2)}) copy-start(bf16[768,512]{1,0:T(8,128)(2,1)S(1)} %get-tuple-element.60.kt) | copy-start | bytes 2359300
  35.2 15.0 %copy-start.22 = (bf16[512,768]{1,0:T(8,128)(2,1)}, bf16[512,768]{1,0:T(8,128)(2,1)S(1)}, u32[]{:S(2)}) copy-start(bf16[512,768]{1,0:T(8,128)(2,1)S(1)} %get-tuple-element.61.v) | copy-start | bytes 2359300
  35.2 15.0 %copy-start.27 = (bf16[512,768]{1,0:T(8,128)(2,1)}, bf16[512,768]{1,0:T(8,128)(2,1)S(1)}, u32[]{:S(2)}) copy-start(bf16[512,768]{1,0:T(8,128)(2,1)S(1)} %get-tuple-element.50.nl) | copy-start | bytes 2359300
  75.4 29.1 %collective-permute-start.9 = (bf16[2,2,2,2,240,384]{5,4,3,2,1,0:T(8,128)(2,1)S(1)}, bf16[2,2,2,2,240,384]{5,4,3,2,1,0:T(8,128)(2,1)}, u32[]{:S(2)}, u32[]{:S(2)}) collective-permute-start(bf16[2,2,2,2,240,384]{5,4,3,2,1,0:T(8,128)(2,1)S(1)} %get-tuple-element.78), channel_id=1, source_target_pairs={{0,2},{2,0},{4,6},{6,4},{8,10},{10,8},{12,14},{14,12},{16,18},{18,... | collective-permute-start | bytes 8847368 | tf_op jit(solution)/shard_map/ppermute | solution.py:544
  96.2 19.3 %copy-start.1 = (bf16[2,2,2,2,144,384]{5,4,3,2,1,0:T(8,128)(2,1)}, bf16[2,2,2,2,144,384]{5,4,3,2,1,0:T(8,128)(2,1)S(1)}, u32[]{:S(2)}) copy-start(bf16[2,2,2,2,144,384]{5,4,3,2,1,0:T(8,128)(2,1)S(1)} %get-tuple-element.74) | copy-start | bytes 5308420
  96.2 6.0 %collective-permute-start.4 = (bf16[2,2,2,2,144,384]{5,4,3,2,1,0:T(8,128)(2,1)S(1)}, bf16[2,2,2,2,144,384]{5,4,3,2,1,0:T(8,128)(2,1)S(1)}, u32[]{:S(2)}, u32[]{:S(2)}) collective-permute-start(bf16[2,2,2,2,144,384]{5,4,3,2,1,0:T(8,128)(2,1)S(1)} %get-tuple-element.75), channel_id=1, source_target_pairs={{0,2},{2,0},{4,6},{6,4},{8,10},{10,8},{12,14},{14,12},{16,18},{18,... | collective-permute-start | bytes 5308424 | tf_op jit(solution)/shard_map/ppermute | solution.py:544
  102.1 6.4 %collective-permute-start.14 = (bf16[2,2,2,2,192,384]{5,4,3,2,1,0:T(8,128)(2,1)S(1)}, bf16[2,2,2,2,192,384]{5,4,3,2,1,0:T(8,128)(2,1)S(1)}, u32[]{:S(2)}, u32[]{:S(2)}) collective-permute-start(bf16[2,2,2,2,192,384]{5,4,3,2,1,0:T(8,128)(2,1)S(1)} %get-tuple-element.81), channel_id=1, source_target_pairs={{0,2},{2,0},{4,6},{6,4},{8,10},{10,8},{12,14},{14,12},{16,18},{18,... | collective-permute-start | bytes 7077896 | tf_op jit(solution)/shard_map/ppermute | solution.py:544
  102.4 13.1 %collective-permute-start.5 = (bf16[2,2,2,144,384]{4,3,2,1,0:T(8,128)(2,1)S(1)}, bf16[2,2,2,144,384]{4,3,2,1,0:T(8,128)(2,1)S(1)}, u32[]{:S(2)}, u32[]{:S(2)}) collective-permute-start(bf16[2,2,2,144,384]{4,3,2,1,0:T(8,128)(2,1)S(1)} %fusion.4), channel_id=1, source_target_pairs={{0,4},{1,5},{2,3},{3,2},{4,0},{5,1},{6,7},{7,6},{8,12},{9,13},{10,... | collective-permute-start | bytes 2654216 | tf_op jit(solution)/shard_map/ppermute | solution.py:552
  107.4 63.1 %collective-permute-start.10 = (bf16[2,2,2,240,384]{4,3,2,1,0:T(8,128)(2,1)}, bf16[2,2,2,240,384]{4,3,2,1,0:T(8,128)(2,1)}, u32[]{:S(2)}, u32[]{:S(2)}) collective-permute-start(bf16[2,2,2,240,384]{4,3,2,1,0:T(8,128)(2,1)} %fusion), channel_id=1, source_target_pairs={{0,4},{1,5},{2,3},{3,2},{4,0},{5,1},{6,7},{7,6},{8,12},{9,13},{10,... | collective-permute-start | bytes 4423688 | tf_op jit(solution)/shard_map/ppermute | solution.py:552
  110.3 58.0 %collective-permute-start.15 = (bf16[2,2,2,192,384]{4,3,2,1,0:T(8,128)(2,1)}, bf16[2,2,2,192,384]{4,3,2,1,0:T(8,128)(2,1)}, u32[]{:S(2)}, u32[]{:S(2)}) collective-permute-start(bf16[2,2,2,192,384]{4,3,2,1,0:T(8,128)(2,1)} %fusion.2), channel_id=1, source_target_pairs={{0,4},{1,5},{2,3},{3,2},{4,0},{5,1},{6,7},{7,6},{8,12},{9,13},{10,... | collective-permute-start | bytes 3538952 | tf_op jit(solution)/shard_map/ppermute | solution.py:552
  115.5 47.3 %copy-start.31 = (bf16[2,2,2,144,384]{4,3,2,1,0:T(8,128)(2,1)}, bf16[2,2,2,144,384]{4,3,2,1,0:T(8,128)(2,1)S(1)}, u32[]{:S(2)}) copy-start(bf16[2,2,2,144,384]{4,3,2,1,0:T(8,128)(2,1)S(1)} %collective-permute-done.5) | copy-start | bytes 2654212
  116.6 48.6 %collective-permute-start.6 = (bf16[2,2,144,384]{3,2,1,0:T(8,128)(2,1)}, bf16[2,2,144,384]{3,2,1,0:T(8,128)(2,1)}, u32[]{:S(2)}, u32[]{:S(2)}) collective-permute-start(bf16[2,2,144,384]{3,2,1,0:T(8,128)(2,1)} %fusion.5), channel_id=1, source_target_pairs={{0,1},{1,0},{2,6},{3,7},{4,5},{5,4},{6,2},{7,3},{8,9},{9,8},{10,14... | collective-permute-start | bytes 1327112 | tf_op jit(solution)/shard_map/ppermute | solution.py:552
  118.7 1.2 collective-permute-start.19
  119.9 29.4 %collective-permute-start.20 = (f32[12,768]{1,0:T(8,128)S(1)}, f32[12,768]{1,0:T(8,128)S(1)}, u32[]{:S(2)}, u32[]{:S(2)}) collective-permute-start(f32[12,768]{1,0:T(8,128)S(1)} %add.259), channel_id=1, source_target_pairs={{0,4},{1,5},{2,3},{3,2},{4,0},{5,1},{6,7},{7,6},{8,12},{9,13},{10,... | collective-permute-start | bytes 110600 | tf_op jit(solution)/shard_map/ppermute | solution.py:552
  149.3 4.2 %collective-permute-start.21 = (f32[12,768]{1,0:T(8,128)S(1)}, f32[12,768]{1,0:T(8,128)S(1)}, u32[]{:S(2)}, u32[]{:S(2)}) collective-permute-start(f32[12,768]{1,0:T(8,128)S(1)} %add.260), channel_id=1, source_target_pairs={{0,1},{1,0},{2,6},{3,7},{4,5},{5,4},{6,2},{7,3},{8,9},{9,8},{10,14... | collective-permute-start | bytes 110600 | tf_op jit(solution)/shard_map/ppermute | solution.py:552
  153.4 4.2 %collective-permute-start.22 = (f32[12,768]{1,0:T(8,128)S(1)}, f32[12,768]{1,0:T(8,128)S(1)}, u32[]{:S(2)}, u32[]{:S(2)}) collective-permute-start(f32[12,768]{1,0:T(8,128)S(1)} %add.261), channel_id=1, source_target_pairs={{0,8},{2,10},{4,12},{6,14},{8,0},{10,2},{12,4},{14,6},{16,24},{18,... | collective-permute-start | bytes 110600 | tf_op jit(solution)/shard_map/ppermute | solution.py:544
  157.6 5.2 %collective-permute-start.23 = (f32[12,768]{1,0:T(8,128)S(1)}, f32[12,768]{1,0:T(8,128)S(1)}, u32[]{:S(2)}, u32[]{:S(2)}) collective-permute-start(f32[12,768]{1,0:T(8,128)S(1)} %add.262), channel_id=1, source_target_pairs={{0,16},{2,18},{4,20},{6,22},{8,24},{10,26},{12,28},{14,30},{16,0},... | collective-permute-start | bytes 110600 | tf_op jit(solution)/shard_map/ppermute | solution.py:544
  160.8 17.8 %collective-permute-start.2 = (bf16[256,768]{1,0:T(8,128)(2,1)}, bf16[256,768]{1,0:T(8,128)(2,1)}, u32[]{:S(2)}, u32[]{:S(2)}) collective-permute-start(bf16[256,768]{1,0:T(8,128)(2,1)} %get-tuple-element.52), channel_id=1, source_target_pairs={{0,1},{1,0},{2,3},{3,2},{4,5},{5,4},{6,7},{7,6},{8,9},{9,8},{10,11... | collective-permute-start | bytes 1179656 | tf_op jit(solution)/shard_map/ppermute | solution.py:543
  162.9 18.2 %collective-permute-start.3 = (bf16[256,768]{1,0:T(8,128)(2,1)}, bf16[256,768]{1,0:T(8,128)(2,1)S(1)}, u32[]{:S(2)}, u32[]{:S(2)}) collective-permute-start(bf16[256,768]{1,0:T(8,128)(2,1)} %get-tuple-element.69), channel_id=1, source_target_pairs={{0,1},{1,0},{2,3},{3,2},{4,5},{5,4},{6,7},{7,6},{8,9},{9,8},{10,11... | collective-permute-start | bytes 1179656 | tf_op jit(solution)/shard_map/ppermute | solution.py:543
  166.7 7.1 %collective-permute-start.7 = (bf16[2,144,384]{2,1,0:T(8,128)(2,1)S(1)}, bf16[2,144,384]{2,1,0:T(8,128)(2,1)S(1)}, u32[]{:S(2)}, u32[]{:S(2)}) collective-permute-start(bf16[2,144,384]{2,1,0:T(8,128)(2,1)S(1)} %fusion.8), channel_id=1, source_target_pairs={{0,8},{2,10},{4,12},{6,14},{8,0},{10,2},{12,4},{14,6},{16,24},{18,... | collective-permute-start | bytes 663560 | tf_op jit(solution)/shard_map/ppermute | solution.py:544
  169.9 13.9 %collective-permute-start.16 = (bf16[2,2,192,384]{3,2,1,0:T(8,128)(2,1)S(1)}, bf16[2,2,192,384]{3,2,1,0:T(8,128)(2,1)S(1)}, u32[]{:S(2)}, u32[]{:S(2)}) collective-permute-start(bf16[2,2,192,384]{3,2,1,0:T(8,128)(2,1)S(1)} %fusion.3), channel_id=1, source_target_pairs={{0,1},{1,0},{2,6},{3,7},{4,5},{5,4},{6,2},{7,3},{8,9},{9,8},{10,14... | collective-permute-start | bytes 1769480 | tf_op jit(solution)/shard_map/ppermute | solution.py:552
  172.1 19.6 %collective-permute-start.11 = (bf16[2,2,240,384]{3,2,1,0:T(8,128)(2,1)S(1)}, bf16[2,2,240,384]{3,2,1,0:T(8,128)(2,1)S(1)}, u32[]{:S(2)}, u32[]{:S(2)}) collective-permute-start(bf16[2,2,240,384]{3,2,1,0:T(8,128)(2,1)S(1)} %fusion.1), channel_id=1, source_target_pairs={{0,1},{1,0},{2,6},{3,7},{4,5},{5,4},{6,2},{7,3},{8,9},{9,8},{10,14... | collective-permute-start | bytes 2211848 | tf_op jit(solution)/shard_map/ppermute | solution.py:552
  174.9 7.7 %collective-permute-start.8 = (bf16[144,384]{1,0:T(8,128)(2,1)S(1)}, bf16[144,384]{1,0:T(8,128)(2,1)S(1)}, u32[]{:S(2)}, u32[]{:S(2)}) collective-permute-start(bf16[144,384]{1,0:T(8,128)(2,1)S(1)} %fusion.13), channel_id=1, source_target_pairs={{0,16},{2,18},{4,20},{6,22},{8,24},{10,26},{12,28},{14,30},{16,0},... | collective-permute-start | bytes 331784 | tf_op jit(solution)/shard_map/ppermute | solution.py:544
  185.1 10.2 %collective-permute-start.17 = (bf16[2,192,384]{2,1,0:T(8,128)(2,1)S(1)}, bf16[2,192,384]{2,1,0:T(8,128)(2,1)S(1)}, u32[]{:S(2)}, u32[]{:S(2)}) collective-permute-start(bf16[2,192,384]{2,1,0:T(8,128)(2,1)S(1)} %fusion.7), channel_id=1, source_target_pairs={{0,8},{2,10},{4,12},{6,14},{8,0},{10,2},{12,4},{14,6},{16,24},{18,... | collective-permute-start | bytes 884744 | tf_op jit(solution)/shard_map/ppermute | solution.py:544
  193.0 9.4 %collective-permute-start.12 = (bf16[2,240,384]{2,1,0:T(8,128)(2,1)S(1)}, bf16[2,240,384]{2,1,0:T(8,128)(2,1)S(1)}, u32[]{:S(2)}, u32[]{:S(2)}) collective-permute-start(bf16[2,240,384]{2,1,0:T(8,128)(2,1)S(1)} %fusion.6), channel_id=1, source_target_pairs={{0,8},{2,10},{4,12},{6,14},{8,0},{10,2},{12,4},{14,6},{16,24},{18,... | collective-permute-start | bytes 1105928 | tf_op jit(solution)/shard_map/ppermute | solution.py:544
  196.5 9.5 %collective-permute-start.18 = (bf16[192,384]{1,0:T(8,128)(2,1)S(1)}, bf16[192,384]{1,0:T(8,128)(2,1)S(1)}, u32[]{:S(2)}, u32[]{:S(2)}) collective-permute-start(bf16[192,384]{1,0:T(8,128)(2,1)S(1)} %fusion.11), channel_id=1, source_target_pairs={{0,16},{2,18},{4,20},{6,22},{8,24},{10,26},{12,28},{14,30},{16,0},... | collective-permute-start | bytes 442376 | tf_op jit(solution)/shard_map/ppermute | solution.py:544
  203.5 8.5 %collective-permute-start.13 = (bf16[240,384]{1,0:T(8,128)(2,1)S(1)}, bf16[240,384]{1,0:T(8,128)(2,1)S(1)}, u32[]{:S(2)}, u32[]{:S(2)}) collective-permute-start(bf16[240,384]{1,0:T(8,128)(2,1)S(1)} %fusion.9), channel_id=1, source_target_pairs={{0,16},{2,18},{4,20},{6,22},{8,24},{10,26},{12,28},{14,30},{16,0},... | collective-permute-start | bytes 552968 | tf_op jit(solution)/shard_map/ppermute | solution.py:544
  (24 other events, 184.7 us)

commit v2 on v1

v2 whole, which is shorter than its diff:
```python
import functools
import math

import jax
import jax.numpy as jnp
from jax import lax
from jax.experimental import pallas as pl
from jax.experimental.pallas import tpu as pltpu
from jax.sharding import PartitionSpec as P

HEADS = 12
F32, BF = jnp.float32, jnp.bfloat16
NEG = -1000000000.0
GELU = math.sqrt(2.0 / math.pi)
VMEM_LIMIT = 20 << 20


def nn(a, b):
    return lax.dot_general(a, b, (((1,), (0,)), ((), ())), preferred_element_type=F32)


def nt(a, b):
    return lax.dot_general(a, b, (((1,), (1,)), ((), ())), preferred_element_type=F32)


def tn(a, b):
    return lax.dot_general(a, b, (((0,), (0,)), ((), ())), preferred_element_type=F32)


def shape(dims, dtype):
    return jax.ShapeDtypeStruct(dims, dtype)


def full(dims):
    return pl.BlockSpec(dims, lambda g, s: (0,) * len(dims))


def cols(rows, width):
    return pl.BlockSpec((rows, width), lambda g, s: (0, g))


def vec(width):
    return pl.BlockSpec((width,), lambda g, s: (g,))


def whole_vec(width):
    return pl.BlockSpec((width,), lambda g, s: (0,))


def lane(ref):
    return ref[...].reshape(1, -1)


def rows_of(height, width):
    return pl.BlockSpec((height, width), lambda g, s: (g, 0))


def own_slot(rows, width):
    return pl.BlockSpec((1, rows, width), lambda g, s: (s[0], 0, 0))


def call(body, grid, in_specs, out_specs, out_shape, scratch, name, flops, nbytes, trans=0, aliases=None):
    return pl.pallas_call(
        body,
        grid_spec=pltpu.PrefetchScalarGridSpec(
            num_scalar_prefetch=1,
            grid=grid,
            in_specs=in_specs,
            out_specs=out_specs,
            scratch_shapes=scratch,
        ),
        out_shape=out_shape,
        input_output_aliases=aliases or {},
        compiler_params=pltpu.CompilerParams(vmem_limit_bytes=VMEM_LIMIT),
        cost_estimate=pl.CostEstimate(flops=flops // 1000, bytes_accessed=nbytes // 1000, transcendentals=0),
        name=name,
    )


def attn_fwd_body(s, own, rem, wq, wk, wv, bq, bv, wm, mb, g1, b1,
                  q_o, kt_o, v_o, e_o, il_o, ctx_o, n1_o, rs_o, nl_o, xs, mask, acc):
    g = pl.program_id(0)
    half = own.shape[1]
    length = 2 * half

    @pl.when(g == 0)
    def _():
        xs[:half] = own[0]
        xs[half:] = rem[...]
        at = lax.broadcasted_iota(jnp.int32, (length, 128), 0) + s[0] * half
        at = jnp.where(at >= length, at - length, at)
        mask[...] = jnp.where(at < s[1], 0.0, NEG)

    x = xs[...]
    q = (nn(x, wq[...]) + lane(bq)).astype(BF) * BF(0.125)
    k = nn(x, wk[...]).astype(BF)
    v = (nn(x, wv[...]) + lane(bv)).astype(BF)
    q_o[...] = q
    v_o[...] = v
    qt = q.T
    kt_o[...] = k.T
    vt = v.T
    zero = jnp.zeros((64, length), BF)
    outs = []
    for h in range(4):
        pair = (h // 2) * 128
        qh = qt[h * 64 : h * 64 + 64]
        qa = jnp.concatenate([qh, zero] if h % 2 == 0 else [zero, qh], 0)
        sc = nn(k[:, pair : pair + 128], qa) + mask[:, :1]
        e = jnp.exp(sc - jnp.max(sc, 0, keepdims=True))
        il = 1.0 / jnp.sum(e, 0, keepdims=True)
        low = e.astype(BF)
        e_o[h] = low
        il_o[h] = il
        outs.append(nn(vt[h * 64 : h * 64 + 64], low) * il)
    ctx = jnp.concatenate(outs, 0).astype(BF).T
    ctx_o[...] = ctx
    part = nn(ctx, wm[...])

    @pl.when(g == 0)
    def _():
        acc[...] = part

    @pl.when(g > 0)
    def _():
        acc[...] += part

    @pl.when(g == pl.num_programs(0) - 1)
    def _():
        for i in range(4):
            at = pl.ds(i * 128, 128)
            r = acc[at] + lane(mb) + xs[at].astype(F32)
            c = r - jnp.mean(r, -1, keepdims=True)
            rs = lax.rsqrt(jnp.mean(c * c, -1, keepdims=True) + 1e-05)
            n = c * rs
            n1_o[at] = n
            rs_o[at] = rs
            nl_o[at] = (n * lane(g1) + lane(b1)).astype(BF)


def attn_fwd(s, tokens, rem, wq, wk, wv, bq, bv, wm, mb, g1, b1):
    half, d = rem.shape
    t = 2 * half
    return call(
        attn_fwd_body,
        (d // 256,),
        [own_slot(half, d), full((half, d))]
        + [cols(d, 256)] * 3
        + [vec(256)] * 2
        + [rows_of(256, d)]
        + [whole_vec(d)] * 3,
        [
            cols(t, 256),
            rows_of(256, t),
            cols(t, 256),
            pl.BlockSpec((4, t, t), lambda g, s: (g, 0, 0)),
            pl.BlockSpec((4, 1, t), lambda g, s: (g, 0, 0)),
            cols(t, 256),
            full((t, d)),
            full((t, 1)),
            full((t, d)),
        ],
        [
            shape((t, d), BF),
            shape((d, t), BF),
            shape((t, d), BF),
            shape((HEADS, t, t), BF),
            shape((HEADS, 1, t), F32),
            shape((t, d), BF),
            shape((t, d), F32),
            shape((t, 1), F32),
            shape((t, d), BF),
        ],
        [pltpu.VMEM((t, d), BF), pltpu.VMEM((t, 128), F32), pltpu.VMEM((t, d), F32)],
        "attn_fwd",
        3_200_000_000,
        18 << 20,
        3 << 20,
    )(s, tokens, rem, wq, wk, wv, bq, bv, wm, mb, g1, b1)


def gelu_both(u):
    u2 = u * u
    a = 0.5 + 0.5 * jnp.tanh(u * (GELU + (GELU * 0.044715) * u2))
    return u * a, a + (2.0 * u) * (a * (1.0 - a)) * (GELU + (3.0 * GELU * 0.044715) * u2)


def norm_back(c, n, rs):
    return rs * (c - jnp.mean(c, -1, keepdims=True) - n * jnp.mean(c * n, -1, keepdims=True))


def mlp_fwd_body(s, nl, wi, bi, wo, bo, n1, g1, b1, g2, b2, cot_own, cot_rem,
                 act_o, dg_o, out_own, rem0, rem1, ss_o, sl_o, vec_o, acc):
    j = pl.program_id(0)
    half = cot_rem.shape[0]
    u = nn(nl[...], wi[...]) + lane(bi)
    act, slope = gelu_both(u)
    act = act.astype(BF)
    act_o[...] = act
    dg_o[...] = slope.astype(BF)
    part = nn(act, wo[...])

    @pl.when(j == 0)
    def _():
        acc[...] = part

    @pl.when(j > 0)
    def _():
        acc[...] += part

    @pl.when(j == pl.num_programs(0) - 1)
    def _():
        gain = jnp.zeros((1, nl.shape[1]), F32)
        bias, outer = gain, gain
        for i in range(4):
            at = pl.ds(i * 128, 128)
            r = acc[at] + lane(bo) + (n1[at] * lane(g1) + lane(b1))
            c = r - jnp.mean(r, -1, keepdims=True)
            rs = lax.rsqrt(jnp.mean(c * c, -1, keepdims=True) + 1e-05)
            n = c * rs
            o = n * lane(g2) + lane(b2)
            if i * 128 < half:
                out_own[0, at] = o
                ct = cot_own[0, at].astype(F32)
            else:
                back = pl.ds(i * 128 - half, 128)
                (rem1 if i * 128 - half >= half // 2 else rem0)[...] = o.astype(BF)
                ct = cot_rem[back].astype(F32)
            gain += jnp.sum(ct * n, 0, keepdims=True)
            bias += jnp.sum(ct, 0, keepdims=True)
            slope2 = norm_back(ct * lane(g2), n, rs)
            ss_o[at] = slope2
            low = slope2.astype(BF)
            sl_o[at] = low
            outer += jnp.sum(low.astype(F32), 0, keepdims=True)
        vec_o[0:1] = gain
        vec_o[1:2] = bias
        vec_o[2:3] = outer


def mlp_fwd(s, nl, wi, bi, wo, bo, n1, g1, b1, g2, b2, cot, cot_rem):
    t, d = nl.shape
    ff = wi.shape[1]
    half = t // 2
    w = 512
    return call(
        mlp_fwd_body,
        (ff // w,),
        [full((t, d)), cols(d, w), vec(w), rows_of(w, d), whole_vec(d), full((t, d))]
        + [whole_vec(d)] * 4
        + [own_slot(half, d), full((half, d))],
        [cols(t, w), cols(t, w), own_slot(half, d)] + [full((half // 2, d))] * 2 + [full((t, d)), full((t, d)), full((3, d))],
        [
            shape((t, ff), BF),
            shape((t, ff), BF),
            shape((2, half, d), F32),
            shape((half // 2, d), BF),
            shape((half // 2, d), BF),
            shape((t, d), F32),
            shape((t, d), BF),
            shape((3, d), F32),
        ],
        [pltpu.VMEM((t, d), F32)],
        "mlp_fwd",
        4_800_000_000,
        24 << 20,
        2 << 20,
    )(s, nl, wi, bi, wo, bo, n1, g1, b1, g2, b2, cot, cot_rem)


def slope_inner_body(s, sl, wo, dg, si_o, bi_o):
    si = (nt(sl[...], wo[...]) * dg[...].astype(F32)).astype(BF)
    si_o[...] = si
    bi_o[...] = jnp.sum(si.astype(F32), 0, keepdims=True)


def slope_inner(s, sl, wo, dg):
    t, d = sl.shape
    ff = wo.shape[0]
    w = 512
    return call(
        slope_inner_body,
        (ff // w,),
        [full((t, d)), rows_of(w, d), cols(t, w)],
        [cols(t, w), cols(1, w)],
        [shape((t, ff), BF), shape((1, ff), F32)],
        [],
        "slope_inner",
        2_400_000_000,
        12 << 20,
    )(s, sl, wo, dg)


def slope_first_body(s, si, wi, ss, n1, rs, g1, sm_o, ml_o, vec_o, acc):
    j = pl.program_id(0)
    part = nt(si[...], wi[...])

    @pl.when(j == 0)
    def _():
        acc[...] = part

    @pl.when(j > 0)
    def _():
        acc[...] += part

    @pl.when(j == pl.num_programs(0) - 1)
    def _():
        gain = jnp.zeros((1, ss.shape[1]), F32)
        bias, mixer = gain, gain
        for i in range(4):
            at = pl.ds(i * 128, 128)
            sf = acc[at] + ss[at]
            n = n1[at]
            gain += jnp.sum(sf * n, 0, keepdims=True)
            bias += jnp.sum(sf, 0, keepdims=True)
            sm = norm_back(sf * lane(g1), n, rs[at])
            sm_o[at] = sm
            low = sm.astype(BF)
            ml_o[at] = low
            mixer += jnp.sum(low.astype(F32), 0, keepdims=True)
        vec_o[0:1] = gain
        vec_o[1:2] = bias
        vec_o[2:3] = mixer


def slope_first(s, si, wi, ss, n1, rs, g1):
    t, d = ss.shape
    ff = wi.shape[1]
    w = 1024
    return call(
        slope_first_body,
        (ff // w,),
        [cols(t, w), cols(d, w), full((t, d)), full((t, d)), full((t, 1)), whole_vec(d)],
        [full((t, d)), full((t, d)), full((3, d))],
        [shape((t, d), F32), shape((t, d), BF), shape((3, d), F32)],
        [pltpu.VMEM((t, d), F32)],
        "slope_first",
        2_400_000_000,
        14 << 20,
    )(s, si, wi, ss, n1, rs, g1)


def attn_bwd_body(s, ml, wm, q, kt, v, e, il, ctx, dq_o, dk_o, dv_o):
    t = ml.shape[0]
    dct = nt(wm[...], ml[...]).astype(BF)
    ctxt = ctx[...].T
    zero = jnp.zeros((64, t), BF)
    lanes = lax.broadcasted_iota(jnp.int32, (t, 128), 1)
    dqs = []
    for pair in range(2):
        dkp = jnp.zeros((t, 128), F32)
        dvp = dkp
        at = slice(pair * 128, pair * 128 + 128)
        vp, qp = v[:, at], q[:, at]
        for one in range(2):
            h = pair * 2 + one
            sub = slice(h * 64, h * 64 + 64)
            dc = (dct[sub].astype(F32) * il[h]).astype(BF)
            da = jnp.concatenate([dc, zero] if one == 0 else [zero, dc], 0)
            delta = jnp.sum(dc.astype(F32) * ctxt[sub].astype(F32), 0, keepdims=True)
            low = e[h]
            ds = (low.astype(F32) * (nn(vp, da) - delta)).astype(BF)
            keep = (lanes < 64) if one == 0 else (lanes >= 64)
            dkp += nn(ds, jnp.where(keep, qp, BF(0)))
            dvp += nn(low, da.T)
            dqs.append(nn(kt[sub], ds) * 0.125)
        dk_o[:, at] = dkp.astype(BF)
        dv_o[:, at] = dvp.astype(BF)
    dq_o[...] = jnp.concatenate(dqs, 0).astype(BF).T


def attn_bwd(g, s, ml, wm, q, kt, v, e, il, ctx):
    t, d = ml.shape

    def at_col(rows):
        return pl.BlockSpec((rows, 256), lambda i, s: (0, g))

    return call(
        attn_bwd_body,
        (1,),
        [
            full((t, d)),
            pl.BlockSpec((256, d), lambda i, s: (g, 0)),
            at_col(t),
            pl.BlockSpec((256, t), lambda i, s: (g, 0)),
            at_col(t),
            pl.BlockSpec((4, t, t), lambda i, s: (g, 0, 0)),
            pl.BlockSpec((4, 1, t), lambda i, s: (g, 0, 0)),
            at_col(t),
        ],
        [full((t, 256))] * 3,
        [shape((t, 256), BF)] * 3,
        [],
        "attn_bwd",
        1_200_000_000,
        5 << 20,
    )(s, ml, wm, q, kt, v, e, il, ctx)


def input_grad_body(s, dq0, dk0, dv0, dq1, dk1, dv1, dq2, dk2, dv2, wq, wk, wv, sm, own_o, rem_o):
    half = sm.shape[0] // 2
    w = dq0.shape[1]
    total = sm[...]
    for g, (dq, dk, dv) in enumerate(((dq0, dk0, dv0), (dq1, dk1, dv1), (dq2, dk2, dv2))):
        at = slice(g * w, g * w + w)
        total += nt(dq[...], wq[:, at]) + nt(dk[...], wk[:, at]) + nt(dv[...], wv[:, at])
    own_o[0] = total[:half]
    rem_o[...] = total[half:].astype(BF)


def input_grad(s, slopes, wq, wk, wv, sm):
    t, d = sm.shape
    half = t // 2
    return call(
        input_grad_body,
        (1,),
        [full((t, 256))] * 9 + [full((d, d))] * 3 + [full((t, d))],
        [own_slot(half, d), full((half, d))],
        [shape((2, half, d), F32), shape((half, d), BF)],
        [],
        "input_grad",
        1_800_000_000,
        8 << 20,
    )(s, *slopes, wq, wk, wv, sm)


XY = (("x", "y", "z1", "z2"), ("y", "x", "z1", "z2"))
XZY = (("x", "z1", "y", "z2"), ("y", "z1", "x", "z2"))


def place(s, core, order, x, y, z1, z2):
    far = {"x": x ^ s[3], "y": y ^ s[0], "z1": z1 ^ s[4], "z2": z2 ^ s[5]}
    return [far[p] if p == q else jnp.where(core == 0, far[p], far[q]) for p, q in zip(*order)]


def outer_jobs(s, core, j):
    for x in range(2):
        for y in range(2):
            yield place(s, core, XZY, x, y, j & 1, j >> 1), (2 * x + core) * 192, 192, y * 384, 0


def thin_jobs(s, core, ys, ats):
    for r in range(8):
        for p in range(2):
            where = place(s, core, XY, r & 1, ys[p], (r >> 1) & 1, r >> 2)
            yield where, (2 * r + core) * 48, 48, 384 * p, ats[p]


def flush(s, tile, outs, sems, jobs_of):
    copies = []
    for away, out in enumerate(outs):
        for where, row, height, col, at in jobs_of(s[2] ^ away):
            copies.append(
                pltpu.make_async_copy(
                    tile.at[pl.ds(pl.multiple_of(row, 16), height), pl.ds(col, 384)],
                    out.at[*where, pl.ds(at, height)],
                    sems.at[len(copies)],
                )
            )
    return copies


def run_tiles(s, steps, tiles, sems, outs, fill, jobs_of):
    j = pl.program_id(0)

    def go(step, slot, wait):
        for copy in flush(s, tiles.at[slot], outs, sems.at[slot], lambda core: jobs_of(core, step)):
            copy.wait() if wait else copy.start()

    slot = lax.rem(j, 2)

    @pl.when(j >= 2)
    def _():
        go(j - 2, slot, True)

    fill(j, tiles.at[slot])
    go(j, slot, False)

    @pl.when(j == steps - 1)
    def _():
        if steps > 1:
            go(j - 1, 1 - slot, True)
        go(j, slot, True)


def outer_body(s, act, sl, keep, send, tiles, sems):
    def fill(_, tile):
        tile[...] = tn(act[...], sl[...]).astype(BF)

    run_tiles(s, 4, tiles, sems, (keep, send), fill, lambda core, step: outer_jobs(s, core, step))


def inner_body(s, nl, si, keep, send, tiles, sems):
    def jobs_of(core, step):
        base = pl.multiple_of((step & 1) * 96, 16)
        return thin_jobs(s, core, (step >> 1, step >> 1), (base, pl.multiple_of(base + 48, 16)))

    def fill(_, tile):
        tile[...] = tn(nl[...], si[...]).astype(BF)

    run_tiles(s, 4, tiles, sems, (keep, send), fill, jobs_of)


def last_body(s, own, rem, dq0, dk0, dv0, dq1, dk1, dv1, dq2, dk2, dv2, ctx, ml, v2, v1, bi,
              keep, send, vec_o, tiles, sems, xs):
    half, d = rem.shape

    def put(row, value):
        vec_o[row : row + 1] = value[:, :384]
        vec_o[12 + row : 13 + row] = value[:, 384:]

    @pl.when(pl.program_id(0) == 0)
    def _():
        xs[:half] = own[0]
        xs[half:] = rem[...]
        for i in range(3):
            put(2 + i, v2[i : i + 1])
            put(5 + i, v1[i : i + 1])
        for i in range(4):
            put(8 + i, bi[:, i * d : i * d + d])
        vec_o[24:] = jnp.zeros((8, 384), F32)

    def jobs_of(core, step):
        at = pl.multiple_of(step * 48, 16)
        return thin_jobs(s, core, (0, 1), (at, at))

    def fill(j, tile):
        for one, parts in enumerate(((dq0, dq1, dq2), (dk0, dk1, dk2), (dv0, dv1, dv2))):

            @pl.when(j == one)
            def _():
                for g, part in enumerate(parts):
                    tile[:, g * 256 : g * 256 + 256] = tn(xs[...], part[...]).astype(BF)
                if one != 1:
                    ones = jnp.ones((8, 2 * half), BF)
                    put(one // 2, jnp.concatenate([nn(ones, part[...])[:1] for part in parts], 1))

        @pl.when(j == 3)
        def _():
            tile[...] = tn(ctx[...], ml[...]).astype(BF)

    run_tiles(s, 4, tiles, sems, (keep, send), fill, jobs_of)


def weight_call(body, in_specs, jobs, name, flops, scratch=(), extra=()):
    block = (2, 2, 2, 2, 192, 384)
    hbm = pl.BlockSpec(memory_space=pl.ANY)
    return call(
        body,
        (4,),
        in_specs,
        [hbm] * 2 + [full(dims) for dims in extra],
        [shape(block, BF)] * 2 + [shape(dims, F32) for dims in extra],
        [pltpu.VMEM((2, 768, 768), BF), pltpu.SemaphoreType.DMA((2, 2 * jobs))] + list(scratch),
        name,
        flops,
        10 << 20,
    )


def vec_terms(vec, vec_in):
    got = vec_in[...].astype(F32)
    return vec[...] + (got if got.shape[0] == 32 else got[:32] + got[32:])


def combine_body(counts, last, s, *refs):
    ins, vec, vec_in = refs[: sum(counts)], refs[sum(counts)], refs[sum(counts) + 1]
    outs = refs[sum(counts) + 2 :]
    at = 0
    for i, count in enumerate(counts):
        total = sum(ref[...].astype(F32) for ref in ins[at : at + count])
        at += count
        if last:
            for j in range(4):
                outs[j][...] = total[j * 48 : j * 48 + 48]
        else:
            outs[i][: total.shape[0]] = total.astype(BF)
    new = vec_terms(vec, vec_in)
    if last:
        outs[-1][:, :384] = new[:12]
        outs[-1][:, 384:] = new[12:24]
    else:
        outs[-1][...] = new
        height = outs[0].shape[0]
        high = new.astype(BF)
        outs[0][height - 64 : height - 32] = high
        outs[0][height - 32 :] = (new - high.astype(F32)).astype(BF)


def combine(s, groups, vec, vec_in, last=False):
    specs, args, outs = [], [], []
    for parts, height, at in groups:
        specs += [pl.BlockSpec((height, 384), lambda g, s, at=at: (at, 0))] * len(parts)
        args += [part.reshape(-1, 384) for part in parts]
        outs.append(shape((height, 384), BF))
    if last:
        outs = [shape((48, 384), F32)] * 4 + [shape((12, 768), F32)]
    else:
        outs[0] = shape((groups[0][1] + 64, 384), BF)
        outs.append(shape((32, 384), F32))
    rows = vec_in.shape[0]
    tail = full((32, 384)) if rows == 32 else pl.BlockSpec((64, 384), lambda g, s: (rows // 64 - 1, 0))
    return call(
        functools.partial(combine_body, [len(parts) for parts, *_ in groups], last),
        (1,),
        specs + [full((32, 384)), tail],
        [full(o.shape) for o in outs],
        outs,
        [],
        "combine",
        0,
        4 << 20,
    )(s, *args, vec, vec_in)


def finish_body(s, *refs):
    *recv, _, out = refs
    at = 0
    for part in recv:
        out[0, at : at + part.shape[0]] = part[...].astype(F32)
        at += part.shape[0]


def finish(s, recv, whole):
    half, d = whole.shape[1:]
    return call(
        finish_body,
        (1,),
        [full(part.shape) for part in recv] + [pl.BlockSpec(memory_space=pl.ANY)],
        pl.BlockSpec((1, half, d), lambda g, s: (1 - s[0], 0, 0)),
        shape(whole.shape, F32),
        [],
        "finish",
        0,
        1 << 20,
        aliases={len(recv) + 1: 0},
    )(s, *recv, whole)


def local(n, tokens, cotangent, lengths, query_weight, query_bias, key_weight, value_weight, value_bias,
          mixer_weight, mixer_bias, first_gain, first_bias, inner_weight, inner_bias, outer_weight,
          outer_bias, second_gain, second_bias):
    d = tokens.shape[2]
    low_n = n // 16
    y = lax.axis_index("seq")
    dp = lax.axis_index("dp")
    hi = dp // low_n
    mine = lax.dynamic_index_in_dim(lengths, y, 0, keepdims=False)
    s = jnp.stack([y, mine, hi & 1, (hi >> 1) & 1, (hi >> 2) & 1, (hi >> 3) & 1]).astype(jnp.int32)

    def trade(value, bit):
        if bit == "y":
            return lax.ppermute(value, "seq", [(0, 1), (1, 0)])
        return lax.ppermute(value, "dp", [(i, i ^ (bit * low_n)) for i in range(n)])

    steps = {"x": 2 * low_n, "z1": 4 * low_n, "z2": 8 * low_n}

    def trade_stage(value, orders, stage):
        pairs = []
        for i in range(n):
            bit = orders[(i // low_n) % 2][stage]
            for r in range(2):
                pairs.append((2 * i + r, 2 * i + 1 - r if bit == "y" else 2 * (i ^ steps[bit]) + r))
        return lax.ppermute(value, ("dp", "seq"), pairs)

    rem = trade(lax.dynamic_index_in_dim(tokens, 1 - y, 0, keepdims=False), "y")
    cot_rem = trade(lax.dynamic_index_in_dim(cotangent, 1 - y, 0, keepdims=False), "y")

    def after(value, *others):
        return lax.optimization_barrier((value, others))[0]

    (tokens, cotangent, query_weight, query_bias, key_weight, value_weight, value_bias, mixer_weight,
     mixer_bias, first_gain, first_bias, inner_weight, inner_bias, outer_weight, outer_bias, second_gain,
     second_bias) = [
        pltpu.with_memory_space_constraint(v, pltpu.HBM)
        for v in (tokens, cotangent, query_weight, query_bias, key_weight, value_weight, value_bias,
                  mixer_weight, mixer_bias, first_gain, first_bias, inner_weight, inner_bias, outer_weight,
                  outer_bias, second_gain, second_bias)
    ]
    g1, b1, g2, b2 = first_gain, first_bias, second_gain, second_bias
    q, kt, v, e, il, ctx, n1, rs, nl = attn_fwd(
        s, tokens, rem, query_weight, key_weight, value_weight, query_bias, value_bias,
        mixer_weight, mixer_bias, g1, b1)
    act, dg, out, out0, out1, ss, sl, v2 = mlp_fwd(
        s, nl, inner_weight, inner_bias, outer_weight, outer_bias, n1, g1, b1, g2, b2,
        cotangent, cot_rem)
    t = sl.shape[0]
    half = t // 2
    piece = cols(t, 768)
    hold = full((t, d))

    def together(*values):
        return lax.optimization_barrier(values)

    class Reduce:
        def __init__(self, made, orders):
            self.keep, self.going = made
            self.orders = orders
            self.got = [self.keep]

        def total(self, index):
            return sum(a[index[max(i - 1, 0):]].astype(F32) for i, a in enumerate(self.got))

        def add(self):
            self.going = self.total((0,) * (len(self.got) - 2) + (1,)).astype(BF)

        def away(self, value):
            stage = len(self.got) - 2
            return trade(value, 1) if stage < 0 else trade_stage(value, self.orders, stage)

        def send(self):
            self.got.append(self.away(self.going))

        def done(self):
            return self.total((0, 0, 0, 0))

    got0 = trade(out0, "y")
    r1 = Reduce(weight_call(outer_body, [piece, hold], 4, "weight_outer", 2_400_000_000)(s, act, sl), XZY)
    r1.going, got0, out1 = together(r1.going, got0, out1)
    r1.send()
    got1 = trade(out1, "y")
    si, bi = slope_inner(after(s, r1.going), sl, outer_weight, dg)

    r1.got[-1], got1, bi = together(r1.got[-1], got1, bi)
    r1.add()
    early = r1.away(r1.going[1])
    r2 = Reduce(weight_call(inner_body, [hold, piece], 16, "weight_inner", 2_400_000_000)(
        after(s, r1.going), nl, si), XY)

    early, r2.going, rest = together(early, r2.going, r1.going[0])
    late = r1.away(rest)
    r2.send()
    sm, ml, v1 = slope_first(after(s, r2.going), si, inner_weight, ss, n1, rs, g1)

    early, late, r2.got[-1], v1 = together(early, late, r2.got[-1], v1)
    r1.got.append([late, early])
    r1.total = lambda index: sum(
        (a[index[1]][index[2:]] if i == 2 else a[index[max(i - 1, 0):]]).astype(F32) for i, a in enumerate(r1.got))
    r1.add()
    r1.send()
    r2.add()
    r2.send()
    back = (mixer_weight, q, kt, v, e, il, ctx)
    first = attn_bwd(0, after(s, r1.going, r2.going), ml, *back)
    second = attn_bwd(1, after(s, first[0]), ml, *back)
    third = attn_bwd(2, after(s, second[0]), ml, *back)

    r1.got[-1], r2.got[-1], *third = together(r1.got[-1], r2.got[-1], *third)
    slopes = (*first, *second, *third)
    r1.add()
    r1.send()
    r2.add()
    r2.send()
    quarter = [full((t, 256))] * 9
    *made, vec = weight_call(
        last_body, [own_slot(half, d), full((half, d))] + quarter + [hold] * 2 + [full((3, d))] * 2 + [full((1, 4 * d))],
        16, "weight_last", 2_400_000_000, [pltpu.VMEM((t, d), BF)], [(32, 384)])(
            after(s, r1.going, r2.going), tokens, rem, *slopes, ctx, ml, v2, v1, bi)
    r3 = Reduce(made, XY)

    r1.got[-1], r2.got[-1], r3.going, vec = together(r1.got[-1], r2.got[-1], r3.going, vec)
    r1.add()
    r1.send()
    r3.send()
    vec_got = trade(vec, 1)
    grad, grad_rem = input_grad(
        after(s, r1.going, r3.going), slopes, query_weight, key_weight, value_weight, sm)

    r1.got[-1], r3.got[-1], vec_got, grad_rem, r2.got[-1] = together(
        r1.got[-1], r3.got[-1], vec_got, grad_rem, r2.got[-1])
    rows = r3.going.size // 384 // 2
    going, r2.going, vec = combine(
        s, [(r3.got, rows, 1), (r2.got, rows // 4, 1)], vec, vec_got)
    r3.got.append(r3.away(going))
    r2.send()
    outer = r1.done()
    out = finish(after(s, going), (got0, got1), out)

    r3.got[-1], r2.got[-1], out, outer = together(r3.got[-1], r2.got[-1], out, outer)
    going, r2.going, vec = combine(
        s, [(r3.got, rows // 2, 1), (r2.got, rows // 8, 1)], vec, r3.got[-1])
    r3.got.append(r3.away(going))
    r2.send()

    r3.got[-1], r2.got[-1], grad_rem = together(r3.got[-1], r2.got[-1], grad_rem)
    going, vec = combine(s, [(r3.got, rows // 4, 1)], vec, r3.got[-1])
    r3.got.append(r3.away(going))
    grad_got = trade(after(grad_rem, going), "y")
    inner = sum(u.reshape(-1, 384)[: rows // 8].astype(F32) for u in r2.got)

    r3.got[-1], inner = together(r3.got[-1], inner)
    going, vec = combine(s, [(r3.got, rows // 8, 1)], vec, r3.got[-1])
    r3.got.append(r3.away(going))
    grad = finish(after(s, going), (grad_got,), grad)

    r3.got[-1], grad = together(r3.got[-1], grad)
    *weights, vec = combine(s, [(r3.got, rows // 8, 0)], vec, r3.got[-1], last=True)

    inner_own = jnp.concatenate([inner[i * 48 : i * 48 + 48] for i in range(4)], 1)
    weights += [inner_own, outer]
    step = low_n // 2
    while step >= 1:
        bit = (dp // step) % 2
        rest = []
        for w in weights:
            two = w.reshape(2, w.shape[0] // 2, w.shape[1])
            away = lax.dynamic_index_in_dim(two, 1 - bit, 0, keepdims=False)
            near = lax.dynamic_index_in_dim(two, bit, 0, keepdims=False)
            rest.append(near + lax.ppermute(away, "dp", [(i, i ^ step) for i in range(n)]))
        weights = rest
        vec = vec + lax.ppermute(vec, "dp", [(i, i ^ step) for i in range(n)])
        step //= 2
    return (out, grad, *weights, vec[0], vec[1], vec[7], vec[8:].reshape(-1), vec[4], vec[5], vec[6], vec[2], vec[3])


def solution(mesh):
    split = P("dp", "seq", None)
    block = P("dp", "seq")
    n = mesh.shape["dp"]

    def run(*args):
        return local(n, *args)

    return jax.shard_map(
        run,
        mesh=mesh,
        in_specs=(split, split, P("dp")) + (P(),) * 15,
        out_specs=(split, split) + (block,) * 6 + (P(),) * 9,
        check_vma=False,
    )
```

time: 216 us -> 170 us (0.79)
  other arithmetic: 21.3 us -> 3.07 us
  local copies, waits for them, and re-layouts: 22.5 us -> 5.43 us
  starting transfers between devices: 35.7 us -> 25.6 us
  Pallas kernels: 80.3 us -> 87.6 us
  waiting for transfers between devices: 53.6 us -> 46.9 us
    ppermute x12 -> x4, starting transfers between devices: 17.4 us -> 0.3 us  [trade(): return lax.ppermute(value, 'dp', [(i, i ^ bit * low_n) for i in range(n)])]
    convert_element_type x12 -> x6, other arithmetic: 16.4 us -> 1.39 us  [add(): self.going = self.total((0,) * (len(self.got) - 2) + (1,)).astype(BF)]
    ppermute x12 -> x4, waiting for transfers between devices: 13 us -> 0.01 us  [trade(): return lax.ppermute(value, 'dp', [(i, i ^ bit * low_n) for i in range(n)])]
    unnamed x64 -> x0, local copies, waits for them, and re-layouts: 10.4 us -> none
    pallas_call x8 -> x17, Pallas kernels: 67 us -> 74.1 us  [the longest x1 14.7 us: mlp_fwd(): call(mlp_fwd_body, (ff // w,), [full((t, d)), cols(d, w), vec(w), rows_of...]
    ppermute x8 -> x13, starting transfers between devices: 11.9 us -> 18.3 us  [trade_stage(): return lax.ppermute(value, ('dp', 'seq'), pairs)]
    ppermute x4 -> x5, waiting for transfers between devices: 1.37 us -> 6.89 us  [trade(): return lax.ppermute(value, 'seq', [(0, 1), (1, 0)])]
    reshape x8 -> x0, local copies, waits for them, and re-layouts: 5.51 us -> none  [row(): return v.reshape(1, -1)]
  transfers between devices with their start and end apart: 24 -> 22, of which waited for: 12 -> 12; matrix products, arithmetic and copies ran while one was open for 14% -> 3% of each run, Pallas kernels for 20% -> 41%
where the time goes in v2:
time: 170 us; the launch traced here: 169 us
  Pallas kernels  87.6 us (52%)
  waiting for transfers between devices  46.9 us (28%)
  starting transfers between devices  25.6 us (15%)
  local copies, waits for them, and re-layouts  5.43 us (3%)
  other arithmetic  3.07 us (2%)
    ppermute x13, waiting for transfers between devices, trade_stage(): return lax.ppermute(value, ('dp', 'seq'), pairs)  40 us
    ppermute x13, starting transfers between devices, trade_stage(): return lax.ppermute(value, ('dp', 'seq'), pairs)  18.3 us
    pallas_call x1, Pallas kernels, mlp_fwd(): call(mlp_fwd_body, (ff // w,), [full((t, d)), cols(d, w), vec(w), rows_of...  14.7 us
    pallas_call x1, Pallas kernels, attn_fwd(): call(attn_fwd_body, (d // 256,), [own_slot(half, d), full((half, d))] + [...  13.5 us
    pallas_call x3, Pallas kernels, attn_bwd(): call(attn_bwd_body, (1,), [full((t, d)), pl.BlockSpec((256, d), lambda i,...  12.7 us
    pallas_call x1, Pallas kernels, local(): weight_call(last_body, [own_slot(half, d), full((half, d))] + quarter + [...  8.11 us
    pallas_call x1, Pallas kernels, slope_first(): call(slope_first_body, (ff // w,), [cols(t, w), cols(d, w), full((t, d)),...  7.17 us
    ppermute x5, starting transfers between devices, trade(): return lax.ppermute(value, 'seq', [(0, 1), (1, 0)])  6.91 us
  transfers between devices with their start and end apart: 22, of which 12 were waited for; matrix products, arithmetic and copies ran while one was open for 3% of the time, Pallas kernels for 41%

profile of v2, /device:TPU:0, one launch (start us, length us, event | category | flops | bytes accessed | tf_op | source)
XLA Modules:
  0.0 169.5 jit_solution(2186085628355679374)
XLA Ops:
  1.7 3.1 %collective-permute-start = (bf16[256,768]{1,0:T(8,128)(2,1)S(1)}, bf16[256,768]{1,0:T(8,128)(2,1)S(1)}, u32[]{:S(2)}, u32[]{:S(2)}) collective-permute-start(bf16[256,768]{1,0:T(8,128)(2,1)S(1)} %dynamic-slice_bitcast_fusion.1), channel_id=1, source_target_pairs={{0,1},{1,0},{2,3},{3,2},{4,5},{5,4},{6,7},{7,6},{8,9},{9,8},{10,11... | collective-permute-start | bytes 1179656 | tf_op jit(solution)/shard_map/ppermute | solution.py:653
  7.8 6.9 %collective-permute-done.rem = bf16[256,768]{1,0:T(8,128)(2,1)S(1)} collective-permute-done((bf16[256,768]{1,0:T(8,128)(2,1)S(1)}, bf16[256,768]{1,0:T(8,128)(2,1)S(1)}, u32[]{:S(2)}, u32[]{:S(2)}) %collective-permute-start) | collective-permute-done | bytes 393248 | tf_op jit(solution)/shard_map/ppermute | solution.py:653
  14.7 13.5 %attn_fwd.1 = (bf16[512,768]{1,0:T(8,128)(2,1)S(1)}, bf16[768,512]{1,0:T(8,128)(2,1)S(1)}, bf16[512,768]{1,0:T(8,128)(2,1)S(1)}, bf16[12,512,512]{2,1,0:T(8,128)...) custom-call(s32[6]{0:T(128)S(1)} %stack.24.s, ...), custom_call_target="tpu_custom_call" | custom-call | flops 3200000 | bytes 18874 | tf_op jit(solution)/shard_map/attn_fwd/pallas_call | solution.py:144
  28.2 14.7 %mlp_fwd.1 = (bf16[512,3072]{1,0:T(8,128)(2,1)S(1)}, bf16[512,3072]{1,0:T(8,128)(2,1)S(1)}, f32[2,256,768]{2,1,0:T(8,128)}, bf16[128,768]{1,0:T(8,128)(2,1)S(1)}...) custom-call(s32[6]{0:T(128)S(1)} %stack.24.s, ...), custom_call_target="tpu_custom_call" | custom-call | flops 4800000 | bytes 25165 | tf_op jit(solution)/shard_map/mlp_fwd/pallas_call | solution.py:246
  42.9 2.0 %collective-permute-start.2 = (bf16[128,768]{1,0:T(8,128)(2,1)S(1)}, bf16[128,768]{1,0:T(8,128)(2,1)S(1)}, u32[]{:S(2)}, u32[]{:S(2)}) collective-permute-start(bf16[128,768]{1,0:T(8,128)(2,1)S(1)} %get-tuple-element.126), channel_id=1, source_target_pairs={{0,1},{1,0},{2,3},{3,2},{4,5},{5,4},{6,7},{7,6},{8,9},{9,8},{10,11... | collective-permute-start | bytes 589832 | tf_op jit(solution)/shard_map/ppermute | solution.py:653
  44.9 5.1 %weight_outer.1 = (bf16[2,2,2,2,192,384]{5,4,3,2,1,0:T(8,128)(2,1)S(1)}, bf16[2,2,2,2,192,384]{5,4,3,2,1,0:T(8,128)(2,1)S(1)}) custom-call(s32[6]{0:T(128)S(1)} %stack.24.s, bf16[512,3072]{1,0:T(8,128)(2,1)S(1)} %get-tuple-element.122.act, bf16[512,768]{1,0:T(8,128)(2,1)S(1)} %get-tuple-element.123.sl), custom_call_target="tpu_custom_call" | custom-call | flops 2400000 | bytes 10485 | tf_op jit(solution)/shard_map/weight_outer/pallas_call | solution.py:718
  50.6 6.9 %slope_inner.1 = (bf16[512,3072]{1,0:T(8,128)(2,1)S(1)}, f32[1,3072]{1,0:T(1,128)S(1)}) custom-call(s32[6]{0:T(128)S(1)} %stack.24.s, bf16[512,768]{1,0:T(8,128)(2,1)S(1)} %get-tuple-element.123.sl, bf16[3072,768]{1,0:T(8,128)(2,1)} %wo.3, bf16[512,3072]{1,0:T(8,128)(2,1)S(1)} %get-tuple-element.131.dg), custom_call_target="tpu_custom_call" | custom-call | flops 2400000 | bytes 12582 | tf_op jit(solution)/shard_map/slope_inner/pallas_call | solution.py:281
  58.0 1.7 collective-permute-start.5
  59.6 6.7 %weight_inner.1 = (bf16[2,2,2,2,192,384]{5,4,3,2,1,0:T(8,128)(2,1)S(1)}, bf16[2,2,2,2,192,384]{5,4,3,2,1,0:T(8,128)(2,1)S(1)}) custom-call(s32[6]{0:T(128)S(1)} %stack.24.s, bf16[512,768]{1,0:T(8,128)(2,1)S(1)} %get-tuple-element.120.nl, bf16[512,3072]{1,0:T(8,128)(2,1)S(1)} %get-tuple-element.134.si), custom_call_target="tpu_custom_call" | custom-call | flops 2400000 | bytes 10485 | tf_op jit(solution)/shard_map/weight_inner/pallas_call | solution.py:727
  66.3 1.6 collective-permute-done.5
  67.9 1.6 collective-permute-start.6
  69.5 7.2 %slope_first.1 = (f32[512,768]{1,0:T(8,128)S(1)}, bf16[512,768]{1,0:T(8,128)(2,1)S(1)}, f32[3,768]{1,0:T(4,128)S(1)}) custom-call(s32[6]{0:T(128)S(1)} %stack.24.s, bf16[512,3072]{1,0:T(8,128)(2,1)S(1)} %get-tuple-element.134.si, bf16[768,3072]{1,0:T(8,128)(2,1)} %wi.3, f32[512,768]{1,0:T(8,128)S(1)} %get-tuple-element.140.ss, ...), custom_call_target="tpu_custom_call" | custom-call | flops 2400000 | bytes 14680 | tf_op jit(solution)/shard_map/slope_first/pallas_call | solution.py:330
  78.1 1.7 collective-permute-start.9
  80.0 1.6 collective-permute-start.8
  81.7 4.2 %attn_bwd.3 = (bf16[512,256]{1,0:T(8,128)(2,1)S(1)}, bf16[512,256]{1,0:T(8,128)(2,1)S(1)}, bf16[512,256]{1,0:T(8,128)(2,1)S(1)}) custom-call(s32[6]{0:T(128)S(1)} %stack.24.s, bf16[512,768]{1,0:T(8,128)(2,1)S(1)} %get-tuple-element.148.ml, bf16[768,768]{1,0:T(8,128)(2,1)} %wm.7, bf16[512,768]{1,0:T(8,128)(2,1)S(1)} %get-tuple-element.149.q, ...), custom_call_target="tpu_custom_call" | custom-call | flops 1200000 | bytes 5242 | tf_op jit(solution)/shard_map/attn_bwd/pallas_call | solution.py:378
  85.9 4.2 %attn_bwd.4 = (bf16[512,256]{1,0:T(8,128)(2,1)S(1)}, bf16[512,256]{1,0:T(8,128)(2,1)S(1)}, bf16[512,256]{1,0:T(8,128)(2,1)S(1)}) custom-call(s32[6]{0:T(128)S(1)} %stack.24.s, bf16[512,768]{1,0:T(8,128)(2,1)S(1)} %get-tuple-element.148.ml, bf16[768,768]{1,0:T(8,128)(2,1)} %wm.7, bf16[512,768]{1,0:T(8,128)(2,1)S(1)} %get-tuple-element.149.q, ...), custom_call_target="tpu_custom_call" | custom-call | flops 1200000 | bytes 5242 | tf_op jit(solution)/shard_map/attn_bwd/pallas_call | solution.py:378
  90.2 4.2 %attn_bwd.5 = (bf16[512,256]{1,0:T(8,128)(2,1)S(1)}, bf16[512,256]{1,0:T(8,128)(2,1)S(1)}, bf16[512,256]{1,0:T(8,128)(2,1)S(1)}) custom-call(s32[6]{0:T(128)S(1)} %stack.24.s, bf16[512,768]{1,0:T(8,128)(2,1)S(1)} %get-tuple-element.148.ml, bf16[768,768]{1,0:T(8,128)(2,1)} %wm.7, bf16[512,768]{1,0:T(8,128)(2,1)S(1)} %get-tuple-element.149.q, ...), custom_call_target="tpu_custom_call" | custom-call | flops 1200000 | bytes 5242 | tf_op jit(solution)/shard_map/attn_bwd/pallas_call | solution.py:378
  95.0 1.4 collective-permute-start.11
  97.3 8.1 %weight_last.1 = (bf16[2,2,2,2,192,384]{5,4,3,2,1,0:T(8,128)(2,1)S(1)}, bf16[2,2,2,2,192,384]{5,4,3,2,1,0:T(8,128)(2,1)S(1)}, f32[32,384]{1,0:T(8,128)S(1)}) custom-call(s32[6]{0:T(128)S(1)} %stack.24.s, bf16[2,256,768]{2,1,0:T(8,128)(2,1)} %own.3, bf16[256,768]{1,0:T(8,128)(2,1)S(1)} %collective-permute-done.rem, ...), custom_call_target="tpu_custom_call" | custom-call | flops 2400000 | bytes 10485 | tf_op jit(solution)/shard_map/weight_last/pallas_call | solution.py:755
  105.4 2.7 %collective-permute-done.10 = bf16[2,192,384]{2,1,0:T(8,128)(2,1)S(1)} collective-permute-done((bf16[2,192,384]{2,1,0:T(8,128)(2,1)S(1)}, bf16[2,192,384]{2,1,0:T(8,128)(2,1)S(1)}, u32[]{:S(2)}, u32[]{:S(2)}) %collective-permute-start.10) | collective-permute-done | bytes 294944 | tf_op jit(solution)/shard_map/ppermute | solution.py:664
  108.2 2.7 %collective-permute-start.12 = (bf16[192,384]{1,0:T(8,128)(2,1)S(1)}, bf16[192,384]{1,0:T(8,128)(2,1)S(1)}, u32[]{:S(2)}, u32[]{:S(2)}) collective-permute-start(bf16[192,384]{1,0:T(8,128)(2,1)S(1)} %fusion.5), channel_id=1, source_target_pairs={{0,16},{1,17},{2,18},{3,19},{4,20},{5,21},{6,22},{7,23},{8,24},{9,... | collective-permute-start | bytes 442376 | tf_op jit(solution)/shard_map/ppermute | solution.py:664
  111.1 5.4 %input_grad.1 = (f32[2,256,768]{2,1,0:T(8,128)}, bf16[256,768]{1,0:T(8,128)(2,1)S(1)}) custom-call(s32[6]{0:T(128)S(1)} %stack.24.s, bf16[512,256]{1,0:T(8,128)(2,1)S(1)} %get-tuple-element.155.dq0, bf16[512,256]{1,0:T(8,128)(2,1)S(1)} %get-tuple-element.165.dk0, bf16[512,256]{1,0:T(8,128)(2,1)S(1)} %get-tuple-element.166.dv0, ...), custom_call_target="tpu_custom_call" | custom-call | flops 1800000 | bytes 8388 | tf_op jit(solution)/shard_map/input_grad/pallas_call | solution.py:414
  116.5 2.1 %collective-permute-done.12 = bf16[192,384]{1,0:T(8,128)(2,1)S(1)} collective-permute-done((bf16[192,384]{1,0:T(8,128)(2,1)S(1)}, bf16[192,384]{1,0:T(8,128)(2,1)S(1)}, u32[]{:S(2)}, u32[]{:S(2)}) %collective-permute-start.12) | collective-permute-done | bytes 147488 | tf_op jit(solution)/shard_map/ppermute | solution.py:664
  119.6 1.6 collective-permute-start.15
  121.8 1.5 finish.2
  124.1 5.1 %collective-permute-done.16.refs_7_ = bf16[384,384]{1,0:T(8,128)(2,1)S(1)} collective-permute-done((bf16[384,384]{1,0:T(8,128)(2,1)S(1)}, bf16[384,384]{1,0:T(8,128)(2,1)S(1)}, u32[]{:S(2)}, u32[]{:S(2)}) %collective-permute-start.16) | collective-permute-done | bytes 294944 | tf_op jit(solution)/shard_map/ppermute | solution.py:664
  129.2 7.2 %collective-permute-done.15.refs_2_.refs_9_ = bf16[1600,384]{1,0:T(8,128)(2,1)S(1)} collective-permute-done((bf16[1600,384]{1,0:T(8,128)(2,1)S(1)}, bf16[1600,384]{1,0:T(8,128)(2,1)S(1)}, u32[]{:S(2)}, u32[]{:S(2)}) %collective-permute-start.15) | collective-permute-done | bytes 1228832 | tf_op jit(solution)/shard_map/ppermute | solution.py:664
  138.6 8.5 %collective-permute-done.18 = bf16[192,384]{1,0:T(8,128)(2,1)S(1)} collective-permute-done((bf16[192,384]{1,0:T(8,128)(2,1)S(1)}, bf16[192,384]{1,0:T(8,128)(2,1)S(1)}, u32[]{:S(2)}, u32[]{:S(2)}) %collective-permute-start.18) | collective-permute-done | bytes 147488 | tf_op jit(solution)/shard_map/ppermute | solution.py:664
  150.6 6.0 %collective-permute-done.19.refs_4_.refs_6_ = bf16[448,384]{1,0:T(8,128)(2,1)S(1)} collective-permute-done((bf16[448,384]{1,0:T(8,128)(2,1)S(1)}, bf16[448,384]{1,0:T(8,128)(2,1)S(1)}, u32[]{:S(2)}, u32[]{:S(2)}) %collective-permute-start.19) | collective-permute-done | bytes 344096 | tf_op jit(solution)/shard_map/ppermute | solution.py:664
  157.3 2.6 %collective-permute-start.20 = (bf16[256,384]{1,0:T(8,128)(2,1)S(1)}, bf16[256,384]{1,0:T(8,128)(2,1)S(1)}, u32[]{:S(2)}, u32[]{:S(2)}) collective-permute-start(bf16[256,384]{1,0:T(8,128)(2,1)S(1)} %get-tuple-element.208), channel_id=1, source_target_pairs={{0,16},{1,17},{2,18},{3,19},{4,20},{5,21},{6,22},{7,23},{8,24},{9,... | collective-permute-start | bytes 589832 | tf_op jit(solution)/shard_map/ppermute | solution.py:664
  160.6 1.5 finish.3
  162.1 4.8 %collective-permute-done.20.refs_5_.refs_7_ = bf16[256,384]{1,0:T(8,128)(2,1)S(1)} collective-permute-done((bf16[256,384]{1,0:T(8,128)(2,1)S(1)}, bf16[256,384]{1,0:T(8,128)(2,1)S(1)}, u32[]{:S(2)}, u32[]{:S(2)}) %collective-permute-start.20) | collective-permute-done | bytes 196640 | tf_op jit(solution)/shard_map/ppermute | solution.py:664
  (48 shorter events, 20.8 us)
Async XLA Ops:
  1.7 13.0 %collective-permute-start = (bf16[256,768]{1,0:T(8,128)(2,1)S(1)}, bf16[256,768]{1,0:T(8,128)(2,1)S(1)}, u32[]{:S(2)}, u32[]{:S(2)}) collective-permute-start(bf16[256,768]{1,0:T(8,128)(2,1)S(1)} %dynamic-slice_bitcast_fusion.1), channel_id=1, source_target_pairs={{0,1},{1,0},{2,3},{3,2},{4,5},{5,4},{6,7},{7,6},{8,9},{9,8},{10,11... | collective-permute-start | bytes 1179656 | tf_op jit(solution)/shard_map/ppermute | solution.py:653
  5.8 22.4 %collective-permute-start.1 = (bf16[256,768]{1,0:T(8,128)(2,1)S(1)}, bf16[256,768]{1,0:T(8,128)(2,1)S(1)}, u32[]{:S(2)}, u32[]{:S(2)}) collective-permute-start(bf16[256,768]{1,0:T(8,128)(2,1)S(1)} %dynamic-slice_bitcast_fusion), channel_id=1, source_target_pairs={{0,1},{1,0},{2,3},{3,2},{4,5},{5,4},{6,7},{7,6},{8,9},{9,8},{10,11... | collective-permute-start | bytes 1179656 | tf_op jit(solution)/shard_map/ppermute | solution.py:653
  42.9 7.1 %collective-permute-start.2 = (bf16[128,768]{1,0:T(8,128)(2,1)S(1)}, bf16[128,768]{1,0:T(8,128)(2,1)S(1)}, u32[]{:S(2)}, u32[]{:S(2)}) collective-permute-start(bf16[128,768]{1,0:T(8,128)(2,1)S(1)} %get-tuple-element.126), channel_id=1, source_target_pairs={{0,1},{1,0},{2,3},{3,2},{4,5},{5,4},{6,7},{7,6},{8,9},{9,8},{10,11... | collective-permute-start | bytes 589832 | tf_op jit(solution)/shard_map/ppermute | solution.py:653
  50.1 7.4 %collective-permute-start.3 = (bf16[2,2,2,2,192,384]{5,4,3,2,1,0:T(8,128)(2,1)S(1)}, bf16[2,2,2,2,192,384]{5,4,3,2,1,0:T(8,128)(2,1)S(1)}, u32[]{:S(2)}, u32[]{:S(2)}) collective-permute-start(bf16[2,2,2,2,192,384]{5,4,3,2,1,0:T(8,128)(2,1)S(1)} %get-tuple-element.128), channel_id=1, source_target_pairs={{0,2},{2,0},{4,6},{6,4},{8,10},{10,8},{12,14},{14,12},{16,18},{18,... | collective-permute-start | bytes 7077896 | tf_op jit(solution)/shard_map/ppermute | solution.py:654
  50.1 7.3 %collective-permute-start.4 = (bf16[128,768]{1,0:T(8,128)(2,1)S(1)}, bf16[128,768]{1,0:T(8,128)(2,1)S(1)}, u32[]{:S(2)}, u32[]{:S(2)}) collective-permute-start(bf16[128,768]{1,0:T(8,128)(2,1)S(1)} %get-tuple-element.129), channel_id=1, source_target_pairs={{0,1},{1,0},{2,3},{3,2},{4,5},{5,4},{6,7},{7,6},{8,9},{9,8},{10,11... | collective-permute-start | bytes 589832 | tf_op jit(solution)/shard_map/ppermute | solution.py:653
  58.0 9.9 %collective-permute-start.5 = (bf16[2,2,192,384]{3,2,1,0:T(8,128)(2,1)S(1)}, bf16[2,2,192,384]{3,2,1,0:T(8,128)(2,1)S(1)}, u32[]{:S(2)}, u32[]{:S(2)}) collective-permute-start(bf16[2,2,192,384]{3,2,1,0:T(8,128)(2,1)S(1)} %get-tuple-element.232), channel_id=1, source_target_pairs={{0,4},{1,5},{2,3},{3,2},{4,0},{5,1},{6,7},{7,6},{8,12},{9,13},{10,... | collective-permute-start | bytes 1769480 | tf_op jit(solution)/shard_map/ppermute | solution.py:664
  67.9 9.9 %collective-permute-start.7 = (bf16[2,2,2,2,192,384]{5,4,3,2,1,0:T(8,128)(2,1)S(1)}, bf16[2,2,2,2,192,384]{5,4,3,2,1,0:T(8,128)(2,1)S(1)}, u32[]{:S(2)}, u32[]{:S(2)}) collective-permute-start(bf16[2,2,2,2,192,384]{5,4,3,2,1,0:T(8,128)(2,1)S(1)} %get-tuple-element.138), channel_id=1, source_target_pairs={{0,2},{2,0},{4,6},{6,4},{8,10},{10,8},{12,14},{14,12},{16,18},{18,... | collective-permute-start | bytes 7077896 | tf_op jit(solution)/shard_map/ppermute | solution.py:654
  67.9 9.9 %collective-permute-start.6 = (bf16[2,2,192,384]{3,2,1,0:T(8,128)(2,1)S(1)}, bf16[2,2,192,384]{3,2,1,0:T(8,128)(2,1)S(1)}, u32[]{:S(2)}, u32[]{:S(2)}) collective-permute-start(bf16[2,2,192,384]{3,2,1,0:T(8,128)(2,1)S(1)} %get-tuple-element.137), channel_id=1, source_target_pairs={{0,4},{1,5},{2,3},{3,2},{4,0},{5,1},{6,7},{7,6},{8,12},{9,13},{10,... | collective-permute-start | bytes 1769480 | tf_op jit(solution)/shard_map/ppermute | solution.py:664
  78.1 16.6 %collective-permute-start.9 = (bf16[2,2,2,192,384]{4,3,2,1,0:T(8,128)(2,1)S(1)}, bf16[2,2,2,192,384]{4,3,2,1,0:T(8,128)(2,1)S(1)}, u32[]{:S(2)}, u32[]{:S(2)}) collective-permute-start(bf16[2,2,2,192,384]{4,3,2,1,0:T(8,128)(2,1)S(1)} %fusion), channel_id=1, source_target_pairs={{0,4},{1,5},{2,3},{3,2},{4,0},{5,1},{6,7},{7,6},{8,12},{9,13},{10,... | collective-permute-start | bytes 3538952 | tf_op jit(solution)/shard_map/ppermute | solution.py:664
  80.0 14.7 %collective-permute-start.8 = (bf16[2,2,192,384]{3,2,1,0:T(8,128)(2,1)S(1)}, bf16[2,2,192,384]{3,2,1,0:T(8,128)(2,1)S(1)}, u32[]{:S(2)}, u32[]{:S(2)}) collective-permute-start(bf16[2,2,192,384]{3,2,1,0:T(8,128)(2,1)S(1)} %fusion.2), channel_id=1, source_target_pairs={{0,8},{1,9},{2,10},{3,11},{4,12},{5,13},{6,14},{7,15},{8,0},{9,1},... | collective-permute-start | bytes 1769480 | tf_op jit(solution)/shard_map/ppermute | solution.py:664
  95.0 13.1 %collective-permute-start.11 = (bf16[2,2,192,384]{3,2,1,0:T(8,128)(2,1)S(1)}, bf16[2,2,192,384]{3,2,1,0:T(8,128)(2,1)S(1)}, u32[]{:S(2)}, u32[]{:S(2)}) collective-permute-start(bf16[2,2,192,384]{3,2,1,0:T(8,128)(2,1)S(1)} %fusion.1), channel_id=1, source_target_pairs={{0,1},{1,0},{2,6},{3,7},{4,5},{5,4},{6,2},{7,3},{8,9},{9,8},{10,14... | collective-permute-start | bytes 1769480 | tf_op jit(solution)/shard_map/ppermute | solution.py:664
  96.5 11.6 %collective-permute-start.10 = (bf16[2,192,384]{2,1,0:T(8,128)(2,1)S(1)}, bf16[2,192,384]{2,1,0:T(8,128)(2,1)S(1)}, u32[]{:S(2)}, u32[]{:S(2)}) collective-permute-start(bf16[2,192,384]{2,1,0:T(8,128)(2,1)S(1)} %fusion.3), channel_id=1, source_target_pairs={{0,1},{1,0},{2,6},{3,7},{4,5},{5,4},{6,2},{7,3},{8,9},{9,8},{10,14... | collective-permute-start | bytes 884744 | tf_op jit(solution)/shard_map/ppermute | solution.py:664
  108.1 10.5 %collective-permute-start.13 = (bf16[2,2,2,2,192,384]{5,4,3,2,1,0:T(8,128)(2,1)S(1)}, bf16[2,2,2,2,192,384]{5,4,3,2,1,0:T(8,128)(2,1)S(1)}, u32[]{:S(2)}, u32[]{:S(2)}) collective-permute-start(bf16[2,2,2,2,192,384]{5,4,3,2,1,0:T(8,128)(2,1)S(1)} %get-tuple-element.179), channel_id=1, source_target_pairs={{0,2},{2,0},{4,6},{6,4},{8,10},{10,8},{12,14},{14,12},{16,18},{18,... | collective-permute-start | bytes 7077896 | tf_op jit(solution)/shard_map/ppermute | solution.py:654
  108.2 10.4 %collective-permute-start.12 = (bf16[192,384]{1,0:T(8,128)(2,1)S(1)}, bf16[192,384]{1,0:T(8,128)(2,1)S(1)}, u32[]{:S(2)}, u32[]{:S(2)}) collective-permute-start(bf16[192,384]{1,0:T(8,128)(2,1)S(1)} %fusion.5), channel_id=1, source_target_pairs={{0,16},{1,17},{2,18},{3,19},{4,20},{5,21},{6,22},{7,23},{8,24},{9,... | collective-permute-start | bytes 442376 | tf_op jit(solution)/shard_map/ppermute | solution.py:664
  110.9 5.6 %collective-permute-start.14 = (f32[32,384]{1,0:T(8,128)S(1)}, f32[32,384]{1,0:T(8,128)S(1)}, u32[]{:S(2)}, u32[]{:S(2)}) collective-permute-start(f32[32,384]{1,0:T(8,128)S(1)} %get-tuple-element.180.refs_6_), channel_id=1, source_target_pairs={{0,2},{2,0},{4,6},{6,4},{8,10},{10,8},{12,14},{14,12},{16,18},{18,... | collective-permute-start | bytes 147464 | tf_op jit(solution)/shard_map/ppermute | solution.py:654
  119.6 16.8 %collective-permute-start.15 = (bf16[1600,384]{1,0:T(8,128)(2,1)S(1)}, bf16[1600,384]{1,0:T(8,128)(2,1)S(1)}, u32[]{:S(2)}, u32[]{:S(2)}) collective-permute-start(bf16[1600,384]{1,0:T(8,128)(2,1)S(1)} %get-tuple-element.188), channel_id=1, source_target_pairs={{0,4},{1,5},{2,3},{3,2},{4,0},{5,1},{6,7},{7,6},{8,12},{9,13},{10,... | collective-permute-start | bytes 3686408 | tf_op jit(solution)/shard_map/ppermute | solution.py:664
  121.1 8.1 %collective-permute-start.16 = (bf16[384,384]{1,0:T(8,128)(2,1)S(1)}, bf16[384,384]{1,0:T(8,128)(2,1)S(1)}, u32[]{:S(2)}, u32[]{:S(2)}) collective-permute-start(bf16[384,384]{1,0:T(8,128)(2,1)S(1)} %get-tuple-element.189), channel_id=1, source_target_pairs={{0,8},{1,9},{2,10},{3,11},{4,12},{5,13},{6,14},{7,15},{8,0},{9,1},... | collective-permute-start | bytes 884744 | tf_op jit(solution)/shard_map/ppermute | solution.py:664
  137.2 10.5 %collective-permute-start.17 = (bf16[832,384]{1,0:T(8,128)(2,1)S(1)}, bf16[832,384]{1,0:T(8,128)(2,1)S(1)}, u32[]{:S(2)}, u32[]{:S(2)}) collective-permute-start(bf16[832,384]{1,0:T(8,128)(2,1)S(1)} %get-tuple-element.199), channel_id=1, source_target_pairs={{0,1},{1,0},{2,6},{3,7},{4,5},{5,4},{6,2},{7,3},{8,9},{9,8},{10,14... | collective-permute-start | bytes 1916936 | tf_op jit(solution)/shard_map/ppermute | solution.py:664
  138.6 8.5 %collective-permute-start.18 = (bf16[192,384]{1,0:T(8,128)(2,1)S(1)}, bf16[192,384]{1,0:T(8,128)(2,1)S(1)}, u32[]{:S(2)}, u32[]{:S(2)}) collective-permute-start(bf16[192,384]{1,0:T(8,128)(2,1)S(1)} %get-tuple-element.200), channel_id=1, source_target_pairs={{0,16},{1,17},{2,18},{3,19},{4,20},{5,21},{6,22},{7,23},{8,24},{9,... | collective-permute-start | bytes 442376 | tf_op jit(solution)/shard_map/ppermute | solution.py:664
  148.4 8.2 %collective-permute-start.19 = (bf16[448,384]{1,0:T(8,128)(2,1)S(1)}, bf16[448,384]{1,0:T(8,128)(2,1)S(1)}, u32[]{:S(2)}, u32[]{:S(2)}) collective-permute-start(bf16[448,384]{1,0:T(8,128)(2,1)S(1)} %get-tuple-element.204), channel_id=1, source_target_pairs={{0,8},{1,9},{2,10},{3,11},{4,12},{5,13},{6,14},{7,15},{8,0},{9,1},... | collective-permute-start | bytes 1032200 | tf_op jit(solution)/shard_map/ppermute | solution.py:664
  149.2 11.4 %collective-permute-start.21 = (bf16[256,768]{1,0:T(8,128)(2,1)S(1)}, bf16[256,768]{1,0:T(8,128)(2,1)S(1)}, u32[]{:S(2)}, u32[]{:S(2)}) collective-permute-start(bf16[256,768]{1,0:T(8,128)(2,1)S(1)} %get-tuple-element.211), channel_id=1, source_target_pairs={{0,1},{1,0},{2,3},{3,2},{4,5},{5,4},{6,7},{7,6},{8,9},{9,8},{10,11... | collective-permute-start | bytes 1179656 | tf_op jit(solution)/shard_map/ppermute | solution.py:653
  157.3 9.6 %collective-permute-start.20 = (bf16[256,384]{1,0:T(8,128)(2,1)S(1)}, bf16[256,384]{1,0:T(8,128)(2,1)S(1)}, u32[]{:S(2)}, u32[]{:S(2)}) collective-permute-start(bf16[256,384]{1,0:T(8,128)(2,1)S(1)} %get-tuple-element.208), channel_id=1, source_target_pairs={{0,16},{1,17},{2,18},{3,19},{4,20},{5,21},{6,22},{7,23},{8,24},{9,... | collective-permute-start | bytes 589832 | tf_op jit(solution)/shard_map/ppermute | solution.py:664

commit v3 on v2

--- a/solution.py
+++ b/solution.py
@@ -59,7 +59,7 @@
     return pl.BlockSpec((1, rows, width), lambda g, s: (s[0], 0, 0))
 
 
-def call(body, grid, in_specs, out_specs, out_shape, scratch, name, flops, nbytes, trans=0, aliases=None):
+def call(body, grid, in_specs, out_specs, out_shape, scratch, name, flops, nbytes, trans=0, aliases=None, vmem=VMEM_LIMIT):
     return pl.pallas_call(
         body,
         grid_spec=pltpu.PrefetchScalarGridSpec(
@@ -71,7 +71,7 @@
         ),
         out_shape=out_shape,
         input_output_aliases=aliases or {},
-        compiler_params=pltpu.CompilerParams(vmem_limit_bytes=VMEM_LIMIT),
+        compiler_params=pltpu.CompilerParams(vmem_limit_bytes=vmem),
         cost_estimate=pl.CostEstimate(flops=flops // 1000, bytes_accessed=nbytes // 1000, transcendentals=0),
         name=name,
     )
@@ -242,7 +242,7 @@
     t, d = nl.shape
     ff = wi.shape[1]
     half = t // 2
-    w = 512
+    w = 1024
     return call(
         mlp_fwd_body,
         (ff // w,),
@@ -265,6 +265,7 @@
         4_800_000_000,
         24 << 20,
         2 << 20,
+        vmem=30 << 20,
     )(s, nl, wi, bi, wo, bo, n1, g1, b1, g2, b2, cot, cot_rem)
 
 
@@ -369,41 +370,33 @@
     dq_o[...] = jnp.concatenate(dqs, 0).astype(BF).T
 
 
-def attn_bwd(g, s, ml, wm, q, kt, v, e, il, ctx):
+def attn_bwd(s, ml, wm, q, kt, v, e, il, ctx):
     t, d = ml.shape
-
-    def at_col(rows):
-        return pl.BlockSpec((rows, 256), lambda i, s: (0, g))
-
     return call(
         attn_bwd_body,
-        (1,),
+        (d // 256,),
         [
             full((t, d)),
-            pl.BlockSpec((256, d), lambda i, s: (g, 0)),
-            at_col(t),
-            pl.BlockSpec((256, t), lambda i, s: (g, 0)),
-            at_col(t),
-            pl.BlockSpec((4, t, t), lambda i, s: (g, 0, 0)),
-            pl.BlockSpec((4, 1, t), lambda i, s: (g, 0, 0)),
-            at_col(t),
+            rows_of(256, d),
+            cols(t, 256),
+            rows_of(256, t),
+            cols(t, 256),
+            pl.BlockSpec((4, t, t), lambda g, s: (g, 0, 0)),
+            pl.BlockSpec((4, 1, t), lambda g, s: (g, 0, 0)),
+            cols(t, 256),
         ],
-        [full((t, 256))] * 3,
-        [shape((t, 256), BF)] * 3,
+        [cols(t, 256)] * 3,
+        [shape((t, d), BF)] * 3,
         [],
         "attn_bwd",
-        1_200_000_000,
-        5 << 20,
+        3_600_000_000,
+        15 << 20,
     )(s, ml, wm, q, kt, v, e, il, ctx)
 
 
-def input_grad_body(s, dq0, dk0, dv0, dq1, dk1, dv1, dq2, dk2, dv2, wq, wk, wv, sm, own_o, rem_o):
+def input_grad_body(s, dq, dk, dv, wq, wk, wv, sm, own_o, rem_o):
     half = sm.shape[0] // 2
-    w = dq0.shape[1]
-    total = sm[...]
-    for g, (dq, dk, dv) in enumerate(((dq0, dk0, dv0), (dq1, dk1, dv1), (dq2, dk2, dv2))):
-        at = slice(g * w, g * w + w)
-        total += nt(dq[...], wq[:, at]) + nt(dk[...], wk[:, at]) + nt(dv[...], wv[:, at])
+    total = sm[...] + nt(dq[...], wq[...]) + nt(dk[...], wk[...]) + nt(dv[...], wv[...])
     own_o[0] = total[:half]
     rem_o[...] = total[half:].astype(BF)
 
@@ -414,7 +407,7 @@
     return call(
         input_grad_body,
         (1,),
-        [full((t, 256))] * 9 + [full((d, d))] * 3 + [full((t, d))],
+        [full((t, d))] * 3 + [full((d, d))] * 3 + [full((t, d))],
         [own_slot(half, d), full((half, d))],
         [shape((2, half, d), F32), shape((half, d), BF)],
         [],
@@ -428,32 +421,43 @@
 XZY = (("x", "z1", "y", "z2"), ("y", "z1", "x", "z2"))
 
 
-def place(s, core, order, x, y, z1, z2):
-    far = {"x": x ^ s[3], "y": y ^ s[0], "z1": z1 ^ s[4], "z2": z2 ^ s[5]}
-    return [far[p] if p == q else jnp.where(core == 0, far[p], far[q]) for p, q in zip(*order)]
+def meets(s, core, a, f):
+    return jnp.where(core == 0, a, f) ^ s[3], jnp.where(core == 0, f, a) ^ s[0]
 
 
 def outer_jobs(s, core, j):
-    for x in range(2):
-        for y in range(2):
-            yield place(s, core, XZY, x, y, j & 1, j >> 1), (2 * x + core) * 192, 192, y * 384, 0
-
-
-def thin_jobs(s, core, ys, ats):
-    for r in range(8):
-        for p in range(2):
-            where = place(s, core, XY, r & 1, ys[p], (r >> 1) & 1, r >> 2)
-            yield where, (2 * r + core) * 48, 48, 384 * p, ats[p]
+    for a in range(2):
+        for f in range(2):
+            x, y = meets(s, core, a, f)
+            yield a, ((j & 1) ^ s[4], f, (j >> 1) ^ s[5]), (2 * x + core) * 192, 192, y * 384, 0
+
+
+def thin_jobs(s, core, j):
+    at = pl.multiple_of(j * 48, 16)
+    for a in range(2):
+        for f in range(2):
+            x, y = meets(s, core, a, f)
+            for e in range(2):
+                for g in range(2):
+                    row = (8 * (g ^ s[5]) + 4 * (e ^ s[4]) + 2 * x + core) * 48
+                    yield a, (f, e, g), row, 48, y * 384, at
 
 
 def flush(s, tile, outs, sems, jobs_of):
     copies = []
-    for away, out in enumerate(outs):
-        for where, row, height, col, at in jobs_of(s[2] ^ away):
+    keep, *send = outs
+    for away in range(2):
+        for a, rest, row, height, col, at in jobs_of(s[2] ^ away):
+            where = (a, *rest)
+            out = keep.at[*where]
+            if away:
+                split = {1: 0, 2: 1, 4: 2}[len(send)]
+                index = sum(i << (split - 1 - n) for n, i in enumerate(where[:split]))
+                out = send[index].at[*where[split:]]
             copies.append(
                 pltpu.make_async_copy(
-                    tile.at[pl.ds(pl.multiple_of(row, 16), height), pl.ds(col, 384)],
-                    out.at[*where, pl.ds(at, height)],
+                    tile.at[pl.ds(pl.multiple_of(row, 16), height), pl.ds(pl.multiple_of(col, 128), 384)],
+                    out.at[pl.ds(at, height)],
                     sems.at[len(copies)],
                 )
             )
@@ -490,19 +494,15 @@
     run_tiles(s, 4, tiles, sems, (keep, send), fill, lambda core, step: outer_jobs(s, core, step))
 
 
-def inner_body(s, nl, si, keep, send, tiles, sems):
-    def jobs_of(core, step):
-        base = pl.multiple_of((step & 1) * 96, 16)
-        return thin_jobs(s, core, (step >> 1, step >> 1), (base, pl.multiple_of(base + 48, 16)))
-
+def inner_body(s, nl, si0, si1, keep, send0, send1, tiles, sems):
     def fill(_, tile):
-        tile[...] = tn(nl[...], si[...]).astype(BF)
-
-    run_tiles(s, 4, tiles, sems, (keep, send), fill, jobs_of)
-
-
-def last_body(s, own, rem, dq0, dk0, dv0, dq1, dk1, dv1, dq2, dk2, dv2, ctx, ml, v2, v1, bi,
-              keep, send, vec_o, tiles, sems, xs):
+        tile[...] = tn(nl[...], jnp.concatenate([si0[...], si1[...]], 1)).astype(BF)
+
+    run_tiles(s, 4, tiles, sems, (keep, send0, send1), fill, lambda core, step: thin_jobs(s, core, step))
+
+
+def last_body(s, own, rem, dq, dk, dv, ctx, ml, v2, v1, bi,
+              keep, send0, send1, send2, send3, vec_o, tiles, sems, xs):
     half, d = rem.shape
 
     def put(row, value):
@@ -520,37 +520,32 @@
             put(8 + i, bi[:, i * d : i * d + d])
         vec_o[24:] = jnp.zeros((8, 384), F32)
 
-    def jobs_of(core, step):
-        at = pl.multiple_of(step * 48, 16)
-        return thin_jobs(s, core, (0, 1), (at, at))
-
     def fill(j, tile):
-        for one, parts in enumerate(((dq0, dq1, dq2), (dk0, dk1, dk2), (dv0, dv1, dv2))):
+        for one, part in enumerate((dq, dk, dv)):
 
             @pl.when(j == one)
             def _():
-                for g, part in enumerate(parts):
-                    tile[:, g * 256 : g * 256 + 256] = tn(xs[...], part[...]).astype(BF)
+                tile[...] = tn(xs[...], part[...]).astype(BF)
                 if one != 1:
-                    ones = jnp.ones((8, 2 * half), BF)
-                    put(one // 2, jnp.concatenate([nn(ones, part[...])[:1] for part in parts], 1))
+                    put(one // 2, nn(jnp.ones((8, 2 * half), BF), part[...])[:1])
 
         @pl.when(j == 3)
         def _():
             tile[...] = tn(ctx[...], ml[...]).astype(BF)
 
-    run_tiles(s, 4, tiles, sems, (keep, send), fill, jobs_of)
-
-
-def weight_call(body, in_specs, jobs, name, flops, scratch=(), extra=()):
+    sends = (send0, send1, send2, send3)
+    run_tiles(s, 4, tiles, sems, (keep, *sends), fill, lambda core, step: thin_jobs(s, core, step))
+
+
+def weight_call(body, in_specs, jobs, name, flops, scratch=(), extra=(), sends=1):
     block = (2, 2, 2, 2, 192, 384)
     hbm = pl.BlockSpec(memory_space=pl.ANY)
     return call(
         body,
         (4,),
         in_specs,
-        [hbm] * 2 + [full(dims) for dims in extra],
-        [shape(block, BF)] * 2 + [shape(dims, F32) for dims in extra],
+        [hbm] * (1 + sends) + [full(dims) for dims in extra],
+        [shape(block, BF)] + [shape(block[sends.bit_length() - 1 :], BF)] * sends + [shape(dims, F32) for dims in extra],
         [pltpu.VMEM((2, 768, 768), BF), pltpu.SemaphoreType.DMA((2, 2 * jobs))] + list(scratch),
         name,
         flops,
@@ -558,53 +553,63 @@
     )
 
 
-def vec_terms(vec, vec_in):
-    got = vec_in[...].astype(F32)
-    return vec[...] + (got if got.shape[0] == 32 else got[:32] + got[32:])
+VECTORS = (0, 1, 7, 8, 4, 5, 6, 2, 3)
 
 
 def combine_body(counts, last, s, *refs):
     ins, vec, vec_in = refs[: sum(counts)], refs[sum(counts)], refs[sum(counts) + 1]
     outs = refs[sum(counts) + 2 :]
+    new = vec[...] + vec_in[...].astype(F32)
     at = 0
     for i, count in enumerate(counts):
-        total = sum(ref[...].astype(F32) for ref in ins[at : at + count])
+        parts = ins[at : at + count]
         at += count
-        if last:
-            for j in range(4):
-                outs[j][...] = total[j * 48 : j * 48 + 48]
-        else:
-            outs[i][: total.shape[0]] = total.astype(BF)
-    new = vec_terms(vec, vec_in)
-    if last:
-        outs[-1][:, :384] = new[:12]
-        outs[-1][:, 384:] = new[12:24]
+        step = min(part.shape[0] for part in parts)
+        for n in range(parts[0].shape[0] // step):
+            rows = slice(n * step, n * step + step)
+            pieces = [part for part in parts if part.shape[0] < parts[0].shape[0]]
+            terms = [part[rows] for part in parts if part.shape[0] == parts[0].shape[0]]
+            terms += [pieces[n][...]] if pieces else []
+            total = sum(u.astype(F32) for u in terms)
+            if last:
+                for j in range(4):
+                    outs[j][...] = total[j * 48 : j * 48 + 48]
+            else:
+                outs[i][rows] = total.astype(BF)
+    if last and len(outs) == 5:
+        outs[4][:, :384] = new[:12]
+        outs[4][:, 384:] = new[12:24]
+    elif last:
+        for out, first in zip(outs[4:], VECTORS):
+            for i in range(out.shape[0] // 768):
+                out[i * 768 : i * 768 + 384] = new[first + i]
+                out[i * 768 + 384 : i * 768 + 768] = new[12 + first + i]
     else:
+        outs[0][outs[0].shape[0] - 32 :] = new.astype(BF)
         outs[-1][...] = new
-        height = outs[0].shape[0]
-        high = new.astype(BF)
-        outs[0][height - 64 : height - 32] = high
-        outs[0][height - 32 :] = (new - high.astype(F32)).astype(BF)
-
-
-def combine(s, groups, vec, vec_in, last=False):
+
+
+def combine(s, groups, vec, vec_in, last=False, apart=False):
     specs, args, outs = [], [], []
-    for parts, height, at in groups:
-        specs += [pl.BlockSpec((height, 384), lambda g, s, at=at: (at, 0))] * len(parts)
-        args += [part.reshape(-1, 384) for part in parts]
+    for height, parts in groups:
+        for part, at in parts:
+            rows = part.size // 384
+            size = min(rows, height)
+            specs.append(pl.BlockSpec((size, 384), lambda g, s, at=at: (at, 0)))
+            args.append(part.reshape(rows, 384))
         outs.append(shape((height, 384), BF))
     if last:
-        outs = [shape((48, 384), F32)] * 4 + [shape((12, 768), F32)]
+        outs = [shape((48, 384), F32)] * 4
+        outs += [shape((3072 if i == 8 else 768,), F32) for i in VECTORS] if apart else [shape((12, 768), F32)]
     else:
-        outs[0] = shape((groups[0][1] + 64, 384), BF)
+        outs[0] = shape((groups[0][0] + 32, 384), BF)
         outs.append(shape((32, 384), F32))
     rows = vec_in.shape[0]
-    tail = full((32, 384)) if rows == 32 else pl.BlockSpec((64, 384), lambda g, s: (rows // 64 - 1, 0))
     return call(
-        functools.partial(combine_body, [len(parts) for parts, *_ in groups], last),
+        functools.partial(combine_body, [len(parts) for _, parts in groups], last),
         (1,),
-        specs + [full((32, 384)), tail],
-        [full(o.shape) for o in outs],
+        specs + [full((32, 384)), pl.BlockSpec((32, 384), lambda g, s: (rows // 32 - 1, 0))],
+        [whole_vec(*o.shape) if len(o.shape) == 1 else full(o.shape) for o in outs],
         outs,
         [],
         "combine",
@@ -711,9 +716,6 @@
         def send(self):
             self.got.append(self.away(self.going))
 
-        def done(self):
-            return self.total((0, 0, 0, 0))
-
     got0 = trade(out0, "y")
     r1 = Reduce(weight_call(outer_body, [piece, hold], 4, "weight_outer", 2_400_000_000)(s, act, sl), XZY)
     r1.going, got0, out1 = together(r1.going, got0, out1)
@@ -723,81 +725,84 @@
 
     r1.got[-1], got1, bi = together(r1.got[-1], got1, bi)
     r1.add()
-    early = r1.away(r1.going[1])
-    r2 = Reduce(weight_call(inner_body, [hold, piece], 16, "weight_inner", 2_400_000_000)(
-        after(s, r1.going), nl, si), XY)
-
-    early, r2.going, rest = together(early, r2.going, r1.going[0])
-    late = r1.away(rest)
+    r1.send()
+    pieces = [pl.BlockSpec((t, 384), lambda g, s, y=y: (0, 4 * y + g)) for y in range(2)]
+    keep, *parts = weight_call(inner_body, [hold] + pieces, 16, "weight_inner", 2_400_000_000, sends=2)(
+        after(s, r1.going), nl, si, si)
+    core = [trade(part, 1) for part in parts]
+    sm, ml, v1 = slope_first(after(s, *parts), si, inner_weight, ss, n1, rs, g1)
+
+    r1.got[-1], core[0], core[1], v1 = together(r1.got[-1], *core, v1)
+    r1.add()
+    r1.send()
+    r2 = Reduce((keep, None), XY)
+    r2.got.append(core[1])
+    r2.going = (keep[1].astype(F32) + core[1].astype(F32)).astype(BF)
+    r2.got[1] = core[0][None]
     r2.send()
-    sm, ml, v1 = slope_first(after(s, r2.going), si, inner_weight, ss, n1, rs, g1)
-
-    early, late, r2.got[-1], v1 = together(early, late, r2.got[-1], v1)
-    r1.got.append([late, early])
-    r1.total = lambda index: sum(
-        (a[index[1]][index[2:]] if i == 2 else a[index[max(i - 1, 0):]]).astype(F32) for i, a in enumerate(r1.got))
+    back = (mixer_weight, q, kt, v, e, il, ctx)
+    slopes = attn_bwd(after(s, r1.going, r2.going), ml, *back)
+
+    r1.got[-1], r2.got[-1], *slopes = together(r1.got[-1], r2.got[-1], *slopes)
     r1.add()
     r1.send()
     r2.add()
     r2.send()
-    back = (mixer_weight, q, kt, v, e, il, ctx)
-    first = attn_bwd(0, after(s, r1.going, r2.going), ml, *back)
-    second = attn_bwd(1, after(s, first[0]), ml, *back)
-    third = attn_bwd(2, after(s, second[0]), ml, *back)
-
-    r1.got[-1], r2.got[-1], *third = together(r1.got[-1], r2.got[-1], *third)
-    slopes = (*first, *second, *third)
-    r1.add()
+    keep, *parts, vec = weight_call(
+        last_body, [own_slot(half, d), full((half, d))] + [hold] * 5 + [full((3, d))] * 2 + [full((1, 4 * d))],
+        16, "weight_last", 2_400_000_000, [pltpu.VMEM((t, d), BF)], [(32, 384)], sends=4)(
+            after(s, r1.going, r2.going), tokens, rem, *slopes, ctx, ml, v2, v1, bi)
+
+    def at(index, *values):
+        return [(value, index) for value in values]
+
+    r1.got[-1], parts[2], parts[3], vec = together(r1.got[-1], parts[2], parts[3], vec)
+    core = [None, None, trade(parts[2], 1), trade(parts[3], 1)]
+    vec_got = trade(vec, 1)
+
+    r1.got[-1], r2.got[-1], core[2], core[3], vec_got = together(
+        r1.got[-1], r2.got[-1], core[2], core[3], vec_got)
+    rows = keep.size // 384 // 2
+    r3 = Reduce((keep, None), XY)
+    r3.got.append(None)
+    going, r2.going, r1.going, vec = combine(
+        s,
+        [(rows, at(1, keep) + at(0, core[2], core[3])), (rows // 4, at(1, *r2.got)), (rows // 8, at(1, *r1.got))],
+        vec, vec_got)
+    r3.got.append(r3.away(going))
+    core[:2] = [trade(after(part, going), 1) for part in parts[:2]]
+    r2.send()
     r1.send()
-    r2.add()
-    r2.send()
-    quarter = [full((t, 256))] * 9
-    *made, vec = weight_call(
-        last_body, [own_slot(half, d), full((half, d))] + quarter + [hold] * 2 + [full((3, d))] * 2 + [full((1, 4 * d))],
-        16, "weight_last", 2_400_000_000, [pltpu.VMEM((t, d), BF)], [(32, 384)])(
-            after(s, r1.going, r2.going), tokens, rem, *slopes, ctx, ml, v2, v1, bi)
-    r3 = Reduce(made, XY)
-
-    r1.got[-1], r2.got[-1], r3.going, vec = together(r1.got[-1], r2.got[-1], r3.going, vec)
-    r1.add()
-    r1.send()
-    r3.send()
-    vec_got = trade(vec, 1)
-    grad, grad_rem = input_grad(
-        after(s, r1.going, r3.going), slopes, query_weight, key_weight, value_weight, sm)
-
-    r1.got[-1], r3.got[-1], vec_got, grad_rem, r2.got[-1] = together(
-        r1.got[-1], r3.got[-1], vec_got, grad_rem, r2.got[-1])
-    rows = r3.going.size // 384 // 2
+    grad, grad_rem = input_grad(after(s, going, *parts[:2]), slopes, query_weight, key_weight, value_weight, sm)
+
+    r3.got[-1], core[0], core[1], r2.got[-1], r1.got[-1], grad_rem = together(
+        r3.got[-1], core[0], core[1], r2.got[-1], r1.got[-1], grad_rem)
     going, r2.going, vec = combine(
-        s, [(r3.got, rows, 1), (r2.got, rows // 4, 1)], vec, vec_got)
+        s, [(rows // 2, at(1, keep, r3.got[-1]) + at(0, core[1])), (rows // 8, at(1, *r2.got))], vec, r3.got[-1])
+    r3.got[1] = core[0]
     r3.got.append(r3.away(going))
     r2.send()
-    outer = r1.done()
-    out = finish(after(s, going), (got0, got1), out)
+    outer = sum(u.reshape(-1, 384)[: rows // 8].astype(F32) for u in r1.got)
+    out = finish(after(s, going, r2.going), (got0, got1), out)
 
     r3.got[-1], r2.got[-1], out, outer = together(r3.got[-1], r2.got[-1], out, outer)
-    going, r2.going, vec = combine(
-        s, [(r3.got, rows // 2, 1), (r2.got, rows // 8, 1)], vec, r3.got[-1])
-    r3.got.append(r3.away(going))
-    r2.send()
-
-    r3.got[-1], r2.got[-1], grad_rem = together(r3.got[-1], r2.got[-1], grad_rem)
-    going, vec = combine(s, [(r3.got, rows // 4, 1)], vec, r3.got[-1])
+    going, vec = combine(s, [(rows // 4, at(1, *r3.got))], vec, r3.got[-1])
     r3.got.append(r3.away(going))
     grad_got = trade(after(grad_rem, going), "y")
-    inner = sum(u.reshape(-1, 384)[: rows // 8].astype(F32) for u in r2.got)
-
-    r3.got[-1], inner = together(r3.got[-1], inner)
-    going, vec = combine(s, [(r3.got, rows // 8, 1)], vec, r3.got[-1])
+
+    going, vec = combine(s, [(rows // 8, at(1, *r3.got))], vec, r3.got[-1])
     r3.got.append(r3.away(going))
+    inner = sum(after(u, going).reshape(-1, 384)[: rows // 8].astype(F32) for u in r2.got)
     grad = finish(after(s, going), (grad_got,), grad)
 
-    r3.got[-1], grad = together(r3.got[-1], grad)
-    *weights, vec = combine(s, [(r3.got, rows // 8, 0)], vec, r3.got[-1], last=True)
-
-    inner_own = jnp.concatenate([inner[i * 48 : i * 48 + 48] for i in range(4)], 1)
-    weights += [inner_own, outer]
+    inner = jnp.concatenate([inner[i * 48 : i * 48 + 48] for i in range(4)], 1)
+    r3.got[-1], grad, inner = together(r3.got[-1], grad, inner)
+    apart = low_n == 1
+    sums = combine(s, [(rows // 8, at(0, *r3.got))], vec, r3.got[-1], last=True, apart=apart)
+    weights = [*sums[:4], inner, outer]
+    if apart:
+        return (out, grad, *weights, *sums[4:])
+    vec = sums[4]
     step = low_n // 2
     while step >= 1:
         bit = (dp // step) % 2
@@ -810,7 +815,7 @@
         weights = rest
         vec = vec + lax.ppermute(vec, "dp", [(i, i ^ step) for i in range(n)])
         step //= 2
-    return (out, grad, *weights, vec[0], vec[1], vec[7], vec[8:].reshape(-1), vec[4], vec[5], vec[6], vec[2], vec[3])
+    return (out, grad, *weights, *(vec[8:].reshape(-1) if i == 8 else vec[i] for i in VECTORS))
 
 
 def solution(mesh):

time: 170 us -> 154 us (0.906)
  waiting for transfers between devices: 46.9 us -> 32.8 us
  Pallas kernels: 87.6 us -> 84.4 us
  starting transfers between devices: 25.6 us -> 28.7 us
  local copies, waits for them, and re-layouts: 5.43 us -> 3.39 us
    ppermute x13 -> x12, waiting for transfers between devices: 40 us -> 22.9 us  [trade_stage(): return lax.ppermute(value, ('dp', 'seq'), pairs)]
    ppermute x4 -> x8, waiting for transfers between devices: 0.01 us -> 2.35 us  [trade(): return lax.ppermute(value, 'dp', [(i, i ^ bit * low_n) for i in range(n)])]
    pallas_call x11 -> x9, Pallas kernels: 37.4 us -> 35.2 us  [the longest x1 9.93 us: attn_bwd(): call(attn_bwd_body, (d // 256,), [full((t, d)), rows_of(256, d), cols(t,...]
    ppermute x13 -> x12, starting transfers between devices: 18.3 us -> 20.4 us  [trade_stage(): return lax.ppermute(value, ('dp', 'seq'), pairs)]
  transfers between devices with their start and end apart: 22 -> 25, of which waited for: 12 -> 10; matrix products, arithmetic and copies ran while one was open for 3% -> 3% of each run, Pallas kernels for 41% -> 44%
where the time goes in v3:
time: 154 us; the launch traced here: 153 us
  Pallas kernels  84.4 us (55%)
  waiting for transfers between devices  32.8 us (21%)
  starting transfers between devices  28.7 us (19%)
  local copies, waits for them, and re-layouts  3.39 us (2%)
  other arithmetic  2.95 us (2%)
    ppermute x12, waiting for transfers between devices, trade_stage(): return lax.ppermute(value, ('dp', 'seq'), pairs)  22.9 us
    ppermute x12, starting transfers between devices, trade_stage(): return lax.ppermute(value, ('dp', 'seq'), pairs)  20.4 us
    pallas_call x1, Pallas kernels, mlp_fwd(): call(mlp_fwd_body, (ff // w,), [full((t, d)), cols(d, w), vec(w), rows_of...  13.6 us
    pallas_call x1, Pallas kernels, attn_fwd(): call(attn_fwd_body, (d // 256,), [own_slot(half, d), full((half, d))] + [...  13.5 us
    pallas_call x1, Pallas kernels, attn_bwd(): call(attn_bwd_body, (d // 256,), [full((t, d)), rows_of(256, d), cols(t,...  9.93 us
    pallas_call x1, Pallas kernels, local(): weight_call(last_body, [own_slot(half, d), full((half, d))] + [hold] * 5...  8.36 us
    ppermute x5, waiting for transfers between devices, trade(): return lax.ppermute(value, 'seq', [(0, 1), (1, 0)])  7.54 us
    pallas_call x1, Pallas kernels, slope_first(): call(slope_first_body, (ff // w,), [cols(t, w), cols(d, w), full((t, d)),...  7.16 us
  transfers between devices with their start and end apart: 25, of which 10 were waited for; matrix products, arithmetic and copies ran while one was open for 3% of the time, Pallas kernels for 44%

profile of v3, /device:TPU:0, one launch (start us, length us, event | category | flops | bytes accessed | tf_op | source)
XLA Modules:
  0.0 153.4 jit_solution(8514946980303379390)
XLA Ops:
  1.7 3.1 %collective-permute-start = (bf16[256,768]{1,0:T(8,128)(2,1)S(1)}, bf16[256,768]{1,0:T(8,128)(2,1)S(1)}, u32[]{:S(2)}, u32[]{:S(2)}) collective-permute-start(bf16[256,768]{1,0:T(8,128)(2,1)S(1)} %dynamic-slice_bitcast_fusion.1), channel_id=1, source_target_pairs={{0,1},{1,0},{2,3},{3,2},{4,5},{5,4},{6,7},{7,6},{8,9},{9,8},{10,11... | collective-permute-start | bytes 1179656 | tf_op jit(solution)/shard_map/ppermute | solution.py:658
  7.2 7.5 %collective-permute-done.rem = bf16[256,768]{1,0:T(8,128)(2,1)S(1)} collective-permute-done((bf16[256,768]{1,0:T(8,128)(2,1)S(1)}, bf16[256,768]{1,0:T(8,128)(2,1)S(1)}, u32[]{:S(2)}, u32[]{:S(2)}) %collective-permute-start) | collective-permute-done | bytes 393248 | tf_op jit(solution)/shard_map/ppermute | solution.py:658
  14.7 13.5 %attn_fwd.1 = (bf16[512,768]{1,0:T(8,128)(2,1)S(1)}, bf16[768,512]{1,0:T(8,128)(2,1)S(1)}, bf16[512,768]{1,0:T(8,128)(2,1)S(1)}, bf16[12,512,512]{2,1,0:T(8,128)...) custom-call(s32[6]{0:T(128)S(1)} %stack.24.s, ...), custom_call_target="tpu_custom_call" | custom-call | flops 3200000 | bytes 18874 | tf_op jit(solution)/shard_map/attn_fwd/pallas_call | solution.py:144
  28.2 13.6 %mlp_fwd.1 = (bf16[512,3072]{1,0:T(8,128)(2,1)S(1)}, bf16[512,3072]{1,0:T(8,128)(2,1)S(1)}, f32[2,256,768]{2,1,0:T(8,128)}, bf16[128,768]{1,0:T(8,128)(2,1)S(1)}...) custom-call(s32[6]{0:T(128)S(1)} %stack.24.s, ...), custom_call_target="tpu_custom_call" | custom-call | flops 4800000 | bytes 25165 | tf_op jit(solution)/shard_map/mlp_fwd/pallas_call | solution.py:246
  41.9 2.0 %collective-permute-start.2 = (bf16[128,768]{1,0:T(8,128)(2,1)S(1)}, bf16[128,768]{1,0:T(8,128)(2,1)S(1)}, u32[]{:S(2)}, u32[]{:S(2)}) collective-permute-start(bf16[128,768]{1,0:T(8,128)(2,1)S(1)} %get-tuple-element.139), channel_id=1, source_target_pairs={{0,1},{1,0},{2,3},{3,2},{4,5},{5,4},{6,7},{7,6},{8,9},{9,8},{10,11... | collective-permute-start | bytes 589832 | tf_op jit(solution)/shard_map/ppermute | solution.py:658
  43.9 5.1 %weight_outer.1 = (bf16[2,2,2,2,192,384]{5,4,3,2,1,0:T(8,128)(2,1)S(1)}, bf16[2,2,2,2,192,384]{5,4,3,2,1,0:T(8,128)(2,1)S(1)}) custom-call(s32[6]{0:T(128)S(1)} %stack.24.s, bf16[512,3072]{1,0:T(8,128)(2,1)S(1)} %get-tuple-element.135.act, bf16[512,768]{1,0:T(8,128)(2,1)S(1)} %get-tuple-element.136.sl), custom_call_target="tpu_custom_call" | custom-call | flops 2400000 | bytes 10485 | tf_op jit(solution)/shard_map/weight_outer/pallas_call | solution.py:720
  49.6 6.9 %slope_inner.1 = (bf16[512,3072]{1,0:T(8,128)(2,1)S(1)}, f32[1,3072]{1,0:T(1,128)S(1)}) custom-call(s32[6]{0:T(128)S(1)} %stack.24.s, bf16[512,768]{1,0:T(8,128)(2,1)S(1)} %get-tuple-element.136.sl, bf16[3072,768]{1,0:T(8,128)(2,1)} %wo.3, bf16[512,3072]{1,0:T(8,128)(2,1)S(1)} %get-tuple-element.144.dg), custom_call_target="tpu_custom_call" | custom-call | flops 2400000 | bytes 12582 | tf_op jit(solution)/shard_map/slope_inner/pallas_call | solution.py:282
  56.8 1.7 %collective-permute-start.5 = (bf16[2,2,2,192,384]{4,3,2,1,0:T(8,128)(2,1)S(1)}, bf16[2,2,2,192,384]{4,3,2,1,0:T(8,128)(2,1)S(1)}, u32[]{:S(2)}, u32[]{:S(2)}) collective-permute-start(bf16[2,2,2,192,384]{4,3,2,1,0:T(8,128)(2,1)S(1)} %fusion.1), channel_id=1, source_target_pairs={{0,4},{1,5},{2,3},{3,2},{4,0},{5,1},{6,7},{7,6},{8,12},{9,13},{10,... | collective-permute-start | bytes 3538952 | tf_op jit(solution)/shard_map/ppermute | solution.py:669
  58.5 6.9 %weight_inner.1 = (bf16[2,2,2,2,192,384]{5,4,3,2,1,0:T(8,128)(2,1)S(1)}, bf16[2,2,2,192,384]{4,3,2,1,0:T(8,128)(2,1)S(1)}, bf16[2,2,2,192,384]{4,3,2,1,0:T(8,128)(2,1)S(1)}) custom-call(s32[6]{0:T(128)S(1)} %stack.24.s, bf16[512,768]{1,0:T(8,128)(2,1)S(1)} %get-tuple-element.133.nl, bf16[512,3072]{1,0:T(8,128)(2,1)S(1)} %get-tuple-element.148.si0.si1.si, ...), custom_call_target="tpu_custom_call" | custom-call | flops 2400000 | bytes 10485 | tf_op jit(solution)/shard_map/weight_inner/pallas_call | solution.py:730
  66.0 7.2 %slope_first.1 = (f32[512,768]{1,0:T(8,128)S(1)}, bf16[512,768]{1,0:T(8,128)(2,1)S(1)}, f32[3,768]{1,0:T(4,128)S(1)}) custom-call(s32[6]{0:T(128)S(1)} %stack.24.s, bf16[512,3072]{1,0:T(8,128)(2,1)S(1)} %get-tuple-element.148.si0.si1.si, bf16[768,3072]{1,0:T(8,128)(2,1)} %wi.3, f32[512,768]{1,0:T(8,128)S(1)} %get-tuple-element.152.ss, ...), custom_call_target="tpu_custom_call" | custom-call | flops 2400000 | bytes 14680 | tf_op jit(solution)/shard_map/slope_first/pallas_call | solution.py:331
  73.5 1.6 %collective-permute-start.9 = (bf16[2,2,2,192,384]{4,3,2,1,0:T(8,128)(2,1)S(1)}, bf16[2,2,2,192,384]{4,3,2,1,0:T(8,128)(2,1)S(1)}, u32[]{:S(2)}, u32[]{:S(2)}) collective-permute-start(bf16[2,2,2,192,384]{4,3,2,1,0:T(8,128)(2,1)S(1)} %fusion), channel_id=1, source_target_pairs={{0,4},{1,5},{2,3},{3,2},{4,0},{5,1},{6,7},{7,6},{8,12},{9,13},{10,... | collective-permute-start | bytes 3538952 | tf_op jit(solution)/shard_map/ppermute | solution.py:669
  75.3 1.6 %collective-permute-start.8 = (bf16[2,2,192,384]{3,2,1,0:T(8,128)(2,1)S(1)}, bf16[2,2,192,384]{3,2,1,0:T(8,128)(2,1)S(1)}, u32[]{:S(2)}, u32[]{:S(2)}) collective-permute-start(bf16[2,2,192,384]{3,2,1,0:T(8,128)(2,1)S(1)} %fusion.3), channel_id=1, source_target_pairs={{0,8},{1,9},{2,10},{3,11},{4,12},{5,13},{6,14},{7,15},{8,0},{9,1},... | collective-permute-start | bytes 1769480 | tf_op jit(solution)/shard_map/ppermute | solution.py:669
  77.0 9.9 %attn_bwd.1 = (bf16[512,768]{1,0:T(8,128)(2,1)S(1)}, bf16[512,768]{1,0:T(8,128)(2,1)S(1)}, bf16[512,768]{1,0:T(8,128)(2,1)S(1)}) custom-call(s32[6]{0:T(128)S(1)} %stack.24.s, bf16[512,768]{1,0:T(8,128)(2,1)S(1)} %get-tuple-element.159.ml, bf16[768,768]{1,0:T(8,128)(2,1)} %wm.3, bf16[512,768]{1,0:T(8,128)(2,1)S(1)} %get-tuple-element.160.q, ...), custom_call_target="tpu_custom_call" | custom-call | flops 3600000 | bytes 15728 | tf_op jit(solution)/shard_map/attn_bwd/pallas_call | solution.py:375
  86.9 3.5 %collective-permute-done.8 = bf16[2,2,192,384]{3,2,1,0:T(8,128)(2,1)S(1)} collective-permute-done((bf16[2,2,192,384]{3,2,1,0:T(8,128)(2,1)S(1)}, bf16[2,2,192,384]{3,2,1,0:T(8,128)(2,1)S(1)}, u32[]{:S(2)}, u32[]{:S(2)}) %collective-permute-start.8) | collective-permute-done | bytes 589856 | tf_op jit(solution)/shard_map/ppermute | solution.py:669
  91.8 1.2 collective-permute-start.11
  93.0 8.4 %weight_last.1 = (bf16[2,2,2,2,192,384]{5,4,3,2,1,0:T(8,128)(2,1)S(1)}, bf16[2,2,192,384]{3,2,1,0:T(8,128)(2,1)S(1)}, bf16[2,2,192,384]{3,2,1,0:T(8,128)(2,1)S(1...) custom-call(s32[6]{0:T(128)S(1)} %stack.24.s, ...), custom_call_target="tpu_custom_call" | custom-call | flops 2400000 | bytes 10485 | tf_op jit(solution)/shard_map/weight_last/pallas_call | solution.py:751
  102.0 2.3 %collective-permute-done.14.refs_13_ = f32[32,384]{1,0:T(8,128)S(1)} collective-permute-done((f32[32,384]{1,0:T(8,128)S(1)}, f32[32,384]{1,0:T(8,128)S(1)}, u32[]{:S(2)}, u32[]{:S(2)}) %collective-permute-start.14) | collective-permute-done | bytes 49184 | tf_op jit(solution)/shard_map/ppermute | solution.py:659
  104.3 1.1 combine.5
  106.9 1.6 %collective-permute-start.18 = (bf16[384,384]{1,0:T(8,128)(2,1)S(1)}, bf16[384,384]{1,0:T(8,128)(2,1)S(1)}, u32[]{:S(2)}, u32[]{:S(2)}) collective-permute-start(bf16[384,384]{1,0:T(8,128)(2,1)S(1)} %get-tuple-element.197), channel_id=1, source_target_pairs={{0,8},{1,9},{2,10},{3,11},{4,12},{5,13},{6,14},{7,15},{8,0},{9,1},... | collective-permute-start | bytes 884744 | tf_op jit(solution)/shard_map/ppermute | solution.py:669
  108.4 2.6 %collective-permute-start.19 = (bf16[192,384]{1,0:T(8,128)(2,1)S(1)}, bf16[192,384]{1,0:T(8,128)(2,1)S(1)}, u32[]{:S(2)}, u32[]{:S(2)}) collective-permute-start(bf16[192,384]{1,0:T(8,128)(2,1)S(1)} %get-tuple-element.198), channel_id=1, source_target_pairs={{0,16},{1,17},{2,18},{3,19},{4,20},{5,21},{6,22},{7,23},{8,24},{9,... | collective-permute-start | bytes 442376 | tf_op jit(solution)/shard_map/ppermute | solution.py:669
  111.0 5.4 %input_grad.1 = (f32[2,256,768]{2,1,0:T(8,128)}, bf16[256,768]{1,0:T(8,128)(2,1)S(1)}) custom-call(s32[6]{0:T(128)S(1)} %stack.24.s, bf16[512,768]{1,0:T(8,128)(2,1)S(1)} %get-tuple-element.173.dq, bf16[512,768]{1,0:T(8,128)(2,1)S(1)} %get-tuple-element.174.dk, bf16[512,768]{1,0:T(8,128)(2,1)S(1)} %get-tuple-element.175.dv, bf16[768,768]{1,0:T(8,128)(2,1)} %wq.3, ...), custom_call_target="tpu_custom_call" | custom-call | flops 1800000 | bytes 8388 | tf_op jit(solution)/shard_map/input_grad/pallas_call | solution.py:407
  116.4 1.6 %collective-permute-done.19 = bf16[192,384]{1,0:T(8,128)(2,1)S(1)} collective-permute-done((bf16[192,384]{1,0:T(8,128)(2,1)S(1)}, bf16[192,384]{1,0:T(8,128)(2,1)S(1)}, u32[]{:S(2)}, u32[]{:S(2)}) %collective-permute-start.19) | collective-permute-done | bytes 147488 | tf_op jit(solution)/shard_map/ppermute | solution.py:669
  118.9 3.0 %collective-permute-done.15.refs_1_.refs_9_.refs_2_ = bf16[1568,384]{1,0:T(8,128)(2,1)S(1)} collective-permute-done((bf16[1568,384]{1,0:T(8,128)(2,1)S(1)}, bf16[1568,384]{1,0:T(8,128)(2,1)S(1)}, u32[]{:S(2)}, u32[]{:S(2)}) %collective-permute-start.15) | collective-permute-done | bytes 1204256 | tf_op jit(solution)/shard_map/ppermute | solution.py:669
  123.8 2.6 %collective-permute-start.21 = (bf16[192,384]{1,0:T(8,128)(2,1)S(1)}, bf16[192,384]{1,0:T(8,128)(2,1)S(1)}, u32[]{:S(2)}, u32[]{:S(2)}) collective-permute-start(bf16[192,384]{1,0:T(8,128)(2,1)S(1)} %get-tuple-element.207), channel_id=1, source_target_pairs={{0,16},{1,17},{2,18},{3,19},{4,20},{5,21},{6,22},{7,23},{8,24},{9,... | collective-permute-start | bytes 442376 | tf_op jit(solution)/shard_map/ppermute | solution.py:669
  126.4 1.5 finish.2
  128.7 3.9 %collective-permute-done.21 = bf16[192,384]{1,0:T(8,128)(2,1)S(1)} collective-permute-done((bf16[192,384]{1,0:T(8,128)(2,1)S(1)}, bf16[192,384]{1,0:T(8,128)(2,1)S(1)}, u32[]{:S(2)}, u32[]{:S(2)}) %collective-permute-start.21) | collective-permute-done | bytes 147488 | tf_op jit(solution)/shard_map/ppermute | solution.py:669
  133.7 1.6 %collective-permute-start.22 = (bf16[416,384]{1,0:T(8,128)(2,1)S(1)}, bf16[416,384]{1,0:T(8,128)(2,1)S(1)}, u32[]{:S(2)}, u32[]{:S(2)}) collective-permute-start(bf16[416,384]{1,0:T(8,128)(2,1)S(1)} %get-tuple-element.217), channel_id=1, source_target_pairs={{0,8},{1,9},{2,10},{3,11},{4,12},{5,13},{6,14},{7,15},{8,0},{9,1},... | collective-permute-start | bytes 958472 | tf_op jit(solution)/shard_map/ppermute | solution.py:669
  136.3 5.5 %collective-permute-done.22.refs_4_.refs_6_ = bf16[416,384]{1,0:T(8,128)(2,1)S(1)} collective-permute-done((bf16[416,384]{1,0:T(8,128)(2,1)S(1)}, bf16[416,384]{1,0:T(8,128)(2,1)S(1)}, u32[]{:S(2)}, u32[]{:S(2)}) %collective-permute-start.22) | collective-permute-done | bytes 319520 | tf_op jit(solution)/shard_map/ppermute | solution.py:669
  142.4 3.1 %collective-permute-start.23 = (bf16[224,384]{1,0:T(8,128)(2,1)S(1)}, bf16[224,384]{1,0:T(8,128)(2,1)S(1)}, u32[]{:S(2)}, u32[]{:S(2)}) collective-permute-start(bf16[224,384]{1,0:T(8,128)(2,1)S(1)} %get-tuple-element.219), channel_id=1, source_target_pairs={{0,16},{1,17},{2,18},{3,19},{4,20},{5,21},{6,22},{7,23},{8,24},{9,... | collective-permute-start | bytes 516104 | tf_op jit(solution)/shard_map/ppermute | solution.py:669
  146.4 1.5 finish.3
  147.9 4.0 %collective-permute-done.23.refs_5_.refs_7_ = bf16[224,384]{1,0:T(8,128)(2,1)S(1)} collective-permute-done((bf16[224,384]{1,0:T(8,128)(2,1)S(1)}, bf16[224,384]{1,0:T(8,128)(2,1)S(1)}, u32[]{:S(2)}, u32[]{:S(2)}) %collective-permute-start.23) | collective-permute-done | bytes 172064 | tf_op jit(solution)/shard_map/ppermute | solution.py:669
  151.8 1.3 combine.9
  (49 shorter events, 16.0 us)
Async XLA Ops:
  0.7 5.2 %copy-start = (s32[2]{0:T(128)S(1)}, s32[2]{0:T(128)}, u32[]{:S(2)}) copy-start(s32[2]{0:T(128)} %param.20) | copy-start | bytes 28
  1.7 13.0 %collective-permute-start = (bf16[256,768]{1,0:T(8,128)(2,1)S(1)}, bf16[256,768]{1,0:T(8,128)(2,1)S(1)}, u32[]{:S(2)}, u32[]{:S(2)}) collective-permute-start(bf16[256,768]{1,0:T(8,128)(2,1)S(1)} %dynamic-slice_bitcast_fusion.1), channel_id=1, source_target_pairs={{0,1},{1,0},{2,3},{3,2},{4,5},{5,4},{6,7},{7,6},{8,9},{9,8},{10,11... | collective-permute-start | bytes 1179656 | tf_op jit(solution)/shard_map/ppermute | solution.py:658
  5.8 22.4 %collective-permute-start.1 = (bf16[256,768]{1,0:T(8,128)(2,1)S(1)}, bf16[256,768]{1,0:T(8,128)(2,1)S(1)}, u32[]{:S(2)}, u32[]{:S(2)}) collective-permute-start(bf16[256,768]{1,0:T(8,128)(2,1)S(1)} %dynamic-slice_bitcast_fusion), channel_id=1, source_target_pairs={{0,1},{1,0},{2,3},{3,2},{4,5},{5,4},{6,7},{7,6},{8,9},{9,8},{10,11... | collective-permute-start | bytes 1179656 | tf_op jit(solution)/shard_map/ppermute | solution.py:658
  41.9 7.2 %collective-permute-start.2 = (bf16[128,768]{1,0:T(8,128)(2,1)S(1)}, bf16[128,768]{1,0:T(8,128)(2,1)S(1)}, u32[]{:S(2)}, u32[]{:S(2)}) collective-permute-start(bf16[128,768]{1,0:T(8,128)(2,1)S(1)} %get-tuple-element.139), channel_id=1, source_target_pairs={{0,1},{1,0},{2,3},{3,2},{4,5},{5,4},{6,7},{7,6},{8,9},{9,8},{10,11... | collective-permute-start | bytes 589832 | tf_op jit(solution)/shard_map/ppermute | solution.py:658
  49.0 7.4 %collective-permute-start.3 = (bf16[2,2,2,2,192,384]{5,4,3,2,1,0:T(8,128)(2,1)S(1)}, bf16[2,2,2,2,192,384]{5,4,3,2,1,0:T(8,128)(2,1)S(1)}, u32[]{:S(2)}, u32[]{:S(2)}) collective-permute-start(bf16[2,2,2,2,192,384]{5,4,3,2,1,0:T(8,128)(2,1)S(1)} %get-tuple-element.141), channel_id=1, source_target_pairs={{0,2},{2,0},{4,6},{6,4},{8,10},{10,8},{12,14},{14,12},{16,18},{18,... | collective-permute-start | bytes 7077896 | tf_op jit(solution)/shard_map/ppermute | solution.py:659
  49.1 7.3 %collective-permute-start.4 = (bf16[128,768]{1,0:T(8,128)(2,1)S(1)}, bf16[128,768]{1,0:T(8,128)(2,1)S(1)}, u32[]{:S(2)}, u32[]{:S(2)}) collective-permute-start(bf16[128,768]{1,0:T(8,128)(2,1)S(1)} %get-tuple-element.142), channel_id=1, source_target_pairs={{0,1},{1,0},{2,3},{3,2},{4,5},{5,4},{6,7},{7,6},{8,9},{9,8},{10,11... | collective-permute-start | bytes 589832 | tf_op jit(solution)/shard_map/ppermute | solution.py:658
  56.8 16.3 %collective-permute-start.5 = (bf16[2,2,2,192,384]{4,3,2,1,0:T(8,128)(2,1)S(1)}, bf16[2,2,2,192,384]{4,3,2,1,0:T(8,128)(2,1)S(1)}, u32[]{:S(2)}, u32[]{:S(2)}) collective-permute-start(bf16[2,2,2,192,384]{4,3,2,1,0:T(8,128)(2,1)S(1)} %fusion.1), channel_id=1, source_target_pairs={{0,4},{1,5},{2,3},{3,2},{4,0},{5,1},{6,7},{7,6},{8,12},{9,13},{10,... | collective-permute-start | bytes 3538952 | tf_op jit(solution)/shard_map/ppermute | solution.py:669
  65.4 7.8 %collective-permute-start.6 = (bf16[2,2,2,192,384]{4,3,2,1,0:T(8,128)(2,1)S(1)}, bf16[2,2,2,192,384]{4,3,2,1,0:T(8,128)(2,1)S(1)}, u32[]{:S(2)}, u32[]{:S(2)}) collective-permute-start(bf16[2,2,2,192,384]{4,3,2,1,0:T(8,128)(2,1)S(1)} %get-tuple-element.149), channel_id=1, source_target_pairs={{0,2},{2,0},{4,6},{6,4},{8,10},{10,8},{12,14},{14,12},{16,18},{18,... | collective-permute-start | bytes 3538952 | tf_op jit(solution)/shard_map/ppermute | solution.py:659
  65.5 7.7 %collective-permute-start.7 = (bf16[2,2,2,192,384]{4,3,2,1,0:T(8,128)(2,1)S(1)}, bf16[2,2,2,192,384]{4,3,2,1,0:T(8,128)(2,1)S(1)}, u32[]{:S(2)}, u32[]{:S(2)}) collective-permute-start(bf16[2,2,2,192,384]{4,3,2,1,0:T(8,128)(2,1)S(1)} %get-tuple-element.150), channel_id=1, source_target_pairs={{0,2},{2,0},{4,6},{6,4},{8,10},{10,8},{12,14},{14,12},{16,18},{18,... | collective-permute-start | bytes 3538952 | tf_op jit(solution)/shard_map/ppermute | solution.py:659
  73.5 16.9 %collective-permute-start.9 = (bf16[2,2,2,192,384]{4,3,2,1,0:T(8,128)(2,1)S(1)}, bf16[2,2,2,192,384]{4,3,2,1,0:T(8,128)(2,1)S(1)}, u32[]{:S(2)}, u32[]{:S(2)}) collective-permute-start(bf16[2,2,2,192,384]{4,3,2,1,0:T(8,128)(2,1)S(1)} %fusion), channel_id=1, source_target_pairs={{0,4},{1,5},{2,3},{3,2},{4,0},{5,1},{6,7},{7,6},{8,12},{9,13},{10,... | collective-permute-start | bytes 3538952 | tf_op jit(solution)/shard_map/ppermute | solution.py:669
  75.3 15.1 %collective-permute-start.8 = (bf16[2,2,192,384]{3,2,1,0:T(8,128)(2,1)S(1)}, bf16[2,2,192,384]{3,2,1,0:T(8,128)(2,1)S(1)}, u32[]{:S(2)}, u32[]{:S(2)}) collective-permute-start(bf16[2,2,192,384]{3,2,1,0:T(8,128)(2,1)S(1)} %fusion.3), channel_id=1, source_target_pairs={{0,8},{1,9},{2,10},{3,11},{4,12},{5,13},{6,14},{7,15},{8,0},{9,1},... | collective-permute-start | bytes 1769480 | tf_op jit(solution)/shard_map/ppermute | solution.py:669
  90.6 10.8 %collective-permute-start.10 = (bf16[2,192,384]{2,1,0:T(8,128)(2,1)S(1)}, bf16[2,192,384]{2,1,0:T(8,128)(2,1)S(1)}, u32[]{:S(2)}, u32[]{:S(2)}) collective-permute-start(bf16[2,192,384]{2,1,0:T(8,128)(2,1)S(1)} %fusion.4), channel_id=1, source_target_pairs={{0,1},{1,0},{2,6},{3,7},{4,5},{5,4},{6,2},{7,3},{8,9},{9,8},{10,14... | collective-permute-start | bytes 884744 | tf_op jit(solution)/shard_map/ppermute | solution.py:669
  91.8 12.6 %collective-permute-start.11 = (bf16[2,2,192,384]{3,2,1,0:T(8,128)(2,1)S(1)}, bf16[2,2,192,384]{3,2,1,0:T(8,128)(2,1)S(1)}, u32[]{:S(2)}, u32[]{:S(2)}) collective-permute-start(bf16[2,2,192,384]{3,2,1,0:T(8,128)(2,1)S(1)} %fusion.2), channel_id=1, source_target_pairs={{0,1},{1,0},{2,6},{3,7},{4,5},{5,4},{6,2},{7,3},{8,9},{9,8},{10,14... | collective-permute-start | bytes 1769480 | tf_op jit(solution)/shard_map/ppermute | solution.py:669
  101.3 3.0 %collective-permute-start.12 = (bf16[2,2,192,384]{3,2,1,0:T(8,128)(2,1)S(1)}, bf16[2,2,192,384]{3,2,1,0:T(8,128)(2,1)S(1)}, u32[]{:S(2)}, u32[]{:S(2)}) collective-permute-start(bf16[2,2,192,384]{3,2,1,0:T(8,128)(2,1)S(1)} %get-tuple-element.184), channel_id=1, source_target_pairs={{0,2},{2,0},{4,6},{6,4},{8,10},{10,8},{12,14},{14,12},{16,18},{18,... | collective-permute-start | bytes 1769480 | tf_op jit(solution)/shard_map/ppermute | solution.py:659
  101.4 2.9 %collective-permute-start.13 = (bf16[2,2,192,384]{3,2,1,0:T(8,128)(2,1)S(1)}, bf16[2,2,192,384]{3,2,1,0:T(8,128)(2,1)S(1)}, u32[]{:S(2)}, u32[]{:S(2)}) collective-permute-start(bf16[2,2,192,384]{3,2,1,0:T(8,128)(2,1)S(1)} %get-tuple-element.185), channel_id=1, source_target_pairs={{0,2},{2,0},{4,6},{6,4},{8,10},{10,8},{12,14},{14,12},{16,18},{18,... | collective-permute-start | bytes 1769480 | tf_op jit(solution)/shard_map/ppermute | solution.py:659
  101.9 2.4 %collective-permute-start.14 = (f32[32,384]{1,0:T(8,128)S(1)}, f32[32,384]{1,0:T(8,128)S(1)}, u32[]{:S(2)}, u32[]{:S(2)}) collective-permute-start(f32[32,384]{1,0:T(8,128)S(1)} %get-tuple-element.186.refs_12_), channel_id=1, source_target_pairs={{0,2},{2,0},{4,6},{6,4},{8,10},{10,8},{12,14},{14,12},{16,18},{18,... | collective-permute-start | bytes 147464 | tf_op jit(solution)/shard_map/ppermute | solution.py:659
  105.4 16.5 %collective-permute-start.15 = (bf16[1568,384]{1,0:T(8,128)(2,1)S(1)}, bf16[1568,384]{1,0:T(8,128)(2,1)S(1)}, u32[]{:S(2)}, u32[]{:S(2)}) collective-permute-start(bf16[1568,384]{1,0:T(8,128)(2,1)S(1)} %get-tuple-element.192), channel_id=1, source_target_pairs={{0,4},{1,5},{2,3},{3,2},{4,0},{5,1},{6,7},{7,6},{8,12},{9,13},{10,... | collective-permute-start | bytes 3612680 | tf_op jit(solution)/shard_map/ppermute | solution.py:669
  106.4 12.6 %collective-permute-start.16 = (bf16[2,2,192,384]{3,2,1,0:T(8,128)(2,1)S(1)}, bf16[2,2,192,384]{3,2,1,0:T(8,128)(2,1)S(1)}, u32[]{:S(2)}, u32[]{:S(2)}) collective-permute-start(bf16[2,2,192,384]{3,2,1,0:T(8,128)(2,1)S(1)} %get-tuple-element.194), channel_id=1, source_target_pairs={{0,2},{2,0},{4,6},{6,4},{8,10},{10,8},{12,14},{14,12},{16,18},{18,... | collective-permute-start | bytes 1769480 | tf_op jit(solution)/shard_map/ppermute | solution.py:659
  106.4 12.6 %collective-permute-start.17 = (bf16[2,2,192,384]{3,2,1,0:T(8,128)(2,1)S(1)}, bf16[2,2,192,384]{3,2,1,0:T(8,128)(2,1)S(1)}, u32[]{:S(2)}, u32[]{:S(2)}) collective-permute-start(bf16[2,2,192,384]{3,2,1,0:T(8,128)(2,1)S(1)} %get-tuple-element.196), channel_id=1, source_target_pairs={{0,2},{2,0},{4,6},{6,4},{8,10},{10,8},{12,14},{14,12},{16,18},{18,... | collective-permute-start | bytes 1769480 | tf_op jit(solution)/shard_map/ppermute | solution.py:659
  106.9 12.1 %collective-permute-start.18 = (bf16[384,384]{1,0:T(8,128)(2,1)S(1)}, bf16[384,384]{1,0:T(8,128)(2,1)S(1)}, u32[]{:S(2)}, u32[]{:S(2)}) collective-permute-start(bf16[384,384]{1,0:T(8,128)(2,1)S(1)} %get-tuple-element.197), channel_id=1, source_target_pairs={{0,8},{1,9},{2,10},{3,11},{4,12},{5,13},{6,14},{7,15},{8,0},{9,1},... | collective-permute-start | bytes 884744 | tf_op jit(solution)/shard_map/ppermute | solution.py:669
  108.4 9.6 %collective-permute-start.19 = (bf16[192,384]{1,0:T(8,128)(2,1)S(1)}, bf16[192,384]{1,0:T(8,128)(2,1)S(1)}, u32[]{:S(2)}, u32[]{:S(2)}) collective-permute-start(bf16[192,384]{1,0:T(8,128)(2,1)S(1)} %get-tuple-element.198), channel_id=1, source_target_pairs={{0,16},{1,17},{2,18},{3,19},{4,20},{5,21},{6,22},{7,23},{8,24},{9,... | collective-permute-start | bytes 442376 | tf_op jit(solution)/shard_map/ppermute | solution.py:669
  122.8 10.2 %collective-permute-start.20 = (bf16[800,384]{1,0:T(8,128)(2,1)S(1)}, bf16[800,384]{1,0:T(8,128)(2,1)S(1)}, u32[]{:S(2)}, u32[]{:S(2)}) collective-permute-start(bf16[800,384]{1,0:T(8,128)(2,1)S(1)} %get-tuple-element.206), channel_id=1, source_target_pairs={{0,1},{1,0},{2,6},{3,7},{4,5},{5,4},{6,2},{7,3},{8,9},{9,8},{10,14... | collective-permute-start | bytes 1843208 | tf_op jit(solution)/shard_map/ppermute | solution.py:669
  123.8 8.8 %collective-permute-start.21 = (bf16[192,384]{1,0:T(8,128)(2,1)S(1)}, bf16[192,384]{1,0:T(8,128)(2,1)S(1)}, u32[]{:S(2)}, u32[]{:S(2)}) collective-permute-start(bf16[192,384]{1,0:T(8,128)(2,1)S(1)} %get-tuple-element.207), channel_id=1, source_target_pairs={{0,16},{1,17},{2,18},{3,19},{4,20},{5,21},{6,22},{7,23},{8,24},{9,... | collective-permute-start | bytes 442376 | tf_op jit(solution)/shard_map/ppermute | solution.py:669
  133.7 8.0 %collective-permute-start.22 = (bf16[416,384]{1,0:T(8,128)(2,1)S(1)}, bf16[416,384]{1,0:T(8,128)(2,1)S(1)}, u32[]{:S(2)}, u32[]{:S(2)}) collective-permute-start(bf16[416,384]{1,0:T(8,128)(2,1)S(1)} %get-tuple-element.217), channel_id=1, source_target_pairs={{0,8},{1,9},{2,10},{3,11},{4,12},{5,13},{6,14},{7,15},{8,0},{9,1},... | collective-permute-start | bytes 958472 | tf_op jit(solution)/shard_map/ppermute | solution.py:669
  135.4 11.0 %collective-permute-start.24 = (bf16[256,768]{1,0:T(8,128)(2,1)S(1)}, bf16[256,768]{1,0:T(8,128)(2,1)S(1)}, u32[]{:S(2)}, u32[]{:S(2)}) collective-permute-start(bf16[256,768]{1,0:T(8,128)(2,1)S(1)} %get-tuple-element.222), channel_id=1, source_target_pairs={{0,1},{1,0},{2,3},{3,2},{4,5},{5,4},{6,7},{7,6},{8,9},{9,8},{10,11... | collective-permute-start | bytes 1179656 | tf_op jit(solution)/shard_map/ppermute | solution.py:658
  142.4 9.4 %collective-permute-start.23 = (bf16[224,384]{1,0:T(8,128)(2,1)S(1)}, bf16[224,384]{1,0:T(8,128)(2,1)S(1)}, u32[]{:S(2)}, u32[]{:S(2)}) collective-permute-start(bf16[224,384]{1,0:T(8,128)(2,1)S(1)} %get-tuple-element.219), channel_id=1, source_target_pairs={{0,16},{1,17},{2,18},{3,19},{4,20},{5,21},{6,22},{7,23},{8,24},{9,... | collective-permute-start | bytes 516104 | tf_op jit(solution)/shard_map/ppermute | solution.py:669

commit v4 on v3

--- a/solution.py
+++ b/solution.py
@@ -425,42 +425,38 @@
     return jnp.where(core == 0, a, f) ^ s[3], jnp.where(core == 0, f, a) ^ s[0]
 
 
-def outer_jobs(s, core, j):
+def cols_of(y):
+    return pl.ds(pl.multiple_of(y * 384, 128), 384)
+
+
+def outer_jobs(s, core, j, tile):
     for a in range(2):
         for f in range(2):
             x, y = meets(s, core, a, f)
-            yield a, ((j & 1) ^ s[4], f, (j >> 1) ^ s[5]), (2 * x + core) * 192, 192, y * 384, 0
-
-
-def thin_jobs(s, core, j):
-    at = pl.multiple_of(j * 48, 16)
+            where = (a, (j & 1) ^ s[4], f, (j >> 1) ^ s[5])
+            yield where, tile.at[2 * x + core, :, cols_of(y)], slice(None)
+
+
+def thin_jobs(s, core, j, tile):
     for a in range(2):
         for f in range(2):
             x, y = meets(s, core, a, f)
-            for e in range(2):
-                for g in range(2):
-                    row = (8 * (g ^ s[5]) + 4 * (e ^ s[4]) + 2 * x + core) * 48
-                    yield a, (f, e, g), row, 48, y * 384, at
-
-
-def flush(s, tile, outs, sems, jobs_of):
+            rows = pl.ds(pl.multiple_of((2 * x + core) * 48, 16), 48)
+            yield (a, f), tile.at[:, rows, cols_of(y)], pl.ds(pl.multiple_of(j * 48, 16), 48)
+
+
+def flush(s, step, tile, outs, sems, jobs_of):
     copies = []
     keep, *send = outs
+    split = len(send).bit_length() - 1
     for away in range(2):
-        for a, rest, row, height, col, at in jobs_of(s[2] ^ away):
-            where = (a, *rest)
+        for where, part, rows in jobs_of(s, s[2] ^ away, step, tile):
             out = keep.at[*where]
             if away:
-                split = {1: 0, 2: 1, 4: 2}[len(send)]
                 index = sum(i << (split - 1 - n) for n, i in enumerate(where[:split]))
-                out = send[index].at[*where[split:]]
-            copies.append(
-                pltpu.make_async_copy(
-                    tile.at[pl.ds(pl.multiple_of(row, 16), height), pl.ds(pl.multiple_of(col, 128), 384)],
-                    out.at[pl.ds(at, height)],
-                    sems.at[len(copies)],
-                )
-            )
+                out = send[index].at[*where[split:]] if where[split:] else send[index]
+            out = out.at[rows] if len(where) == 4 else out.at[:, rows]
+            copies.append(pltpu.make_async_copy(part, out, sems.at[len(copies)]))
     return copies
 
 
@@ -468,7 +464,7 @@
     j = pl.program_id(0)
 
     def go(step, slot, wait):
-        for copy in flush(s, tiles.at[slot], outs, sems.at[slot], lambda core: jobs_of(core, step)):
+        for copy in flush(s, step, tiles.at[slot], outs, sems.at[slot], jobs_of):
             copy.wait() if wait else copy.start()
 
     slot = lax.rem(j, 2)
@@ -489,16 +485,16 @@
 
 def outer_body(s, act, sl, keep, send, tiles, sems):
     def fill(_, tile):
-        tile[...] = tn(act[...], sl[...]).astype(BF)
-
-    run_tiles(s, 4, tiles, sems, (keep, send), fill, lambda core, step: outer_jobs(s, core, step))
+        tile[...] = tn(act[...], sl[...]).astype(BF).reshape(tile.shape)
+
+    run_tiles(s, 4, tiles, sems, (keep, send), fill, outer_jobs)
 
 
 def inner_body(s, nl, si0, si1, keep, send0, send1, tiles, sems):
     def fill(_, tile):
-        tile[...] = tn(nl[...], jnp.concatenate([si0[...], si1[...]], 1)).astype(BF)
-
-    run_tiles(s, 4, tiles, sems, (keep, send0, send1), fill, lambda core, step: thin_jobs(s, core, step))
+        tile[...] = tn(nl[...], jnp.concatenate([si0[...], si1[...]], 1)).astype(BF).reshape(tile.shape)
+
+    run_tiles(s, 4, tiles, sems, (keep, send0, send1), fill, thin_jobs)
 
 
 def last_body(s, own, rem, dq, dk, dv, ctx, ml, v2, v1, bi,
@@ -525,20 +521,19 @@
 
             @pl.when(j == one)
             def _():
-                tile[...] = tn(xs[...], part[...]).astype(BF)
+                tile[...] = tn(xs[...], part[...]).astype(BF).reshape(tile.shape)
                 if one != 1:
                     put(one // 2, nn(jnp.ones((8, 2 * half), BF), part[...])[:1])
 
         @pl.when(j == 3)
         def _():
-            tile[...] = tn(ctx[...], ml[...]).astype(BF)
+            tile[...] = tn(ctx[...], ml[...]).astype(BF).reshape(tile.shape)
 
     sends = (send0, send1, send2, send3)
-    run_tiles(s, 4, tiles, sems, (keep, *sends), fill, lambda core, step: thin_jobs(s, core, step))
-
-
-def weight_call(body, in_specs, jobs, name, flops, scratch=(), extra=(), sends=1):
-    block = (2, 2, 2, 2, 192, 384)
+    run_tiles(s, 4, tiles, sems, (keep, *sends), fill, thin_jobs)
+
+
+def weight_call(body, in_specs, block, name, flops, scratch=(), extra=(), sends=1):
     hbm = pl.BlockSpec(memory_space=pl.ANY)
     return call(
         body,
@@ -546,7 +541,7 @@
         in_specs,
         [hbm] * (1 + sends) + [full(dims) for dims in extra],
         [shape(block, BF)] + [shape(block[sends.bit_length() - 1 :], BF)] * sends + [shape(dims, F32) for dims in extra],
-        [pltpu.VMEM((2, 768, 768), BF), pltpu.SemaphoreType.DMA((2, 2 * jobs))] + list(scratch),
+        [pltpu.VMEM((2, 4, 192, 768), BF), pltpu.SemaphoreType.DMA((2, 8))] + list(scratch),
         name,
         flops,
         10 << 20,
@@ -557,25 +552,19 @@
 
 
 def combine_body(counts, last, s, *refs):
-    ins, vec, vec_in = refs[: sum(counts)], refs[sum(counts)], refs[sum(counts) + 1]
-    outs = refs[sum(counts) + 2 :]
+    n = sum(sum(chunks) for chunks in counts)
+    ins, vec, vec_in, outs = list(refs[:n]), refs[n], refs[n + 1], refs[n + 2 :]
     new = vec[...] + vec_in[...].astype(F32)
-    at = 0
-    for i, count in enumerate(counts):
-        parts = ins[at : at + count]
-        at += count
-        step = min(part.shape[0] for part in parts)
-        for n in range(parts[0].shape[0] // step):
-            rows = slice(n * step, n * step + step)
-            pieces = [part for part in parts if part.shape[0] < parts[0].shape[0]]
-            terms = [part[rows] for part in parts if part.shape[0] == parts[0].shape[0]]
-            terms += [pieces[n][...]] if pieces else []
-            total = sum(u.astype(F32) for u in terms)
+    for out, chunks in zip(outs, counts):
+        at = 0
+        for count in chunks:
+            total = sum(ins.pop(0)[...].astype(F32) for _ in range(count))
             if last:
                 for j in range(4):
                     outs[j][...] = total[j * 48 : j * 48 + 48]
             else:
-                outs[i][rows] = total.astype(BF)
+                out[at : at + total.shape[0]] = total.astype(BF)
+            at += total.shape[0]
     if last and len(outs) == 5:
         outs[4][:, :384] = new[:12]
         outs[4][:, 384:] = new[12:24]
@@ -589,24 +578,51 @@
         outs[-1][...] = new
 
 
+def block_of(height, part, at):
+    index = at if callable(at) else lambda s: at
+    return part.reshape(-1, 384), pl.BlockSpec((height, 384), lambda g, s: (index(s), 0))
+
+
+def total_body(s, *refs):
+    *ins, out = refs
+    total = sum(ref[...].astype(F32) for ref in ins)
+    for i in range(4):
+        out[:, i * 384 : i * 384 + 384] = total[i * 48 : i * 48 + 48]
+
+
+def total_inner(s, parts):
+    args, specs = zip(*(block_of(192, *part) for part in parts))
+    return call(
+        total_body,
+        (1,),
+        list(specs),
+        full((48, 1536)),
+        shape((48, 1536), F32),
+        [],
+        "total_inner",
+        0,
+        1 << 20,
+    )(s, *args)
+
+
 def combine(s, groups, vec, vec_in, last=False, apart=False):
     specs, args, outs = [], [], []
-    for height, parts in groups:
-        for part, at in parts:
-            rows = part.size // 384
-            size = min(rows, height)
-            specs.append(pl.BlockSpec((size, 384), lambda g, s, at=at: (at, 0)))
-            args.append(part.reshape(rows, 384))
-        outs.append(shape((height, 384), BF))
+    for group in groups:
+        for height, parts in group:
+            for part in parts:
+                value, spec = block_of(height, *part)
+                args.append(value)
+                specs.append(spec)
+        outs.append(shape((sum(height for height, _ in group), 384), BF))
     if last:
         outs = [shape((48, 384), F32)] * 4
         outs += [shape((3072 if i == 8 else 768,), F32) for i in VECTORS] if apart else [shape((12, 768), F32)]
     else:
-        outs[0] = shape((groups[0][0] + 32, 384), BF)
+        outs[0] = shape((outs[0].shape[0] + 32, 384), BF)
         outs.append(shape((32, 384), F32))
     rows = vec_in.shape[0]
     return call(
-        functools.partial(combine_body, [len(parts) for _, parts in groups], last),
+        functools.partial(combine_body, [[len(parts) for _, parts in group] for group in groups], last),
         (1,),
         specs + [full((32, 384)), pl.BlockSpec((32, 384), lambda g, s: (rows // 32 - 1, 0))],
         [whole_vec(*o.shape) if len(o.shape) == 1 else full(o.shape) for o in outs],
@@ -717,7 +733,7 @@
             self.got.append(self.away(self.going))
 
     got0 = trade(out0, "y")
-    r1 = Reduce(weight_call(outer_body, [piece, hold], 4, "weight_outer", 2_400_000_000)(s, act, sl), XZY)
+    r1 = Reduce(weight_call(outer_body, [piece, hold], (2, 2, 2, 2, 192, 384), "weight_outer", 2_400_000_000)(s, act, sl), XZY)
     r1.going, got0, out1 = together(r1.going, got0, out1)
     r1.send()
     got1 = trade(out1, "y")
@@ -727,7 +743,7 @@
     r1.add()
     r1.send()
     pieces = [pl.BlockSpec((t, 384), lambda g, s, y=y: (0, 4 * y + g)) for y in range(2)]
-    keep, *parts = weight_call(inner_body, [hold] + pieces, 16, "weight_inner", 2_400_000_000, sends=2)(
+    keep, *parts = weight_call(inner_body, [hold] + pieces, (2, 2, 4, 192, 384), "weight_inner", 2_400_000_000, sends=2)(
         after(s, r1.going), nl, si, si)
     core = [trade(part, 1) for part in parts]
     sm, ml, v1 = slope_first(after(s, *parts), si, inner_weight, ss, n1, rs, g1)
@@ -750,11 +766,20 @@
     r2.send()
     keep, *parts, vec = weight_call(
         last_body, [own_slot(half, d), full((half, d))] + [hold] * 5 + [full((3, d))] * 2 + [full((1, 4 * d))],
-        16, "weight_last", 2_400_000_000, [pltpu.VMEM((t, d), BF)], [(32, 384)], sends=4)(
+        (2, 2, 4, 192, 384), "weight_last", 2_400_000_000, [pltpu.VMEM((t, d), BF)], [(32, 384)], sends=4)(
             after(s, r1.going, r2.going), tokens, rem, *slopes, ctx, ml, v2, v1, bi)
 
     def at(index, *values):
         return [(value, index) for value in values]
+
+    def of_z(far1, far2):
+        return lambda s: 2 * (s[5] ^ far2) + (s[4] ^ far1)
+
+    def far_z1(*values):
+        return [(192, at(lambda s, z2=z2: 2 * z2 + (1 - s[4]), *values)) for z2 in range(2)]
+
+    def of_z2(far2):
+        return lambda s: s[5] ^ far2
 
     r1.got[-1], parts[2], parts[3], vec = together(r1.got[-1], parts[2], parts[3], vec)
     core = [None, None, trade(parts[2], 1), trade(parts[3], 1)]
@@ -762,12 +787,12 @@
 
     r1.got[-1], r2.got[-1], core[2], core[3], vec_got = together(
         r1.got[-1], r2.got[-1], core[2], core[3], vec_got)
-    rows = keep.size // 384 // 2
     r3 = Reduce((keep, None), XY)
     r3.got.append(None)
     going, r2.going, r1.going, vec = combine(
         s,
-        [(rows, at(1, keep) + at(0, core[2], core[3])), (rows // 4, at(1, *r2.got)), (rows // 8, at(1, *r1.got))],
+        [[(768, at(2, keep) + at(0, core[2])), (768, at(3, keep) + at(0, core[3]))],
+         far_z1(*r2.got), [(192, at(1, *r1.got))]],
         vec, vec_got)
     r3.got.append(r3.away(going))
     core[:2] = [trade(after(part, going), 1) for part in parts[:2]]
@@ -778,27 +803,33 @@
     r3.got[-1], core[0], core[1], r2.got[-1], r1.got[-1], grad_rem = together(
         r3.got[-1], core[0], core[1], r2.got[-1], r1.got[-1], grad_rem)
     going, r2.going, vec = combine(
-        s, [(rows // 2, at(1, keep, r3.got[-1]) + at(0, core[1])), (rows // 8, at(1, *r2.got))], vec, r3.got[-1])
+        s,
+        [[(768, at(1, keep, r3.got[-1]) + at(0, core[1]))],
+         [(192, at(of_z(0, 1), *r2.got[:4]) + at(of_z2(1), r2.got[4]))]],
+        vec, r3.got[-1])
     r3.got[1] = core[0]
     r3.got.append(r3.away(going))
     r2.send()
-    outer = sum(u.reshape(-1, 384)[: rows // 8].astype(F32) for u in r1.got)
+    outer = sum(u.reshape(-1, 384)[:192].astype(F32) for u in r1.got)
     out = finish(after(s, going, r2.going), (got0, got1), out)
 
     r3.got[-1], r2.got[-1], out, outer = together(r3.got[-1], r2.got[-1], out, outer)
-    going, vec = combine(s, [(rows // 4, at(1, *r3.got))], vec, r3.got[-1])
+    going, vec = combine(s, [far_z1(*r3.got)], vec, r3.got[-1])
     r3.got.append(r3.away(going))
     grad_got = trade(after(grad_rem, going), "y")
 
-    going, vec = combine(s, [(rows // 8, at(1, *r3.got))], vec, r3.got[-1])
+    going, vec = combine(
+        s, [[(192, at(of_z(0, 1), *r3.got[:4]) + at(of_z2(1), r3.got[4]))]], vec, r3.got[-1])
     r3.got.append(r3.away(going))
-    inner = sum(after(u, going).reshape(-1, 384)[: rows // 8].astype(F32) for u in r2.got)
     grad = finish(after(s, going), (grad_got,), grad)
-
-    inner = jnp.concatenate([inner[i * 48 : i * 48 + 48] for i in range(4)], 1)
+    inner = total_inner(
+        after(s, going, grad), at(of_z(0, 0), *r2.got[:4]) + at(of_z2(0), r2.got[4]) + at(0, r2.got[5]))
+
     r3.got[-1], grad, inner = together(r3.got[-1], grad, inner)
     apart = low_n == 1
-    sums = combine(s, [(rows // 8, at(0, *r3.got))], vec, r3.got[-1], last=True, apart=apart)
+    sums = combine(
+        s, [[(192, at(of_z(0, 0), *r3.got[:4]) + at(of_z2(0), r3.got[4]) + at(0, r3.got[5]))]],
+        vec, r3.got[-1], last=True, apart=apart)
     weights = [*sums[:4], inner, outer]
     if apart:
         return (out, grad, *weights, *sums[4:])

time: 154 us -> 150 us (0.974)
  starting transfers between devices: 28.7 us -> 31.3 us
  waiting for transfers between devices: 32.8 us -> 30.2 us
  Pallas kernels: 84.4 us -> 82.1 us
    ppermute x12, waiting for transfers between devices: 22.9 us -> 20.3 us  [trade_stage(): return lax.ppermute(value, ('dp', 'seq'), pairs)]
    ppermute x12, starting transfers between devices: 20.4 us -> 22.4 us  [trade_stage(): return lax.ppermute(value, ('dp', 'seq'), pairs)]
    pallas_call x1, Pallas kernels: 8.36 us -> 6.52 us  [local(): weight_call(last_body, [own_slot(half, d), full((half, d))] + [hold] * 5...]
    pallas_call x7 -> x8, Pallas kernels: 16.7 us -> 16.3 us  [the longest x1 5.2 us: local(): weight_call(inner_body, [hold] + pieces, (2, 2, 4, 192, 384), 'weight_inn...]
  transfers between devices with their start and end apart: 25 -> 25, of which waited for: 10 -> 12; matrix products, arithmetic and copies ran while one was open for 3% -> 2% of each run, Pallas kernels for 44% -> 43%
where the time goes in v4:
time: 150 us
  Pallas kernels  82.1 us (55%)
  starting transfers between devices  31.3 us (21%)
  waiting for transfers between devices  30.2 us (20%)
  local copies, waits for them, and re-layouts  3.37 us (2%)
  other arithmetic  2.1 us (1%)
    ppermute x12, starting transfers between devices, trade_stage(): return lax.ppermute(value, ('dp', 'seq'), pairs)  22.4 us
    ppermute x12, waiting for transfers between devices, trade_stage(): return lax.ppermute(value, ('dp', 'seq'), pairs)  20.3 us
    pallas_call x1, Pallas kernels, attn_fwd(): call(attn_fwd_body, (d // 256,), [own_slot(half, d), full((half, d))] + [...  13.5 us
    pallas_call x1, Pallas kernels, mlp_fwd(): call(mlp_fwd_body, (ff // w,), [full((t, d)), cols(d, w), vec(w), rows_of...  13.5 us
    pallas_call x1, Pallas kernels, attn_bwd(): call(attn_bwd_body, (d // 256,), [full((t, d)), rows_of(256, d), cols(t,...  9.94 us
    ppermute x5, waiting for transfers between devices, trade(): return lax.ppermute(value, 'seq', [(0, 1), (1, 0)])  7.54 us
    ppermute x5, starting transfers between devices, trade(): return lax.ppermute(value, 'seq', [(0, 1), (1, 0)])  7.17 us
    pallas_call x1, Pallas kernels, slope_first(): call(slope_first_body, (ff // w,), [cols(t, w), cols(d, w), full((t, d)),...  7.15 us
  transfers between devices with their start and end apart: 25, of which 12 were waited for; matrix products, arithmetic and copies ran while one was open for 2% of the time, Pallas kernels for 43%

profile of v4, /device:TPU:0, one launch (start us, length us, event | category | flops | bytes accessed | tf_op | source)
XLA Modules:
  0.0 150.1 jit_solution(9787793839956531271)
XLA Ops:
  1.7 3.1 %collective-permute-start = (bf16[256,768]{1,0:T(8,128)(2,1)S(1)}, bf16[256,768]{1,0:T(8,128)(2,1)S(1)}, u32[]{:S(2)}, u32[]{:S(2)}) collective-permute-start(bf16[256,768]{1,0:T(8,128)(2,1)S(1)} %dynamic-slice_bitcast_fusion.1), channel_id=1, source_target_pairs={{0,1},{1,0},{2,3},{3,2},{4,5},{5,4},{6,7},{7,6},{8,9},{9,8},{10,11... | collective-permute-start | bytes 1179656 | tf_op jit(solution)/shard_map/ppermute | solution.py:674
  7.2 7.5 %collective-permute-done.rem = bf16[256,768]{1,0:T(8,128)(2,1)S(1)} collective-permute-done((bf16[256,768]{1,0:T(8,128)(2,1)S(1)}, bf16[256,768]{1,0:T(8,128)(2,1)S(1)}, u32[]{:S(2)}, u32[]{:S(2)}) %collective-permute-start) | collective-permute-done | bytes 393248 | tf_op jit(solution)/shard_map/ppermute | solution.py:674
  14.7 13.5 %attn_fwd.1 = (bf16[512,768]{1,0:T(8,128)(2,1)S(1)}, bf16[768,512]{1,0:T(8,128)(2,1)S(1)}, bf16[512,768]{1,0:T(8,128)(2,1)S(1)}, bf16[12,512,512]{2,1,0:T(8,128)...) custom-call(s32[6]{0:T(128)S(1)} %stack.24.s, ...), custom_call_target="tpu_custom_call" | custom-call | flops 3200000 | bytes 18874 | tf_op jit(solution)/shard_map/attn_fwd/pallas_call | solution.py:144
  28.2 13.5 %mlp_fwd.1 = (bf16[512,3072]{1,0:T(8,128)(2,1)S(1)}, bf16[512,3072]{1,0:T(8,128)(2,1)S(1)}, f32[2,256,768]{2,1,0:T(8,128)}, bf16[128,768]{1,0:T(8,128)(2,1)S(1)}...) custom-call(s32[6]{0:T(128)S(1)} %stack.24.s, ...), custom_call_target="tpu_custom_call" | custom-call | flops 4800000 | bytes 25165 | tf_op jit(solution)/shard_map/mlp_fwd/pallas_call | solution.py:246
  41.7 2.0 %collective-permute-start.2 = (bf16[128,768]{1,0:T(8,128)(2,1)S(1)}, bf16[128,768]{1,0:T(8,128)(2,1)S(1)}, u32[]{:S(2)}, u32[]{:S(2)}) collective-permute-start(bf16[128,768]{1,0:T(8,128)(2,1)S(1)} %get-tuple-element.134), channel_id=1, source_target_pairs={{0,1},{1,0},{2,3},{3,2},{4,5},{5,4},{6,7},{7,6},{8,9},{9,8},{10,11... | collective-permute-start | bytes 589832 | tf_op jit(solution)/shard_map/ppermute | solution.py:674
  43.7 5.1 %weight_outer.1 = (bf16[2,2,2,2,192,384]{5,4,3,2,1,0:T(8,128)(2,1)S(1)}, bf16[2,2,2,2,192,384]{5,4,3,2,1,0:T(8,128)(2,1)S(1)}) custom-call(s32[6]{0:T(128)S(1)} %stack.24.s, bf16[512,3072]{1,0:T(8,128)(2,1)S(1)} %get-tuple-element.130.act, bf16[512,768]{1,0:T(8,128)(2,1)S(1)} %get-tuple-element.131.sl), custom_call_target="tpu_custom_call" | custom-call | flops 2400000 | bytes 10485 | tf_op jit(solution)/shard_map/weight_outer/pallas_call | solution.py:736
  49.4 6.9 %slope_inner.1 = (bf16[512,3072]{1,0:T(8,128)(2,1)S(1)}, f32[1,3072]{1,0:T(1,128)S(1)}) custom-call(s32[6]{0:T(128)S(1)} %stack.24.s, bf16[512,768]{1,0:T(8,128)(2,1)S(1)} %get-tuple-element.131.sl, bf16[3072,768]{1,0:T(8,128)(2,1)} %wo.3, bf16[512,3072]{1,0:T(8,128)(2,1)S(1)} %get-tuple-element.139.dg), custom_call_target="tpu_custom_call" | custom-call | flops 2400000 | bytes 12582 | tf_op jit(solution)/shard_map/slope_inner/pallas_call | solution.py:282
  56.6 1.7 %collective-permute-start.5 = (bf16[2,2,2,192,384]{4,3,2,1,0:T(8,128)(2,1)S(1)}, bf16[2,2,2,192,384]{4,3,2,1,0:T(8,128)(2,1)S(1)}, u32[]{:S(2)}, u32[]{:S(2)}) collective-permute-start(bf16[2,2,2,192,384]{4,3,2,1,0:T(8,128)(2,1)S(1)} %fusion.1), channel_id=1, source_target_pairs={{0,4},{1,5},{2,3},{3,2},{4,0},{5,1},{6,7},{7,6},{8,12},{9,13},{10,... | collective-permute-start | bytes 3538952 | tf_op jit(solution)/shard_map/ppermute | solution.py:685
  58.3 5.2 %weight_inner.1 = (bf16[2,2,4,192,384]{4,3,2,1,0:T(8,128)(2,1)S(1)}, bf16[2,4,192,384]{3,2,1,0:T(8,128)(2,1)S(1)}, bf16[2,4,192,384]{3,2,1,0:T(8,128)(2,1)S(1)}) custom-call(s32[6]{0:T(128)S(1)} %stack.24.s, bf16[512,768]{1,0:T(8,128)(2,1)S(1)} %get-tuple-element.128.nl, bf16[512,3072]{1,0:T(8,128)(2,1)S(1)} %get-tuple-element.143.si0.si1.si, ...), custom_call_target="tpu_custom_call" | custom-call | flops 2400000 | bytes 10485 | tf_op jit(solution)/shard_map/weight_inner/pallas_call | solution.py:746
  64.1 7.2 %slope_first.1 = (f32[512,768]{1,0:T(8,128)S(1)}, bf16[512,768]{1,0:T(8,128)(2,1)S(1)}, f32[3,768]{1,0:T(4,128)S(1)}) custom-call(s32[6]{0:T(128)S(1)} %stack.24.s, bf16[512,3072]{1,0:T(8,128)(2,1)S(1)} %get-tuple-element.143.si0.si1.si, bf16[768,3072]{1,0:T(8,128)(2,1)} %wi.3, f32[512,768]{1,0:T(8,128)S(1)} %get-tuple-element.147.ss, ...), custom_call_target="tpu_custom_call" | custom-call | flops 2400000 | bytes 14680 | tf_op jit(solution)/shard_map/slope_first/pallas_call | solution.py:331
  71.2 1.7 %collective-permute-done.5 = bf16[2,2,2,192,384]{4,3,2,1,0:T(8,128)(2,1)S(1)} collective-permute-done((bf16[2,2,2,192,384]{4,3,2,1,0:T(8,128)(2,1)S(1)}, bf16[2,2,2,192,384]{4,3,2,1,0:T(8,128)(2,1)S(1)}, u32[]{:S(2)}, u32[]{:S(2)}) %collective-permute-start.5) | collective-permute-done | bytes 1179680 | tf_op jit(solution)/shard_map/ppermute | solution.py:685
  73.2 1.7 %collective-permute-start.9 = (bf16[2,4,192,384]{3,2,1,0:T(8,128)(2,1)S(1)}, bf16[2,4,192,384]{3,2,1,0:T(8,128)(2,1)S(1)}, u32[]{:S(2)}, u32[]{:S(2)}) collective-permute-start(bf16[2,4,192,384]{3,2,1,0:T(8,128)(2,1)S(1)} %fusion), channel_id=1, source_target_pairs={{0,4},{1,5},{2,3},{3,2},{4,0},{5,1},{6,7},{7,6},{8,12},{9,13},{10,... | collective-permute-start | bytes 3538952 | tf_op jit(solution)/shard_map/ppermute | solution.py:685
  75.1 1.6 %collective-permute-start.8 = (bf16[2,2,192,384]{3,2,1,0:T(8,128)(2,1)S(1)}, bf16[2,2,192,384]{3,2,1,0:T(8,128)(2,1)S(1)}, u32[]{:S(2)}, u32[]{:S(2)}) collective-permute-start(bf16[2,2,192,384]{3,2,1,0:T(8,128)(2,1)S(1)} %fusion.3), channel_id=1, source_target_pairs={{0,8},{1,9},{2,10},{3,11},{4,12},{5,13},{6,14},{7,15},{8,0},{9,1},... | collective-permute-start | bytes 1769480 | tf_op jit(solution)/shard_map/ppermute | solution.py:685
  76.8 9.9 %attn_bwd.1 = (bf16[512,768]{1,0:T(8,128)(2,1)S(1)}, bf16[512,768]{1,0:T(8,128)(2,1)S(1)}, bf16[512,768]{1,0:T(8,128)(2,1)S(1)}) custom-call(s32[6]{0:T(128)S(1)} %stack.24.s, bf16[512,768]{1,0:T(8,128)(2,1)S(1)} %get-tuple-element.154.ml, bf16[768,768]{1,0:T(8,128)(2,1)} %wm.3, bf16[512,768]{1,0:T(8,128)(2,1)S(1)} %get-tuple-element.155.q, ...), custom_call_target="tpu_custom_call" | custom-call | flops 3600000 | bytes 15728 | tf_op jit(solution)/shard_map/attn_bwd/pallas_call | solution.py:375
  86.7 2.8 %collective-permute-done.8 = bf16[2,2,192,384]{3,2,1,0:T(8,128)(2,1)S(1)} collective-permute-done((bf16[2,2,192,384]{3,2,1,0:T(8,128)(2,1)S(1)}, bf16[2,2,192,384]{3,2,1,0:T(8,128)(2,1)S(1)}, u32[]{:S(2)}, u32[]{:S(2)}) %collective-permute-start.8) | collective-permute-done | bytes 589856 | tf_op jit(solution)/shard_map/ppermute | solution.py:685
  89.6 1.7 %collective-permute-start.10 = (bf16[2,192,384]{2,1,0:T(8,128)(2,1)S(1)}, bf16[2,192,384]{2,1,0:T(8,128)(2,1)S(1)}, u32[]{:S(2)}, u32[]{:S(2)}) collective-permute-start(bf16[2,192,384]{2,1,0:T(8,128)(2,1)S(1)} %fusion.4), channel_id=1, source_target_pairs={{0,1},{1,0},{2,6},{3,7},{4,5},{5,4},{6,2},{7,3},{8,9},{9,8},{10,14... | collective-permute-start | bytes 884744 | tf_op jit(solution)/shard_map/ppermute | solution.py:685
  92.0 6.5 %weight_last.1 = (bf16[2,2,4,192,384]{4,3,2,1,0:T(8,128)(2,1)S(1)}, bf16[4,192,384]{2,1,0:T(8,128)(2,1)S(1)}, bf16[4,192,384]{2,1,0:T(8,128)(2,1)S(1)}, bf16[4,1...) custom-call(s32[6]{0:T(128)S(1)} %stack.24.s, bf16[2,256,768]{2,1,0:T(8,128)(2,1)} %own.3, ...), custom_call_target="tpu_custom_call" | custom-call | flops 2400000 | bytes 10485 | tf_op jit(solution)/shard_map/weight_last/pallas_call | solution.py:767
  99.2 2.3 %collective-permute-done.14.refs_18_ = f32[32,384]{1,0:T(8,128)S(1)} collective-permute-done((f32[32,384]{1,0:T(8,128)S(1)}, f32[32,384]{1,0:T(8,128)S(1)}, u32[]{:S(2)}, u32[]{:S(2)}) %collective-permute-start.14) | collective-permute-done | bytes 49184 | tf_op jit(solution)/shard_map/ppermute | solution.py:675
  103.8 1.7 %collective-permute-start.15 = (bf16[1568,384]{1,0:T(8,128)(2,1)S(1)}, bf16[1568,384]{1,0:T(8,128)(2,1)S(1)}, u32[]{:S(2)}, u32[]{:S(2)}) collective-permute-start(bf16[1568,384]{1,0:T(8,128)(2,1)S(1)} %get-tuple-element.187), channel_id=1, source_target_pairs={{0,4},{1,5},{2,3},{3,2},{4,0},{5,1},{6,7},{7,6},{8,12},{9,13},{10,... | collective-permute-start | bytes 3612680 | tf_op jit(solution)/shard_map/ppermute | solution.py:685
  106.0 1.6 %collective-permute-start.18 = (bf16[384,384]{1,0:T(8,128)(2,1)S(1)}, bf16[384,384]{1,0:T(8,128)(2,1)S(1)}, u32[]{:S(2)}, u32[]{:S(2)}) collective-permute-start(bf16[384,384]{1,0:T(8,128)(2,1)S(1)} %get-tuple-element.192), channel_id=1, source_target_pairs={{0,8},{1,9},{2,10},{3,11},{4,12},{5,13},{6,14},{7,15},{8,0},{9,1},... | collective-permute-start | bytes 884744 | tf_op jit(solution)/shard_map/ppermute | solution.py:685
  107.6 2.6 %collective-permute-start.19 = (bf16[192,384]{1,0:T(8,128)(2,1)S(1)}, bf16[192,384]{1,0:T(8,128)(2,1)S(1)}, u32[]{:S(2)}, u32[]{:S(2)}) collective-permute-start(bf16[192,384]{1,0:T(8,128)(2,1)S(1)} %get-tuple-element.193), channel_id=1, source_target_pairs={{0,16},{1,17},{2,18},{3,19},{4,20},{5,21},{6,22},{7,23},{8,24},{9,... | collective-permute-start | bytes 442376 | tf_op jit(solution)/shard_map/ppermute | solution.py:685
  110.2 5.4 %input_grad.1 = (f32[2,256,768]{2,1,0:T(8,128)}, bf16[256,768]{1,0:T(8,128)(2,1)S(1)}) custom-call(s32[6]{0:T(128)S(1)} %stack.24.s, bf16[512,768]{1,0:T(8,128)(2,1)S(1)} %get-tuple-element.168.dq, bf16[512,768]{1,0:T(8,128)(2,1)S(1)} %get-tuple-element.169.dk, bf16[512,768]{1,0:T(8,128)(2,1)S(1)} %get-tuple-element.170.dv, bf16[768,768]{1,0:T(8,128)(2,1)} %wq.3, ...), custom_call_target="tpu_custom_call" | custom-call | flops 1800000 | bytes 8388 | tf_op jit(solution)/shard_map/input_grad/pallas_call | solution.py:407
  115.5 1.6 %collective-permute-done.19 = bf16[192,384]{1,0:T(8,128)(2,1)S(1)} collective-permute-done((bf16[192,384]{1,0:T(8,128)(2,1)S(1)}, bf16[192,384]{1,0:T(8,128)(2,1)S(1)}, u32[]{:S(2)}, u32[]{:S(2)}) %collective-permute-start.19) | collective-permute-done | bytes 147488 | tf_op jit(solution)/shard_map/ppermute | solution.py:685
  118.1 2.3 %collective-permute-done.15.refs_1_.refs_9_.refs_2_.refs_6_ = bf16[1568,384]{1,0:T(8,128)(2,1)S(1)} collective-permute-done((bf16[1568,384]{1,0:T(8,128)(2,1)S(1)}, bf16[1568,384]{1,0:T(8,128)(2,1)S(1)}, u32[]{:S(2)}, u32[]{:S(2)}) %collective-permute-start.15) | collective-permute-done | bytes 1204256 | tf_op jit(solution)/shard_map/ppermute | solution.py:685
  121.2 1.7 %collective-permute-start.20 = (bf16[800,384]{1,0:T(8,128)(2,1)S(1)}, bf16[800,384]{1,0:T(8,128)(2,1)S(1)}, u32[]{:S(2)}, u32[]{:S(2)}) collective-permute-start(bf16[800,384]{1,0:T(8,128)(2,1)S(1)} %get-tuple-element.201), channel_id=1, source_target_pairs={{0,1},{1,0},{2,6},{3,7},{4,5},{5,4},{6,2},{7,3},{8,9},{9,8},{10,14... | collective-permute-start | bytes 1843208 | tf_op jit(solution)/shard_map/ppermute | solution.py:685
  122.9 2.6 %collective-permute-start.21 = (bf16[192,384]{1,0:T(8,128)(2,1)S(1)}, bf16[192,384]{1,0:T(8,128)(2,1)S(1)}, u32[]{:S(2)}, u32[]{:S(2)}) collective-permute-start(bf16[192,384]{1,0:T(8,128)(2,1)S(1)} %get-tuple-element.202), channel_id=1, source_target_pairs={{0,16},{1,17},{2,18},{3,19},{4,20},{5,21},{6,22},{7,23},{8,24},{9,... | collective-permute-start | bytes 442376 | tf_op jit(solution)/shard_map/ppermute | solution.py:685
  127.8 2.7 %collective-permute-done.21.refs_5_ = bf16[192,384]{1,0:T(8,128)(2,1)S(1)} collective-permute-done((bf16[192,384]{1,0:T(8,128)(2,1)S(1)}, bf16[192,384]{1,0:T(8,128)(2,1)S(1)}, u32[]{:S(2)}, u32[]{:S(2)}) %collective-permute-start.21) | collective-permute-done | bytes 147488 | tf_op jit(solution)/shard_map/ppermute | solution.py:685
  132.2 1.7 %collective-permute-start.22 = (bf16[416,384]{1,0:T(8,128)(2,1)S(1)}, bf16[416,384]{1,0:T(8,128)(2,1)S(1)}, u32[]{:S(2)}, u32[]{:S(2)}) collective-permute-start(bf16[416,384]{1,0:T(8,128)(2,1)S(1)} %get-tuple-element.212), channel_id=1, source_target_pairs={{0,8},{1,9},{2,10},{3,11},{4,12},{5,13},{6,14},{7,15},{8,0},{9,1},... | collective-permute-start | bytes 958472 | tf_op jit(solution)/shard_map/ppermute | solution.py:685
  133.9 1.5 %collective-permute-start.24 = (bf16[256,768]{1,0:T(8,128)(2,1)S(1)}, bf16[256,768]{1,0:T(8,128)(2,1)S(1)}, u32[]{:S(2)}, u32[]{:S(2)}) collective-permute-start(bf16[256,768]{1,0:T(8,128)(2,1)S(1)} %get-tuple-element.217), channel_id=1, source_target_pairs={{0,1},{1,0},{2,3},{3,2},{4,5},{5,4},{6,7},{7,6},{8,9},{9,8},{10,11... | collective-permute-start | bytes 1179656 | tf_op jit(solution)/shard_map/ppermute | solution.py:674
  135.4 3.8 %collective-permute-done.22.refs_4_.refs_6_ = bf16[416,384]{1,0:T(8,128)(2,1)S(1)} collective-permute-done((bf16[416,384]{1,0:T(8,128)(2,1)S(1)}, bf16[416,384]{1,0:T(8,128)(2,1)S(1)}, u32[]{:S(2)}, u32[]{:S(2)}) %collective-permute-start.22) | collective-permute-done | bytes 319520 | tf_op jit(solution)/shard_map/ppermute | solution.py:685
  139.9 3.4 %collective-permute-start.23 = (bf16[224,384]{1,0:T(8,128)(2,1)S(1)}, bf16[224,384]{1,0:T(8,128)(2,1)S(1)}, u32[]{:S(2)}, u32[]{:S(2)}) collective-permute-start(bf16[224,384]{1,0:T(8,128)(2,1)S(1)} %get-tuple-element.214), channel_id=1, source_target_pairs={{0,16},{1,17},{2,18},{3,19},{4,20},{5,21},{6,22},{7,23},{8,24},{9,... | collective-permute-start | bytes 516104 | tf_op jit(solution)/shard_map/ppermute | solution.py:685
  146.2 2.4 %collective-permute-done.23.refs_5_.refs_7_ = bf16[224,384]{1,0:T(8,128)(2,1)S(1)} collective-permute-done((bf16[224,384]{1,0:T(8,128)(2,1)S(1)}, bf16[224,384]{1,0:T(8,128)(2,1)S(1)}, u32[]{:S(2)}, u32[]{:S(2)}) %collective-permute-start.23) | collective-permute-done | bytes 172064 | tf_op jit(solution)/shard_map/ppermute | solution.py:685
  (47 shorter events, 20.3 us)
Async XLA Ops:
  0.7 5.2 %copy-start = (s32[2]{0:T(128)S(1)}, s32[2]{0:T(128)}, u32[]{:S(2)}) copy-start(s32[2]{0:T(128)} %param.20) | copy-start | bytes 28
  1.7 13.0 %collective-permute-start = (bf16[256,768]{1,0:T(8,128)(2,1)S(1)}, bf16[256,768]{1,0:T(8,128)(2,1)S(1)}, u32[]{:S(2)}, u32[]{:S(2)}) collective-permute-start(bf16[256,768]{1,0:T(8,128)(2,1)S(1)} %dynamic-slice_bitcast_fusion.1), channel_id=1, source_target_pairs={{0,1},{1,0},{2,3},{3,2},{4,5},{5,4},{6,7},{7,6},{8,9},{9,8},{10,11... | collective-permute-start | bytes 1179656 | tf_op jit(solution)/shard_map/ppermute | solution.py:674
  5.8 22.4 %collective-permute-start.1 = (bf16[256,768]{1,0:T(8,128)(2,1)S(1)}, bf16[256,768]{1,0:T(8,128)(2,1)S(1)}, u32[]{:S(2)}, u32[]{:S(2)}) collective-permute-start(bf16[256,768]{1,0:T(8,128)(2,1)S(1)} %dynamic-slice_bitcast_fusion), channel_id=1, source_target_pairs={{0,1},{1,0},{2,3},{3,2},{4,5},{5,4},{6,7},{7,6},{8,9},{9,8},{10,11... | collective-permute-start | bytes 1179656 | tf_op jit(solution)/shard_map/ppermute | solution.py:674
  41.7 7.1 %collective-permute-start.2 = (bf16[128,768]{1,0:T(8,128)(2,1)S(1)}, bf16[128,768]{1,0:T(8,128)(2,1)S(1)}, u32[]{:S(2)}, u32[]{:S(2)}) collective-permute-start(bf16[128,768]{1,0:T(8,128)(2,1)S(1)} %get-tuple-element.134), channel_id=1, source_target_pairs={{0,1},{1,0},{2,3},{3,2},{4,5},{5,4},{6,7},{7,6},{8,9},{9,8},{10,11... | collective-permute-start | bytes 589832 | tf_op jit(solution)/shard_map/ppermute | solution.py:674
  48.8 7.4 %collective-permute-start.3 = (bf16[2,2,2,2,192,384]{5,4,3,2,1,0:T(8,128)(2,1)S(1)}, bf16[2,2,2,2,192,384]{5,4,3,2,1,0:T(8,128)(2,1)S(1)}, u32[]{:S(2)}, u32[]{:S(2)}) collective-permute-start(bf16[2,2,2,2,192,384]{5,4,3,2,1,0:T(8,128)(2,1)S(1)} %get-tuple-element.136), channel_id=1, source_target_pairs={{0,2},{2,0},{4,6},{6,4},{8,10},{10,8},{12,14},{14,12},{16,18},{18,... | collective-permute-start | bytes 7077896 | tf_op jit(solution)/shard_map/ppermute | solution.py:675
  48.9 7.3 %collective-permute-start.4 = (bf16[128,768]{1,0:T(8,128)(2,1)S(1)}, bf16[128,768]{1,0:T(8,128)(2,1)S(1)}, u32[]{:S(2)}, u32[]{:S(2)}) collective-permute-start(bf16[128,768]{1,0:T(8,128)(2,1)S(1)} %get-tuple-element.137), channel_id=1, source_target_pairs={{0,1},{1,0},{2,3},{3,2},{4,5},{5,4},{6,7},{7,6},{8,9},{9,8},{10,11... | collective-permute-start | bytes 589832 | tf_op jit(solution)/shard_map/ppermute | solution.py:674
  56.6 16.3 %collective-permute-start.5 = (bf16[2,2,2,192,384]{4,3,2,1,0:T(8,128)(2,1)S(1)}, bf16[2,2,2,192,384]{4,3,2,1,0:T(8,128)(2,1)S(1)}, u32[]{:S(2)}, u32[]{:S(2)}) collective-permute-start(bf16[2,2,2,192,384]{4,3,2,1,0:T(8,128)(2,1)S(1)} %fusion.1), channel_id=1, source_target_pairs={{0,4},{1,5},{2,3},{3,2},{4,0},{5,1},{6,7},{7,6},{8,12},{9,13},{10,... | collective-permute-start | bytes 3538952 | tf_op jit(solution)/shard_map/ppermute | solution.py:685
  63.5 9.4 %collective-permute-start.6 = (bf16[2,4,192,384]{3,2,1,0:T(8,128)(2,1)S(1)}, bf16[2,4,192,384]{3,2,1,0:T(8,128)(2,1)S(1)}, u32[]{:S(2)}, u32[]{:S(2)}) collective-permute-start(bf16[2,4,192,384]{3,2,1,0:T(8,128)(2,1)S(1)} %get-tuple-element.144), channel_id=1, source_target_pairs={{0,2},{2,0},{4,6},{6,4},{8,10},{10,8},{12,14},{14,12},{16,18},{18,... | collective-permute-start | bytes 3538952 | tf_op jit(solution)/shard_map/ppermute | solution.py:675
  63.6 9.3 %collective-permute-start.7 = (bf16[2,4,192,384]{3,2,1,0:T(8,128)(2,1)S(1)}, bf16[2,4,192,384]{3,2,1,0:T(8,128)(2,1)S(1)}, u32[]{:S(2)}, u32[]{:S(2)}) collective-permute-start(bf16[2,4,192,384]{3,2,1,0:T(8,128)(2,1)S(1)} %get-tuple-element.145), channel_id=1, source_target_pairs={{0,2},{2,0},{4,6},{6,4},{8,10},{10,8},{12,14},{14,12},{16,18},{18,... | collective-permute-start | bytes 3538952 | tf_op jit(solution)/shard_map/ppermute | solution.py:675
  73.2 16.3 %collective-permute-start.9 = (bf16[2,4,192,384]{3,2,1,0:T(8,128)(2,1)S(1)}, bf16[2,4,192,384]{3,2,1,0:T(8,128)(2,1)S(1)}, u32[]{:S(2)}, u32[]{:S(2)}) collective-permute-start(bf16[2,4,192,384]{3,2,1,0:T(8,128)(2,1)S(1)} %fusion), channel_id=1, source_target_pairs={{0,4},{1,5},{2,3},{3,2},{4,0},{5,1},{6,7},{7,6},{8,12},{9,13},{10,... | collective-permute-start | bytes 3538952 | tf_op jit(solution)/shard_map/ppermute | solution.py:685
  75.1 14.3 %collective-permute-start.8 = (bf16[2,2,192,384]{3,2,1,0:T(8,128)(2,1)S(1)}, bf16[2,2,192,384]{3,2,1,0:T(8,128)(2,1)S(1)}, u32[]{:S(2)}, u32[]{:S(2)}) collective-permute-start(bf16[2,2,192,384]{3,2,1,0:T(8,128)(2,1)S(1)} %fusion.3), channel_id=1, source_target_pairs={{0,8},{1,9},{2,10},{3,11},{4,12},{5,13},{6,14},{7,15},{8,0},{9,1},... | collective-permute-start | bytes 1769480 | tf_op jit(solution)/shard_map/ppermute | solution.py:685
  89.6 8.9 %collective-permute-start.10 = (bf16[2,192,384]{2,1,0:T(8,128)(2,1)S(1)}, bf16[2,192,384]{2,1,0:T(8,128)(2,1)S(1)}, u32[]{:S(2)}, u32[]{:S(2)}) collective-permute-start(bf16[2,192,384]{2,1,0:T(8,128)(2,1)S(1)} %fusion.4), channel_id=1, source_target_pairs={{0,1},{1,0},{2,6},{3,7},{4,5},{5,4},{6,2},{7,3},{8,9},{9,8},{10,14... | collective-permute-start | bytes 884744 | tf_op jit(solution)/shard_map/ppermute | solution.py:685
  91.6 11.2 %collective-permute-start.11 = (bf16[4,192,384]{2,1,0:T(8,128)(2,1)S(1)}, bf16[4,192,384]{2,1,0:T(8,128)(2,1)S(1)}, u32[]{:S(2)}, u32[]{:S(2)}) collective-permute-start(bf16[4,192,384]{2,1,0:T(8,128)(2,1)S(1)} %fusion.2), channel_id=1, source_target_pairs={{0,1},{1,0},{2,6},{3,7},{4,5},{5,4},{6,2},{7,3},{8,9},{9,8},{10,14... | collective-permute-start | bytes 1769480 | tf_op jit(solution)/shard_map/ppermute | solution.py:685
  98.6 4.2 %collective-permute-start.12 = (bf16[4,192,384]{2,1,0:T(8,128)(2,1)S(1)}, bf16[4,192,384]{2,1,0:T(8,128)(2,1)S(1)}, u32[]{:S(2)}, u32[]{:S(2)}) collective-permute-start(bf16[4,192,384]{2,1,0:T(8,128)(2,1)S(1)} %get-tuple-element.179), channel_id=1, source_target_pairs={{0,2},{2,0},{4,6},{6,4},{8,10},{10,8},{12,14},{14,12},{16,18},{18,... | collective-permute-start | bytes 1769480 | tf_op jit(solution)/shard_map/ppermute | solution.py:675
  98.7 4.1 %collective-permute-start.13 = (bf16[4,192,384]{2,1,0:T(8,128)(2,1)S(1)}, bf16[4,192,384]{2,1,0:T(8,128)(2,1)S(1)}, u32[]{:S(2)}, u32[]{:S(2)}) collective-permute-start(bf16[4,192,384]{2,1,0:T(8,128)(2,1)S(1)} %get-tuple-element.180), channel_id=1, source_target_pairs={{0,2},{2,0},{4,6},{6,4},{8,10},{10,8},{12,14},{14,12},{16,18},{18,... | collective-permute-start | bytes 1769480 | tf_op jit(solution)/shard_map/ppermute | solution.py:675
  99.2 2.4 %collective-permute-start.14 = (f32[32,384]{1,0:T(8,128)S(1)}, f32[32,384]{1,0:T(8,128)S(1)}, u32[]{:S(2)}, u32[]{:S(2)}) collective-permute-start(f32[32,384]{1,0:T(8,128)S(1)} %get-tuple-element.181.refs_17_), channel_id=1, source_target_pairs={{0,2},{2,0},{4,6},{6,4},{8,10},{10,8},{12,14},{14,12},{16,18},{18,... | collective-permute-start | bytes 147464 | tf_op jit(solution)/shard_map/ppermute | solution.py:675
  103.8 16.5 %collective-permute-start.15 = (bf16[1568,384]{1,0:T(8,128)(2,1)S(1)}, bf16[1568,384]{1,0:T(8,128)(2,1)S(1)}, u32[]{:S(2)}, u32[]{:S(2)}) collective-permute-start(bf16[1568,384]{1,0:T(8,128)(2,1)S(1)} %get-tuple-element.187), channel_id=1, source_target_pairs={{0,4},{1,5},{2,3},{3,2},{4,0},{5,1},{6,7},{7,6},{8,12},{9,13},{10,... | collective-permute-start | bytes 3612680 | tf_op jit(solution)/shard_map/ppermute | solution.py:685
  105.5 12.6 %collective-permute-start.16 = (bf16[4,192,384]{2,1,0:T(8,128)(2,1)S(1)}, bf16[4,192,384]{2,1,0:T(8,128)(2,1)S(1)}, u32[]{:S(2)}, u32[]{:S(2)}) collective-permute-start(bf16[4,192,384]{2,1,0:T(8,128)(2,1)S(1)} %get-tuple-element.189), channel_id=1, source_target_pairs={{0,2},{2,0},{4,6},{6,4},{8,10},{10,8},{12,14},{14,12},{16,18},{18,... | collective-permute-start | bytes 1769480 | tf_op jit(solution)/shard_map/ppermute | solution.py:675
  105.5 12.6 %collective-permute-start.17 = (bf16[4,192,384]{2,1,0:T(8,128)(2,1)S(1)}, bf16[4,192,384]{2,1,0:T(8,128)(2,1)S(1)}, u32[]{:S(2)}, u32[]{:S(2)}) collective-permute-start(bf16[4,192,384]{2,1,0:T(8,128)(2,1)S(1)} %get-tuple-element.191), channel_id=1, source_target_pairs={{0,2},{2,0},{4,6},{6,4},{8,10},{10,8},{12,14},{14,12},{16,18},{18,... | collective-permute-start | bytes 1769480 | tf_op jit(solution)/shard_map/ppermute | solution.py:675
  106.0 12.1 %collective-permute-start.18 = (bf16[384,384]{1,0:T(8,128)(2,1)S(1)}, bf16[384,384]{1,0:T(8,128)(2,1)S(1)}, u32[]{:S(2)}, u32[]{:S(2)}) collective-permute-start(bf16[384,384]{1,0:T(8,128)(2,1)S(1)} %get-tuple-element.192), channel_id=1, source_target_pairs={{0,8},{1,9},{2,10},{3,11},{4,12},{5,13},{6,14},{7,15},{8,0},{9,1},... | collective-permute-start | bytes 884744 | tf_op jit(solution)/shard_map/ppermute | solution.py:685
  107.6 9.6 %collective-permute-start.19 = (bf16[192,384]{1,0:T(8,128)(2,1)S(1)}, bf16[192,384]{1,0:T(8,128)(2,1)S(1)}, u32[]{:S(2)}, u32[]{:S(2)}) collective-permute-start(bf16[192,384]{1,0:T(8,128)(2,1)S(1)} %get-tuple-element.193), channel_id=1, source_target_pairs={{0,16},{1,17},{2,18},{3,19},{4,20},{5,21},{6,22},{7,23},{8,24},{9,... | collective-permute-start | bytes 442376 | tf_op jit(solution)/shard_map/ppermute | solution.py:685
  121.2 10.2 %collective-permute-start.20 = (bf16[800,384]{1,0:T(8,128)(2,1)S(1)}, bf16[800,384]{1,0:T(8,128)(2,1)S(1)}, u32[]{:S(2)}, u32[]{:S(2)}) collective-permute-start(bf16[800,384]{1,0:T(8,128)(2,1)S(1)} %get-tuple-element.201), channel_id=1, source_target_pairs={{0,1},{1,0},{2,6},{3,7},{4,5},{5,4},{6,2},{7,3},{8,9},{9,8},{10,14... | collective-permute-start | bytes 1843208 | tf_op jit(solution)/shard_map/ppermute | solution.py:685
  122.9 7.6 %collective-permute-start.21 = (bf16[192,384]{1,0:T(8,128)(2,1)S(1)}, bf16[192,384]{1,0:T(8,128)(2,1)S(1)}, u32[]{:S(2)}, u32[]{:S(2)}) collective-permute-start(bf16[192,384]{1,0:T(8,128)(2,1)S(1)} %get-tuple-element.202), channel_id=1, source_target_pairs={{0,16},{1,17},{2,18},{3,19},{4,20},{5,21},{6,22},{7,23},{8,24},{9,... | collective-permute-start | bytes 442376 | tf_op jit(solution)/shard_map/ppermute | solution.py:685
  132.2 7.1 %collective-permute-start.22 = (bf16[416,384]{1,0:T(8,128)(2,1)S(1)}, bf16[416,384]{1,0:T(8,128)(2,1)S(1)}, u32[]{:S(2)}, u32[]{:S(2)}) collective-permute-start(bf16[416,384]{1,0:T(8,128)(2,1)S(1)} %get-tuple-element.212), channel_id=1, source_target_pairs={{0,8},{1,9},{2,10},{3,11},{4,12},{5,13},{6,14},{7,15},{8,0},{9,1},... | collective-permute-start | bytes 958472 | tf_op jit(solution)/shard_map/ppermute | solution.py:685
  133.9 9.4 %collective-permute-start.24 = (bf16[256,768]{1,0:T(8,128)(2,1)S(1)}, bf16[256,768]{1,0:T(8,128)(2,1)S(1)}, u32[]{:S(2)}, u32[]{:S(2)}) collective-permute-start(bf16[256,768]{1,0:T(8,128)(2,1)S(1)} %get-tuple-element.217), channel_id=1, source_target_pairs={{0,1},{1,0},{2,3},{3,2},{4,5},{5,4},{6,7},{7,6},{8,9},{9,8},{10,11... | collective-permute-start | bytes 1179656 | tf_op jit(solution)/shard_map/ppermute | solution.py:674
  139.9 8.7 %collective-permute-start.23 = (bf16[224,384]{1,0:T(8,128)(2,1)S(1)}, bf16[224,384]{1,0:T(8,128)(2,1)S(1)}, u32[]{:S(2)}, u32[]{:S(2)}) collective-permute-start(bf16[224,384]{1,0:T(8,128)(2,1)S(1)} %get-tuple-element.214), channel_id=1, source_target_pairs={{0,16},{1,17},{2,18},{3,19},{4,20},{5,21},{6,22},{7,23},{8,24},{9,... | collective-permute-start | bytes 516104 | tf_op jit(solution)/shard_map/ppermute | solution.py:685

commit v5 on v4

--- a/solution.py
+++ b/solution.py
@@ -278,7 +278,7 @@
 def slope_inner(s, sl, wo, dg):
     t, d = sl.shape
     ff = wo.shape[0]
-    w = 512
+    w = 1536
     return call(
         slope_inner_body,
         (ff // w,),
@@ -634,28 +634,24 @@
     )(s, *args, vec, vec_in)
 
 
-def finish_body(s, *refs):
-    *recv, _, out = refs
-    at = 0
-    for part in recv:
-        out[0, at : at + part.shape[0]] = part[...].astype(F32)
-        at += part.shape[0]
-
-
-def finish(s, recv, whole):
-    half, d = whole.shape[1:]
+def finish_body(s, recv, whole, out):
+    out[0] = recv[...].astype(F32)
+
+
+def finish(s, recv, whole, part=0):
+    rows, d = recv.shape
     return call(
         finish_body,
         (1,),
-        [full(part.shape) for part in recv] + [pl.BlockSpec(memory_space=pl.ANY)],
-        pl.BlockSpec((1, half, d), lambda g, s: (1 - s[0], 0, 0)),
+        [full(recv.shape), pl.BlockSpec(memory_space=pl.ANY)],
+        pl.BlockSpec((1, rows, d), lambda g, s: (1 - s[0], part, 0)),
         shape(whole.shape, F32),
         [],
         "finish",
         0,
         1 << 20,
-        aliases={len(recv) + 1: 0},
-    )(s, *recv, whole)
+        aliases={2: 0},
+    )(s, recv, whole)
 
 
 def local(n, tokens, cotangent, lengths, query_weight, query_bias, key_weight, value_weight, value_bias,
@@ -734,12 +730,11 @@
 
     got0 = trade(out0, "y")
     r1 = Reduce(weight_call(outer_body, [piece, hold], (2, 2, 2, 2, 192, 384), "weight_outer", 2_400_000_000)(s, act, sl), XZY)
-    r1.going, got0, out1 = together(r1.going, got0, out1)
+    r1.going, got0 = together(r1.going, got0)
     r1.send()
-    got1 = trade(out1, "y")
     si, bi = slope_inner(after(s, r1.going), sl, outer_weight, dg)
 
-    r1.got[-1], got1, bi = together(r1.got[-1], got1, bi)
+    r1.got[-1], bi = together(r1.got[-1], bi)
     r1.add()
     r1.send()
     pieces = [pl.BlockSpec((t, 384), lambda g, s, y=y: (0, 4 * y + g)) for y in range(2)]
@@ -811,21 +806,24 @@
     r3.got.append(r3.away(going))
     r2.send()
     outer = sum(u.reshape(-1, 384)[:192].astype(F32) for u in r1.got)
-    out = finish(after(s, going, r2.going), (got0, got1), out)
+    out = finish(after(s, going, r2.going), got0, out)
 
     r3.got[-1], r2.got[-1], out, outer = together(r3.got[-1], r2.got[-1], out, outer)
     going, vec = combine(s, [far_z1(*r3.got)], vec, r3.got[-1])
     r3.got.append(r3.away(going))
     grad_got = trade(after(grad_rem, going), "y")
+    got1 = trade(after(out1, going), "y")
 
     going, vec = combine(
         s, [[(192, at(of_z(0, 1), *r3.got[:4]) + at(of_z2(1), r3.got[4]))]], vec, r3.got[-1])
     r3.got.append(r3.away(going))
-    grad = finish(after(s, going), (grad_got,), grad)
+    grad = finish(after(s, going), grad_got, grad)
     inner = total_inner(
         after(s, going, grad), at(of_z(0, 0), *r2.got[:4]) + at(of_z2(0), r2.got[4]) + at(0, r2.got[5]))
 
-    r3.got[-1], grad, inner = together(r3.got[-1], grad, inner)
+    out = finish(after(s, inner), got1, out, 1)
+
+    r3.got[-1], grad, inner, out = together(r3.got[-1], grad, inner, out)
     apart = low_n == 1
     sums = combine(
         s, [[(192, at(of_z(0, 0), *r3.got[:4]) + at(of_z2(0), r3.got[4]) + at(0, r3.got[5]))]],

time: 150 us -> 148 us (0.987)
  starting transfers between devices: 31.3 us -> 29.2 us
    ppermute x12, starting transfers between devices: 22.4 us -> 20.2 us  [trade_stage(): return lax.ppermute(value, ('dp', 'seq'), pairs)]
    pallas_call x2 -> x3, Pallas kernels: 2.94 us -> 4.09 us  [finish(): call(finish_body, (1,), [full(recv.shape), pl.BlockSpec(memory_space=pl.A...]
  transfers between devices with their start and end apart: 25 -> 25, of which waited for: 12 -> 14; matrix products, arithmetic and copies ran while one was open for 2% -> 2% of each run, Pallas kernels for 43% -> 43%
where the time goes in v5:
time: 148 us
  Pallas kernels  81.8 us (55%)
  waiting for transfers between devices  30.6 us (21%)
  starting transfers between devices  29.2 us (20%)
  local copies, waits for them, and re-layouts  3.37 us (2%)
  other arithmetic  2.11 us (1%)
    ppermute x12, starting transfers between devices, trade_stage(): return lax.ppermute(value, ('dp', 'seq'), pairs)  20.2 us
    ppermute x12, waiting for transfers between devices, trade_stage(): return lax.ppermute(value, ('dp', 'seq'), pairs)  19.7 us
    pallas_call x1, Pallas kernels, attn_fwd(): call(attn_fwd_body, (d // 256,), [own_slot(half, d), full((half, d))] + [...  13.5 us
    pallas_call x1, Pallas kernels, mlp_fwd(): call(mlp_fwd_body, (ff // w,), [full((t, d)), cols(d, w), vec(w), rows_of...  13.5 us
    pallas_call x1, Pallas kernels, attn_bwd(): call(attn_bwd_body, (d // 256,), [full((t, d)), rows_of(256, d), cols(t,...  9.94 us
    ppermute x5, waiting for transfers between devices, trade(): return lax.ppermute(value, 'seq', [(0, 1), (1, 0)])  8.58 us
    ppermute x5, starting transfers between devices, trade(): return lax.ppermute(value, 'seq', [(0, 1), (1, 0)])  7.2 us
    pallas_call x1, Pallas kernels, slope_first(): call(slope_first_body, (ff // w,), [cols(t, w), cols(d, w), full((t, d)),...  6.97 us
  transfers between devices with their start and end apart: 25, of which 14 were waited for; matrix products, arithmetic and copies ran while one was open for 2% of the time, Pallas kernels for 43%

profile of v5, /device:TPU:0, one launch (start us, length us, event | category | flops | bytes accessed | tf_op | source)
XLA Modules:
  0.0 148.2 jit_solution(6053777365555481538)
XLA Ops:
  1.7 3.1 %collective-permute-start = (bf16[256,768]{1,0:T(8,128)(2,1)S(1)}, bf16[256,768]{1,0:T(8,128)(2,1)S(1)}, u32[]{:S(2)}, u32[]{:S(2)}) collective-permute-start(bf16[256,768]{1,0:T(8,128)(2,1)S(1)} %dynamic-slice_bitcast_fusion.1), channel_id=1, source_target_pairs={{0,1},{1,0},{2,3},{3,2},{4,5},{5,4},{6,7},{7,6},{8,9},{9,8},{10,11... | collective-permute-start | bytes 1179656 | tf_op jit(solution)/shard_map/ppermute | solution.py:670
  7.2 7.5 %collective-permute-done.rem = bf16[256,768]{1,0:T(8,128)(2,1)S(1)} collective-permute-done((bf16[256,768]{1,0:T(8,128)(2,1)S(1)}, bf16[256,768]{1,0:T(8,128)(2,1)S(1)}, u32[]{:S(2)}, u32[]{:S(2)}) %collective-permute-start) | collective-permute-done | bytes 393248 | tf_op jit(solution)/shard_map/ppermute | solution.py:670
  14.7 13.5 %attn_fwd.1 = (bf16[512,768]{1,0:T(8,128)(2,1)S(1)}, bf16[768,512]{1,0:T(8,128)(2,1)S(1)}, bf16[512,768]{1,0:T(8,128)(2,1)S(1)}, bf16[12,512,512]{2,1,0:T(8,128)...) custom-call(s32[6]{0:T(128)S(1)} %stack.24.s, ...), custom_call_target="tpu_custom_call" | custom-call | flops 3200000 | bytes 18874 | tf_op jit(solution)/shard_map/attn_fwd/pallas_call | solution.py:144
  28.2 13.5 %mlp_fwd.1 = (bf16[512,3072]{1,0:T(8,128)(2,1)S(1)}, bf16[512,3072]{1,0:T(8,128)(2,1)S(1)}, f32[2,256,768]{2,1,0:T(8,128)}, bf16[128,768]{1,0:T(8,128)(2,1)S(1)}...) custom-call(s32[6]{0:T(128)S(1)} %stack.24.s, ...), custom_call_target="tpu_custom_call" | custom-call | flops 4800000 | bytes 25165 | tf_op jit(solution)/shard_map/mlp_fwd/pallas_call | solution.py:246
  41.7 2.0 %collective-permute-start.2 = (bf16[128,768]{1,0:T(8,128)(2,1)S(1)}, bf16[128,768]{1,0:T(8,128)(2,1)S(1)}, u32[]{:S(2)}, u32[]{:S(2)}) collective-permute-start(bf16[128,768]{1,0:T(8,128)(2,1)S(1)} %get-tuple-element.135), channel_id=1, source_target_pairs={{0,1},{1,0},{2,3},{3,2},{4,5},{5,4},{6,7},{7,6},{8,9},{9,8},{10,11... | collective-permute-start | bytes 589832 | tf_op jit(solution)/shard_map/ppermute | solution.py:670
  43.7 5.1 %weight_outer.1 = (bf16[2,2,2,2,192,384]{5,4,3,2,1,0:T(8,128)(2,1)S(1)}, bf16[2,2,2,2,192,384]{5,4,3,2,1,0:T(8,128)(2,1)S(1)}) custom-call(s32[6]{0:T(128)S(1)} %stack.24.s, bf16[512,3072]{1,0:T(8,128)(2,1)S(1)} %get-tuple-element.131.act, bf16[512,768]{1,0:T(8,128)(2,1)S(1)} %get-tuple-element.132.sl), custom_call_target="tpu_custom_call" | custom-call | flops 2400000 | bytes 10485 | tf_op jit(solution)/shard_map/weight_outer/pallas_call | solution.py:732
  48.9 5.5 %slope_inner.1 = (bf16[512,3072]{1,0:T(8,128)(2,1)S(1)}, f32[1,3072]{1,0:T(1,128)S(1)}) custom-call(s32[6]{0:T(128)S(1)} %stack.24.s, bf16[512,768]{1,0:T(8,128)(2,1)S(1)} %get-tuple-element.132.sl, bf16[3072,768]{1,0:T(8,128)(2,1)} %wo.3, bf16[512,3072]{1,0:T(8,128)(2,1)S(1)} %get-tuple-element.138.dg), custom_call_target="tpu_custom_call" | custom-call | flops 2400000 | bytes 12582 | tf_op jit(solution)/shard_map/slope_inner/pallas_call | solution.py:282
  54.7 1.6 %collective-permute-start.4 = (bf16[2,2,2,192,384]{4,3,2,1,0:T(8,128)(2,1)S(1)}, bf16[2,2,2,192,384]{4,3,2,1,0:T(8,128)(2,1)S(1)}, u32[]{:S(2)}, u32[]{:S(2)}) collective-permute-start(bf16[2,2,2,192,384]{4,3,2,1,0:T(8,128)(2,1)S(1)} %fusion.1), channel_id=1, source_target_pairs={{0,4},{1,5},{2,3},{3,2},{4,0},{5,1},{6,7},{7,6},{8,12},{9,13},{10,... | collective-permute-start | bytes 3538952 | tf_op jit(solution)/shard_map/ppermute | solution.py:681
  56.3 5.4 %weight_inner.1 = (bf16[2,2,4,192,384]{4,3,2,1,0:T(8,128)(2,1)S(1)}, bf16[2,4,192,384]{3,2,1,0:T(8,128)(2,1)S(1)}, bf16[2,4,192,384]{3,2,1,0:T(8,128)(2,1)S(1)}) custom-call(s32[6]{0:T(128)S(1)} %stack.24.s, bf16[512,768]{1,0:T(8,128)(2,1)S(1)} %get-tuple-element.129.nl, bf16[512,3072]{1,0:T(8,128)(2,1)S(1)} %get-tuple-element.142.si0.si1.si, ...), custom_call_target="tpu_custom_call" | custom-call | flops 2400000 | bytes 10485 | tf_op jit(solution)/shard_map/weight_inner/pallas_call | solution.py:741
  62.3 7.0 %slope_first.1 = (f32[512,768]{1,0:T(8,128)S(1)}, bf16[512,768]{1,0:T(8,128)(2,1)S(1)}, f32[3,768]{1,0:T(4,128)S(1)}) custom-call(s32[6]{0:T(128)S(1)} %stack.24.s, bf16[512,3072]{1,0:T(8,128)(2,1)S(1)} %get-tuple-element.142.si0.si1.si, bf16[768,3072]{1,0:T(8,128)(2,1)} %wi.3, f32[512,768]{1,0:T(8,128)S(1)} %get-tuple-element.146.ss, ...), custom_call_target="tpu_custom_call" | custom-call | flops 2400000 | bytes 14680 | tf_op jit(solution)/shard_map/slope_first/pallas_call | solution.py:331
  69.2 1.8 %collective-permute-done.4 = bf16[2,2,2,192,384]{4,3,2,1,0:T(8,128)(2,1)S(1)} collective-permute-done((bf16[2,2,2,192,384]{4,3,2,1,0:T(8,128)(2,1)S(1)}, bf16[2,2,2,192,384]{4,3,2,1,0:T(8,128)(2,1)S(1)}, u32[]{:S(2)}, u32[]{:S(2)}) %collective-permute-start.4) | collective-permute-done | bytes 1179680 | tf_op jit(solution)/shard_map/ppermute | solution.py:681
  71.3 1.6 %collective-permute-start.8 = (bf16[2,4,192,384]{3,2,1,0:T(8,128)(2,1)S(1)}, bf16[2,4,192,384]{3,2,1,0:T(8,128)(2,1)S(1)}, u32[]{:S(2)}, u32[]{:S(2)}) collective-permute-start(bf16[2,4,192,384]{3,2,1,0:T(8,128)(2,1)S(1)} %fusion), channel_id=1, source_target_pairs={{0,4},{1,5},{2,3},{3,2},{4,0},{5,1},{6,7},{7,6},{8,12},{9,13},{10,... | collective-permute-start | bytes 3538952 | tf_op jit(solution)/shard_map/ppermute | solution.py:681
  73.1 1.6 %collective-permute-start.7 = (bf16[2,2,192,384]{3,2,1,0:T(8,128)(2,1)S(1)}, bf16[2,2,192,384]{3,2,1,0:T(8,128)(2,1)S(1)}, u32[]{:S(2)}, u32[]{:S(2)}) collective-permute-start(bf16[2,2,192,384]{3,2,1,0:T(8,128)(2,1)S(1)} %fusion.3), channel_id=1, source_target_pairs={{0,8},{1,9},{2,10},{3,11},{4,12},{5,13},{6,14},{7,15},{8,0},{9,1},... | collective-permute-start | bytes 1769480 | tf_op jit(solution)/shard_map/ppermute | solution.py:681
  74.8 9.9 %attn_bwd.1 = (bf16[512,768]{1,0:T(8,128)(2,1)S(1)}, bf16[512,768]{1,0:T(8,128)(2,1)S(1)}, bf16[512,768]{1,0:T(8,128)(2,1)S(1)}) custom-call(s32[6]{0:T(128)S(1)} %stack.24.s, bf16[512,768]{1,0:T(8,128)(2,1)S(1)} %get-tuple-element.153.ml, bf16[768,768]{1,0:T(8,128)(2,1)} %wm.3, bf16[512,768]{1,0:T(8,128)(2,1)S(1)} %get-tuple-element.154.q, ...), custom_call_target="tpu_custom_call" | custom-call | flops 3600000 | bytes 15728 | tf_op jit(solution)/shard_map/attn_bwd/pallas_call | solution.py:375
  84.7 2.1 %collective-permute-done.7 = bf16[2,2,192,384]{3,2,1,0:T(8,128)(2,1)S(1)} collective-permute-done((bf16[2,2,192,384]{3,2,1,0:T(8,128)(2,1)S(1)}, bf16[2,2,192,384]{3,2,1,0:T(8,128)(2,1)S(1)}, u32[]{:S(2)}, u32[]{:S(2)}) %collective-permute-start.7) | collective-permute-done | bytes 589856 | tf_op jit(solution)/shard_map/ppermute | solution.py:681
  88.8 1.4 collective-permute-start.10
  90.2 6.5 %weight_last.1 = (bf16[2,2,4,192,384]{4,3,2,1,0:T(8,128)(2,1)S(1)}, bf16[4,192,384]{2,1,0:T(8,128)(2,1)S(1)}, bf16[4,192,384]{2,1,0:T(8,128)(2,1)S(1)}, bf16[4,1...) custom-call(s32[6]{0:T(128)S(1)} %stack.24.s, bf16[2,256,768]{2,1,0:T(8,128)(2,1)} %own.3, ...), custom_call_target="tpu_custom_call" | custom-call | flops 2400000 | bytes 10485 | tf_op jit(solution)/shard_map/weight_last/pallas_call | solution.py:762
  97.4 2.3 %collective-permute-done.13.refs_18_ = f32[32,384]{1,0:T(8,128)S(1)} collective-permute-done((f32[32,384]{1,0:T(8,128)S(1)}, f32[32,384]{1,0:T(8,128)S(1)}, u32[]{:S(2)}, u32[]{:S(2)}) %collective-permute-start.13) | collective-permute-done | bytes 49184 | tf_op jit(solution)/shard_map/ppermute | solution.py:671
  102.0 1.6 %collective-permute-start.14 = (bf16[1568,384]{1,0:T(8,128)(2,1)S(1)}, bf16[1568,384]{1,0:T(8,128)(2,1)S(1)}, u32[]{:S(2)}, u32[]{:S(2)}) collective-permute-start(bf16[1568,384]{1,0:T(8,128)(2,1)S(1)} %get-tuple-element.186), channel_id=1, source_target_pairs={{0,4},{1,5},{2,3},{3,2},{4,0},{5,1},{6,7},{7,6},{8,12},{9,13},{10,... | collective-permute-start | bytes 3612680 | tf_op jit(solution)/shard_map/ppermute | solution.py:681
  104.0 1.6 %collective-permute-start.17 = (bf16[384,384]{1,0:T(8,128)(2,1)S(1)}, bf16[384,384]{1,0:T(8,128)(2,1)S(1)}, u32[]{:S(2)}, u32[]{:S(2)}) collective-permute-start(bf16[384,384]{1,0:T(8,128)(2,1)S(1)} %get-tuple-element.191), channel_id=1, source_target_pairs={{0,8},{1,9},{2,10},{3,11},{4,12},{5,13},{6,14},{7,15},{8,0},{9,1},... | collective-permute-start | bytes 884744 | tf_op jit(solution)/shard_map/ppermute | solution.py:681
  105.6 2.6 %collective-permute-start.18 = (bf16[192,384]{1,0:T(8,128)(2,1)S(1)}, bf16[192,384]{1,0:T(8,128)(2,1)S(1)}, u32[]{:S(2)}, u32[]{:S(2)}) collective-permute-start(bf16[192,384]{1,0:T(8,128)(2,1)S(1)} %get-tuple-element.192), channel_id=1, source_target_pairs={{0,16},{1,17},{2,18},{3,19},{4,20},{5,21},{6,22},{7,23},{8,24},{9,... | collective-permute-start | bytes 442376 | tf_op jit(solution)/shard_map/ppermute | solution.py:681
  108.2 5.4 %input_grad.1 = (f32[2,256,768]{2,1,0:T(8,128)}, bf16[256,768]{1,0:T(8,128)(2,1)S(1)}) custom-call(s32[6]{0:T(128)S(1)} %stack.24.s, bf16[512,768]{1,0:T(8,128)(2,1)S(1)} %get-tuple-element.167.dq, bf16[512,768]{1,0:T(8,128)(2,1)S(1)} %get-tuple-element.168.dk, bf16[512,768]{1,0:T(8,128)(2,1)S(1)} %get-tuple-element.169.dv, bf16[768,768]{1,0:T(8,128)(2,1)} %wq.3, ...), custom_call_target="tpu_custom_call" | custom-call | flops 1800000 | bytes 8388 | tf_op jit(solution)/shard_map/input_grad/pallas_call | solution.py:407
  113.6 1.6 %collective-permute-done.18 = bf16[192,384]{1,0:T(8,128)(2,1)S(1)} collective-permute-done((bf16[192,384]{1,0:T(8,128)(2,1)S(1)}, bf16[192,384]{1,0:T(8,128)(2,1)S(1)}, u32[]{:S(2)}, u32[]{:S(2)}) %collective-permute-start.18) | collective-permute-done | bytes 147488 | tf_op jit(solution)/shard_map/ppermute | solution.py:681
  116.1 2.4 %collective-permute-done.14.refs_1_.refs_9_.refs_2_.refs_6_ = bf16[1568,384]{1,0:T(8,128)(2,1)S(1)} collective-permute-done((bf16[1568,384]{1,0:T(8,128)(2,1)S(1)}, bf16[1568,384]{1,0:T(8,128)(2,1)S(1)}, u32[]{:S(2)}, u32[]{:S(2)}) %collective-permute-start.14) | collective-permute-done | bytes 1204256 | tf_op jit(solution)/shard_map/ppermute | solution.py:681
  120.2 2.6 %collective-permute-start.20 = (bf16[192,384]{1,0:T(8,128)(2,1)S(1)}, bf16[192,384]{1,0:T(8,128)(2,1)S(1)}, u32[]{:S(2)}, u32[]{:S(2)}) collective-permute-start(bf16[192,384]{1,0:T(8,128)(2,1)S(1)} %get-tuple-element.202), channel_id=1, source_target_pairs={{0,16},{1,17},{2,18},{3,19},{4,20},{5,21},{6,22},{7,23},{8,24},{9,... | collective-permute-start | bytes 442376 | tf_op jit(solution)/shard_map/ppermute | solution.py:681
  124.9 3.7 %collective-permute-done.20.refs_5_ = bf16[192,384]{1,0:T(8,128)(2,1)S(1)} collective-permute-done((bf16[192,384]{1,0:T(8,128)(2,1)S(1)}, bf16[192,384]{1,0:T(8,128)(2,1)S(1)}, u32[]{:S(2)}, u32[]{:S(2)}) %collective-permute-start.20) | collective-permute-done | bytes 147488 | tf_op jit(solution)/shard_map/ppermute | solution.py:681
  130.3 1.6 %collective-permute-start.21 = (bf16[416,384]{1,0:T(8,128)(2,1)S(1)}, bf16[416,384]{1,0:T(8,128)(2,1)S(1)}, u32[]{:S(2)}, u32[]{:S(2)}) collective-permute-start(bf16[416,384]{1,0:T(8,128)(2,1)S(1)} %get-tuple-element.209), channel_id=1, source_target_pairs={{0,8},{1,9},{2,10},{3,11},{4,12},{5,13},{6,14},{7,15},{8,0},{9,1},... | collective-permute-start | bytes 958472 | tf_op jit(solution)/shard_map/ppermute | solution.py:681
  134.0 3.8 %collective-permute-done.21.refs_4_.refs_6_ = bf16[416,384]{1,0:T(8,128)(2,1)S(1)} collective-permute-done((bf16[416,384]{1,0:T(8,128)(2,1)S(1)}, bf16[416,384]{1,0:T(8,128)(2,1)S(1)}, u32[]{:S(2)}, u32[]{:S(2)}) %collective-permute-start.21) | collective-permute-done | bytes 319520 | tf_op jit(solution)/shard_map/ppermute | solution.py:681
  138.4 2.6 %collective-permute-start.22 = (bf16[224,384]{1,0:T(8,128)(2,1)S(1)}, bf16[224,384]{1,0:T(8,128)(2,1)S(1)}, u32[]{:S(2)}, u32[]{:S(2)}) collective-permute-start(bf16[224,384]{1,0:T(8,128)(2,1)S(1)} %get-tuple-element.211), channel_id=1, source_target_pairs={{0,16},{1,17},{2,18},{3,19},{4,20},{5,21},{6,22},{7,23},{8,24},{9,... | collective-permute-start | bytes 516104 | tf_op jit(solution)/shard_map/ppermute | solution.py:681
  142.1 1.5 finish.4
  143.6 1.4 total_inner.1
  146.7 1.3 combine.9
  (48 shorter events, 22.3 us)
Async XLA Ops:
  0.7 5.2 %copy-start = (s32[2]{0:T(128)S(1)}, s32[2]{0:T(128)}, u32[]{:S(2)}) copy-start(s32[2]{0:T(128)} %param.20) | copy-start | bytes 28
  1.7 13.0 %collective-permute-start = (bf16[256,768]{1,0:T(8,128)(2,1)S(1)}, bf16[256,768]{1,0:T(8,128)(2,1)S(1)}, u32[]{:S(2)}, u32[]{:S(2)}) collective-permute-start(bf16[256,768]{1,0:T(8,128)(2,1)S(1)} %dynamic-slice_bitcast_fusion.1), channel_id=1, source_target_pairs={{0,1},{1,0},{2,3},{3,2},{4,5},{5,4},{6,7},{7,6},{8,9},{9,8},{10,11... | collective-permute-start | bytes 1179656 | tf_op jit(solution)/shard_map/ppermute | solution.py:670
  5.8 22.4 %collective-permute-start.1 = (bf16[256,768]{1,0:T(8,128)(2,1)S(1)}, bf16[256,768]{1,0:T(8,128)(2,1)S(1)}, u32[]{:S(2)}, u32[]{:S(2)}) collective-permute-start(bf16[256,768]{1,0:T(8,128)(2,1)S(1)} %dynamic-slice_bitcast_fusion), channel_id=1, source_target_pairs={{0,1},{1,0},{2,3},{3,2},{4,5},{5,4},{6,7},{7,6},{8,9},{9,8},{10,11... | collective-permute-start | bytes 1179656 | tf_op jit(solution)/shard_map/ppermute | solution.py:670
  41.7 7.1 %collective-permute-start.2 = (bf16[128,768]{1,0:T(8,128)(2,1)S(1)}, bf16[128,768]{1,0:T(8,128)(2,1)S(1)}, u32[]{:S(2)}, u32[]{:S(2)}) collective-permute-start(bf16[128,768]{1,0:T(8,128)(2,1)S(1)} %get-tuple-element.135), channel_id=1, source_target_pairs={{0,1},{1,0},{2,3},{3,2},{4,5},{5,4},{6,7},{7,6},{8,9},{9,8},{10,11... | collective-permute-start | bytes 589832 | tf_op jit(solution)/shard_map/ppermute | solution.py:670
  48.8 5.5 %collective-permute-start.3 = (bf16[2,2,2,2,192,384]{5,4,3,2,1,0:T(8,128)(2,1)S(1)}, bf16[2,2,2,2,192,384]{5,4,3,2,1,0:T(8,128)(2,1)S(1)}, u32[]{:S(2)}, u32[]{:S(2)}) collective-permute-start(bf16[2,2,2,2,192,384]{5,4,3,2,1,0:T(8,128)(2,1)S(1)} %get-tuple-element.136), channel_id=1, source_target_pairs={{0,2},{2,0},{4,6},{6,4},{8,10},{10,8},{12,14},{14,12},{16,18},{18,... | collective-permute-start | bytes 7077896 | tf_op jit(solution)/shard_map/ppermute | solution.py:671
  54.7 16.3 %collective-permute-start.4 = (bf16[2,2,2,192,384]{4,3,2,1,0:T(8,128)(2,1)S(1)}, bf16[2,2,2,192,384]{4,3,2,1,0:T(8,128)(2,1)S(1)}, u32[]{:S(2)}, u32[]{:S(2)}) collective-permute-start(bf16[2,2,2,192,384]{4,3,2,1,0:T(8,128)(2,1)S(1)} %fusion.1), channel_id=1, source_target_pairs={{0,4},{1,5},{2,3},{3,2},{4,0},{5,1},{6,7},{7,6},{8,12},{9,13},{10,... | collective-permute-start | bytes 3538952 | tf_op jit(solution)/shard_map/ppermute | solution.py:681
  61.7 9.3 %collective-permute-start.5 = (bf16[2,4,192,384]{3,2,1,0:T(8,128)(2,1)S(1)}, bf16[2,4,192,384]{3,2,1,0:T(8,128)(2,1)S(1)}, u32[]{:S(2)}, u32[]{:S(2)}) collective-permute-start(bf16[2,4,192,384]{3,2,1,0:T(8,128)(2,1)S(1)} %get-tuple-element.143), channel_id=1, source_target_pairs={{0,2},{2,0},{4,6},{6,4},{8,10},{10,8},{12,14},{14,12},{16,18},{18,... | collective-permute-start | bytes 3538952 | tf_op jit(solution)/shard_map/ppermute | solution.py:671
  61.8 9.2 %collective-permute-start.6 = (bf16[2,4,192,384]{3,2,1,0:T(8,128)(2,1)S(1)}, bf16[2,4,192,384]{3,2,1,0:T(8,128)(2,1)S(1)}, u32[]{:S(2)}, u32[]{:S(2)}) collective-permute-start(bf16[2,4,192,384]{3,2,1,0:T(8,128)(2,1)S(1)} %get-tuple-element.144), channel_id=1, source_target_pairs={{0,2},{2,0},{4,6},{6,4},{8,10},{10,8},{12,14},{14,12},{16,18},{18,... | collective-permute-start | bytes 3538952 | tf_op jit(solution)/shard_map/ppermute | solution.py:671
  71.3 16.3 %collective-permute-start.8 = (bf16[2,4,192,384]{3,2,1,0:T(8,128)(2,1)S(1)}, bf16[2,4,192,384]{3,2,1,0:T(8,128)(2,1)S(1)}, u32[]{:S(2)}, u32[]{:S(2)}) collective-permute-start(bf16[2,4,192,384]{3,2,1,0:T(8,128)(2,1)S(1)} %fusion), channel_id=1, source_target_pairs={{0,4},{1,5},{2,3},{3,2},{4,0},{5,1},{6,7},{7,6},{8,12},{9,13},{10,... | collective-permute-start | bytes 3538952 | tf_op jit(solution)/shard_map/ppermute | solution.py:681
  73.1 13.7 %collective-permute-start.7 = (bf16[2,2,192,384]{3,2,1,0:T(8,128)(2,1)S(1)}, bf16[2,2,192,384]{3,2,1,0:T(8,128)(2,1)S(1)}, u32[]{:S(2)}, u32[]{:S(2)}) collective-permute-start(bf16[2,2,192,384]{3,2,1,0:T(8,128)(2,1)S(1)} %fusion.3), channel_id=1, source_target_pairs={{0,8},{1,9},{2,10},{3,11},{4,12},{5,13},{6,14},{7,15},{8,0},{9,1},... | collective-permute-start | bytes 1769480 | tf_op jit(solution)/shard_map/ppermute | solution.py:681
  87.8 8.9 %collective-permute-start.9 = (bf16[2,192,384]{2,1,0:T(8,128)(2,1)S(1)}, bf16[2,192,384]{2,1,0:T(8,128)(2,1)S(1)}, u32[]{:S(2)}, u32[]{:S(2)}) collective-permute-start(bf16[2,192,384]{2,1,0:T(8,128)(2,1)S(1)} %fusion.4), channel_id=1, source_target_pairs={{0,1},{1,0},{2,6},{3,7},{4,5},{5,4},{6,2},{7,3},{8,9},{9,8},{10,14... | collective-permute-start | bytes 884744 | tf_op jit(solution)/shard_map/ppermute | solution.py:681
  88.8 12.1 %collective-permute-start.10 = (bf16[4,192,384]{2,1,0:T(8,128)(2,1)S(1)}, bf16[4,192,384]{2,1,0:T(8,128)(2,1)S(1)}, u32[]{:S(2)}, u32[]{:S(2)}) collective-permute-start(bf16[4,192,384]{2,1,0:T(8,128)(2,1)S(1)} %fusion.2), channel_id=1, source_target_pairs={{0,1},{1,0},{2,6},{3,7},{4,5},{5,4},{6,2},{7,3},{8,9},{9,8},{10,14... | collective-permute-start | bytes 1769480 | tf_op jit(solution)/shard_map/ppermute | solution.py:681
  96.7 4.2 %collective-permute-start.11 = (bf16[4,192,384]{2,1,0:T(8,128)(2,1)S(1)}, bf16[4,192,384]{2,1,0:T(8,128)(2,1)S(1)}, u32[]{:S(2)}, u32[]{:S(2)}) collective-permute-start(bf16[4,192,384]{2,1,0:T(8,128)(2,1)S(1)} %get-tuple-element.178), channel_id=1, source_target_pairs={{0,2},{2,0},{4,6},{6,4},{8,10},{10,8},{12,14},{14,12},{16,18},{18,... | collective-permute-start | bytes 1769480 | tf_op jit(solution)/shard_map/ppermute | solution.py:671
  96.8 4.1 %collective-permute-start.12 = (bf16[4,192,384]{2,1,0:T(8,128)(2,1)S(1)}, bf16[4,192,384]{2,1,0:T(8,128)(2,1)S(1)}, u32[]{:S(2)}, u32[]{:S(2)}) collective-permute-start(bf16[4,192,384]{2,1,0:T(8,128)(2,1)S(1)} %get-tuple-element.179), channel_id=1, source_target_pairs={{0,2},{2,0},{4,6},{6,4},{8,10},{10,8},{12,14},{14,12},{16,18},{18,... | collective-permute-start | bytes 1769480 | tf_op jit(solution)/shard_map/ppermute | solution.py:671
  97.3 2.4 %collective-permute-start.13 = (f32[32,384]{1,0:T(8,128)S(1)}, f32[32,384]{1,0:T(8,128)S(1)}, u32[]{:S(2)}, u32[]{:S(2)}) collective-permute-start(f32[32,384]{1,0:T(8,128)S(1)} %get-tuple-element.180.refs_17_), channel_id=1, source_target_pairs={{0,2},{2,0},{4,6},{6,4},{8,10},{10,8},{12,14},{14,12},{16,18},{18,... | collective-permute-start | bytes 147464 | tf_op jit(solution)/shard_map/ppermute | solution.py:671
  102.0 16.5 %collective-permute-start.14 = (bf16[1568,384]{1,0:T(8,128)(2,1)S(1)}, bf16[1568,384]{1,0:T(8,128)(2,1)S(1)}, u32[]{:S(2)}, u32[]{:S(2)}) collective-permute-start(bf16[1568,384]{1,0:T(8,128)(2,1)S(1)} %get-tuple-element.186), channel_id=1, source_target_pairs={{0,4},{1,5},{2,3},{3,2},{4,0},{5,1},{6,7},{7,6},{8,12},{9,13},{10,... | collective-permute-start | bytes 3612680 | tf_op jit(solution)/shard_map/ppermute | solution.py:681
  103.5 12.6 %collective-permute-start.15 = (bf16[4,192,384]{2,1,0:T(8,128)(2,1)S(1)}, bf16[4,192,384]{2,1,0:T(8,128)(2,1)S(1)}, u32[]{:S(2)}, u32[]{:S(2)}) collective-permute-start(bf16[4,192,384]{2,1,0:T(8,128)(2,1)S(1)} %get-tuple-element.188), channel_id=1, source_target_pairs={{0,2},{2,0},{4,6},{6,4},{8,10},{10,8},{12,14},{14,12},{16,18},{18,... | collective-permute-start | bytes 1769480 | tf_op jit(solution)/shard_map/ppermute | solution.py:671
  103.5 12.6 %collective-permute-start.16 = (bf16[4,192,384]{2,1,0:T(8,128)(2,1)S(1)}, bf16[4,192,384]{2,1,0:T(8,128)(2,1)S(1)}, u32[]{:S(2)}, u32[]{:S(2)}) collective-permute-start(bf16[4,192,384]{2,1,0:T(8,128)(2,1)S(1)} %get-tuple-element.190), channel_id=1, source_target_pairs={{0,2},{2,0},{4,6},{6,4},{8,10},{10,8},{12,14},{14,12},{16,18},{18,... | collective-permute-start | bytes 1769480 | tf_op jit(solution)/shard_map/ppermute | solution.py:671
  104.0 12.1 %collective-permute-start.17 = (bf16[384,384]{1,0:T(8,128)(2,1)S(1)}, bf16[384,384]{1,0:T(8,128)(2,1)S(1)}, u32[]{:S(2)}, u32[]{:S(2)}) collective-permute-start(bf16[384,384]{1,0:T(8,128)(2,1)S(1)} %get-tuple-element.191), channel_id=1, source_target_pairs={{0,8},{1,9},{2,10},{3,11},{4,12},{5,13},{6,14},{7,15},{8,0},{9,1},... | collective-permute-start | bytes 884744 | tf_op jit(solution)/shard_map/ppermute | solution.py:681
  105.6 9.6 %collective-permute-start.18 = (bf16[192,384]{1,0:T(8,128)(2,1)S(1)}, bf16[192,384]{1,0:T(8,128)(2,1)S(1)}, u32[]{:S(2)}, u32[]{:S(2)}) collective-permute-start(bf16[192,384]{1,0:T(8,128)(2,1)S(1)} %get-tuple-element.192), channel_id=1, source_target_pairs={{0,16},{1,17},{2,18},{3,19},{4,20},{5,21},{6,22},{7,23},{8,24},{9,... | collective-permute-start | bytes 442376 | tf_op jit(solution)/shard_map/ppermute | solution.py:681
  119.4 10.2 %collective-permute-start.19 = (bf16[800,384]{1,0:T(8,128)(2,1)S(1)}, bf16[800,384]{1,0:T(8,128)(2,1)S(1)}, u32[]{:S(2)}, u32[]{:S(2)}) collective-permute-start(bf16[800,384]{1,0:T(8,128)(2,1)S(1)} %get-tuple-element.201), channel_id=1, source_target_pairs={{0,1},{1,0},{2,6},{3,7},{4,5},{5,4},{6,2},{7,3},{8,9},{9,8},{10,14... | collective-permute-start | bytes 1843208 | tf_op jit(solution)/shard_map/ppermute | solution.py:681
  120.2 8.4 %collective-permute-start.20 = (bf16[192,384]{1,0:T(8,128)(2,1)S(1)}, bf16[192,384]{1,0:T(8,128)(2,1)S(1)}, u32[]{:S(2)}, u32[]{:S(2)}) collective-permute-start(bf16[192,384]{1,0:T(8,128)(2,1)S(1)} %get-tuple-element.202), channel_id=1, source_target_pairs={{0,16},{1,17},{2,18},{3,19},{4,20},{5,21},{6,22},{7,23},{8,24},{9,... | collective-permute-start | bytes 442376 | tf_op jit(solution)/shard_map/ppermute | solution.py:681
  130.3 7.5 %collective-permute-start.21 = (bf16[416,384]{1,0:T(8,128)(2,1)S(1)}, bf16[416,384]{1,0:T(8,128)(2,1)S(1)}, u32[]{:S(2)}, u32[]{:S(2)}) collective-permute-start(bf16[416,384]{1,0:T(8,128)(2,1)S(1)} %get-tuple-element.209), channel_id=1, source_target_pairs={{0,8},{1,9},{2,10},{3,11},{4,12},{5,13},{6,14},{7,15},{8,0},{9,1},... | collective-permute-start | bytes 958472 | tf_op jit(solution)/shard_map/ppermute | solution.py:681
  131.9 10.2 %collective-permute-start.23 = (bf16[256,768]{1,0:T(8,128)(2,1)S(1)}, bf16[256,768]{1,0:T(8,128)(2,1)S(1)}, u32[]{:S(2)}, u32[]{:S(2)}) collective-permute-start(bf16[256,768]{1,0:T(8,128)(2,1)S(1)} %get-tuple-element.214), channel_id=1, source_target_pairs={{0,1},{1,0},{2,3},{3,2},{4,5},{5,4},{6,7},{7,6},{8,9},{9,8},{10,11... | collective-permute-start | bytes 1179656 | tf_op jit(solution)/shard_map/ppermute | solution.py:670
  132.7 12.3 %collective-permute-start.24 = (bf16[128,768]{1,0:T(8,128)(2,1)S(1)}, bf16[128,768]{1,0:T(8,128)(2,1)S(1)}, u32[]{:S(2)}, u32[]{:S(2)}) collective-permute-start(bf16[128,768]{1,0:T(8,128)(2,1)S(1)} %get-tuple-element.220), channel_id=1, source_target_pairs={{0,1},{1,0},{2,3},{3,2},{4,5},{5,4},{6,7},{7,6},{8,9},{9,8},{10,11... | collective-permute-start | bytes 589832 | tf_op jit(solution)/shard_map/ppermute | solution.py:670
  138.4 8.2 %collective-permute-start.22 = (bf16[224,384]{1,0:T(8,128)(2,1)S(1)}, bf16[224,384]{1,0:T(8,128)(2,1)S(1)}, u32[]{:S(2)}, u32[]{:S(2)}) collective-permute-start(bf16[224,384]{1,0:T(8,128)(2,1)S(1)} %get-tuple-element.211), channel_id=1, source_target_pairs={{0,16},{1,17},{2,18},{3,19},{4,20},{5,21},{6,22},{7,23},{8,24},{9,... | collective-permute-start | bytes 516104 | tf_op jit(solution)/shard_map/ppermute | solution.py:681

commit v6 on v5

--- a/solution.py
+++ b/solution.py
@@ -78,7 +78,7 @@
 
 
 def attn_fwd_body(s, own, rem, wq, wk, wv, bq, bv, wm, mb, g1, b1,
-                  q_o, kt_o, v_o, e_o, il_o, ctx_o, n1_o, rs_o, nl_o, xs, mask, acc):
+                  q_o, kt_o, v_o, e_o, il_o, ctx_o, n1_o, rs_o, nl_o, xs, mask, cs, acc):
     g = pl.program_id(0)
     half = own.shape[1]
     length = 2 * half
@@ -115,18 +115,11 @@
         outs.append(nn(vt[h * 64 : h * 64 + 64], low) * il)
     ctx = jnp.concatenate(outs, 0).astype(BF).T
     ctx_o[...] = ctx
-    part = nn(ctx, wm[...])
-
-    @pl.when(g == 0)
-    def _():
-        acc[...] = part
-
-    @pl.when(g > 0)
-    def _():
-        acc[...] += part
+    cs[:, pl.ds(pl.multiple_of(g * 256, 256), 256)] = ctx
 
     @pl.when(g == pl.num_programs(0) - 1)
     def _():
+        acc[...] = nn(cs[...], wm[...])
         for i in range(4):
             at = pl.ds(i * 128, 128)
             r = acc[at] + lane(mb) + xs[at].astype(F32)
@@ -147,7 +140,7 @@
         [own_slot(half, d), full((half, d))]
         + [cols(d, 256)] * 3
         + [vec(256)] * 2
-        + [rows_of(256, d)]
+        + [full((d, d))]
         + [whole_vec(d)] * 3,
         [
             cols(t, 256),
@@ -171,7 +164,7 @@
             shape((t, 1), F32),
             shape((t, d), BF),
         ],
-        [pltpu.VMEM((t, d), BF), pltpu.VMEM((t, 128), F32), pltpu.VMEM((t, d), F32)],
+        [pltpu.VMEM((t, d), BF), pltpu.VMEM((t, 128), F32), pltpu.VMEM((t, d), BF), pltpu.VMEM((t, d), F32)],
         "attn_fwd",
         3_200_000_000,
         18 << 20,

time: 148 us -> 148 us (level)
  no operation moved by 1% of the time
where the time goes in v6:
time: 148 us; the launch traced here: 147 us
  Pallas kernels  81 us (55%)
  waiting for transfers between devices  30.6 us (21%)
  starting transfers between devices  29.2 us (20%)
  local copies, waits for them, and re-layouts  3.37 us (2%)
  other arithmetic  2.11 us (1%)
    ppermute x12, starting transfers between devices, trade_stage(): return lax.ppermute(value, ('dp', 'seq'), pairs)  20.2 us
    ppermute x12, waiting for transfers between devices, trade_stage(): return lax.ppermute(value, ('dp', 'seq'), pairs)  19.7 us
    pallas_call x1, Pallas kernels, mlp_fwd(): call(mlp_fwd_body, (ff // w,), [full((t, d)), cols(d, w), vec(w), rows_of...  13.5 us
    pallas_call x1, Pallas kernels, attn_fwd(): call(attn_fwd_body, (d // 256,), [own_slot(half, d), full((half, d))] + [...  12.7 us
    pallas_call x1, Pallas kernels, attn_bwd(): call(attn_bwd_body, (d // 256,), [full((t, d)), rows_of(256, d), cols(t,...  9.94 us
    ppermute x5, waiting for transfers between devices, trade(): return lax.ppermute(value, 'seq', [(0, 1), (1, 0)])  8.58 us
    ppermute x5, starting transfers between devices, trade(): return lax.ppermute(value, 'seq', [(0, 1), (1, 0)])  7.2 us
    pallas_call x1, Pallas kernels, slope_first(): call(slope_first_body, (ff // w,), [cols(t, w), cols(d, w), full((t, d)),...  6.97 us
  transfers between devices with their start and end apart: 25, of which 14 were waited for; matrix products, arithmetic and copies ran while one was open for 2% of the time, Pallas kernels for 43%

profile of v6, /device:TPU:0, one launch (start us, length us, event | category | flops | bytes accessed | tf_op | source)
XLA Modules:
  0.0 147.4 jit_solution(18366261761571339461)
XLA Ops:
  1.7 3.1 %collective-permute-start = (bf16[256,768]{1,0:T(8,128)(2,1)S(1)}, bf16[256,768]{1,0:T(8,128)(2,1)S(1)}, u32[]{:S(2)}, u32[]{:S(2)}) collective-permute-start(bf16[256,768]{1,0:T(8,128)(2,1)S(1)} %dynamic-slice_bitcast_fusion.1), channel_id=1, source_target_pairs={{0,1},{1,0},{2,3},{3,2},{4,5},{5,4},{6,7},{7,6},{8,9},{9,8},{10,11... | collective-permute-start | bytes 1179656 | tf_op jit(solution)/shard_map/ppermute | solution.py:663
  7.2 7.5 %collective-permute-done.rem = bf16[256,768]{1,0:T(8,128)(2,1)S(1)} collective-permute-done((bf16[256,768]{1,0:T(8,128)(2,1)S(1)}, bf16[256,768]{1,0:T(8,128)(2,1)S(1)}, u32[]{:S(2)}, u32[]{:S(2)}) %collective-permute-start) | collective-permute-done | bytes 393248 | tf_op jit(solution)/shard_map/ppermute | solution.py:663
  14.7 12.7 %attn_fwd.1 = (bf16[512,768]{1,0:T(8,128)(2,1)S(1)}, bf16[768,512]{1,0:T(8,128)(2,1)S(1)}, bf16[512,768]{1,0:T(8,128)(2,1)S(1)}, bf16[12,512,512]{2,1,0:T(8,128)...) custom-call(s32[6]{0:T(128)S(1)} %stack.24.s, ...), custom_call_target="tpu_custom_call" | custom-call | flops 3200000 | bytes 18874 | tf_op jit(solution)/shard_map/attn_fwd/pallas_call | solution.py:137
  27.4 13.5 %mlp_fwd.1 = (bf16[512,3072]{1,0:T(8,128)(2,1)S(1)}, bf16[512,3072]{1,0:T(8,128)(2,1)S(1)}, f32[2,256,768]{2,1,0:T(8,128)}, bf16[128,768]{1,0:T(8,128)(2,1)S(1)}...) custom-call(s32[6]{0:T(128)S(1)} %stack.24.s, ...), custom_call_target="tpu_custom_call" | custom-call | flops 4800000 | bytes 25165 | tf_op jit(solution)/shard_map/mlp_fwd/pallas_call | solution.py:239
  40.9 2.0 %collective-permute-start.2 = (bf16[128,768]{1,0:T(8,128)(2,1)S(1)}, bf16[128,768]{1,0:T(8,128)(2,1)S(1)}, u32[]{:S(2)}, u32[]{:S(2)}) collective-permute-start(bf16[128,768]{1,0:T(8,128)(2,1)S(1)} %get-tuple-element.135), channel_id=1, source_target_pairs={{0,1},{1,0},{2,3},{3,2},{4,5},{5,4},{6,7},{7,6},{8,9},{9,8},{10,11... | collective-permute-start | bytes 589832 | tf_op jit(solution)/shard_map/ppermute | solution.py:663
  42.9 5.1 %weight_outer.1 = (bf16[2,2,2,2,192,384]{5,4,3,2,1,0:T(8,128)(2,1)S(1)}, bf16[2,2,2,2,192,384]{5,4,3,2,1,0:T(8,128)(2,1)S(1)}) custom-call(s32[6]{0:T(128)S(1)} %stack.24.s, bf16[512,3072]{1,0:T(8,128)(2,1)S(1)} %get-tuple-element.131.act, bf16[512,768]{1,0:T(8,128)(2,1)S(1)} %get-tuple-element.132.sl), custom_call_target="tpu_custom_call" | custom-call | flops 2400000 | bytes 10485 | tf_op jit(solution)/shard_map/weight_outer/pallas_call | solution.py:725
  48.1 5.5 %slope_inner.1 = (bf16[512,3072]{1,0:T(8,128)(2,1)S(1)}, f32[1,3072]{1,0:T(1,128)S(1)}) custom-call(s32[6]{0:T(128)S(1)} %stack.24.s, bf16[512,768]{1,0:T(8,128)(2,1)S(1)} %get-tuple-element.132.sl, bf16[3072,768]{1,0:T(8,128)(2,1)} %wo.3, bf16[512,3072]{1,0:T(8,128)(2,1)S(1)} %get-tuple-element.138.dg), custom_call_target="tpu_custom_call" | custom-call | flops 2400000 | bytes 12582 | tf_op jit(solution)/shard_map/slope_inner/pallas_call | solution.py:275
  53.9 1.6 %collective-permute-start.4 = (bf16[2,2,2,192,384]{4,3,2,1,0:T(8,128)(2,1)S(1)}, bf16[2,2,2,192,384]{4,3,2,1,0:T(8,128)(2,1)S(1)}, u32[]{:S(2)}, u32[]{:S(2)}) collective-permute-start(bf16[2,2,2,192,384]{4,3,2,1,0:T(8,128)(2,1)S(1)} %fusion.1), channel_id=1, source_target_pairs={{0,4},{1,5},{2,3},{3,2},{4,0},{5,1},{6,7},{7,6},{8,12},{9,13},{10,... | collective-permute-start | bytes 3538952 | tf_op jit(solution)/shard_map/ppermute | solution.py:674
  55.5 5.4 %weight_inner.1 = (bf16[2,2,4,192,384]{4,3,2,1,0:T(8,128)(2,1)S(1)}, bf16[2,4,192,384]{3,2,1,0:T(8,128)(2,1)S(1)}, bf16[2,4,192,384]{3,2,1,0:T(8,128)(2,1)S(1)}) custom-call(s32[6]{0:T(128)S(1)} %stack.24.s, bf16[512,768]{1,0:T(8,128)(2,1)S(1)} %get-tuple-element.129.nl, bf16[512,3072]{1,0:T(8,128)(2,1)S(1)} %get-tuple-element.142.si0.si1.si, ...), custom_call_target="tpu_custom_call" | custom-call | flops 2400000 | bytes 10485 | tf_op jit(solution)/shard_map/weight_inner/pallas_call | solution.py:734
  61.4 7.0 %slope_first.1 = (f32[512,768]{1,0:T(8,128)S(1)}, bf16[512,768]{1,0:T(8,128)(2,1)S(1)}, f32[3,768]{1,0:T(4,128)S(1)}) custom-call(s32[6]{0:T(128)S(1)} %stack.24.s, bf16[512,3072]{1,0:T(8,128)(2,1)S(1)} %get-tuple-element.142.si0.si1.si, bf16[768,3072]{1,0:T(8,128)(2,1)} %wi.3, f32[512,768]{1,0:T(8,128)S(1)} %get-tuple-element.146.ss, ...), custom_call_target="tpu_custom_call" | custom-call | flops 2400000 | bytes 14680 | tf_op jit(solution)/shard_map/slope_first/pallas_call | solution.py:324
  68.4 1.8 %collective-permute-done.4 = bf16[2,2,2,192,384]{4,3,2,1,0:T(8,128)(2,1)S(1)} collective-permute-done((bf16[2,2,2,192,384]{4,3,2,1,0:T(8,128)(2,1)S(1)}, bf16[2,2,2,192,384]{4,3,2,1,0:T(8,128)(2,1)S(1)}, u32[]{:S(2)}, u32[]{:S(2)}) %collective-permute-start.4) | collective-permute-done | bytes 1179680 | tf_op jit(solution)/shard_map/ppermute | solution.py:674
  70.5 1.6 %collective-permute-start.8 = (bf16[2,4,192,384]{3,2,1,0:T(8,128)(2,1)S(1)}, bf16[2,4,192,384]{3,2,1,0:T(8,128)(2,1)S(1)}, u32[]{:S(2)}, u32[]{:S(2)}) collective-permute-start(bf16[2,4,192,384]{3,2,1,0:T(8,128)(2,1)S(1)} %fusion), channel_id=1, source_target_pairs={{0,4},{1,5},{2,3},{3,2},{4,0},{5,1},{6,7},{7,6},{8,12},{9,13},{10,... | collective-permute-start | bytes 3538952 | tf_op jit(solution)/shard_map/ppermute | solution.py:674
  72.3 1.6 %collective-permute-start.7 = (bf16[2,2,192,384]{3,2,1,0:T(8,128)(2,1)S(1)}, bf16[2,2,192,384]{3,2,1,0:T(8,128)(2,1)S(1)}, u32[]{:S(2)}, u32[]{:S(2)}) collective-permute-start(bf16[2,2,192,384]{3,2,1,0:T(8,128)(2,1)S(1)} %fusion.3), channel_id=1, source_target_pairs={{0,8},{1,9},{2,10},{3,11},{4,12},{5,13},{6,14},{7,15},{8,0},{9,1},... | collective-permute-start | bytes 1769480 | tf_op jit(solution)/shard_map/ppermute | solution.py:674
  74.0 9.9 %attn_bwd.1 = (bf16[512,768]{1,0:T(8,128)(2,1)S(1)}, bf16[512,768]{1,0:T(8,128)(2,1)S(1)}, bf16[512,768]{1,0:T(8,128)(2,1)S(1)}) custom-call(s32[6]{0:T(128)S(1)} %stack.24.s, bf16[512,768]{1,0:T(8,128)(2,1)S(1)} %get-tuple-element.153.ml, bf16[768,768]{1,0:T(8,128)(2,1)} %wm.3, bf16[512,768]{1,0:T(8,128)(2,1)S(1)} %get-tuple-element.154.q, ...), custom_call_target="tpu_custom_call" | custom-call | flops 3600000 | bytes 15728 | tf_op jit(solution)/shard_map/attn_bwd/pallas_call | solution.py:368
  83.9 2.1 %collective-permute-done.7 = bf16[2,2,192,384]{3,2,1,0:T(8,128)(2,1)S(1)} collective-permute-done((bf16[2,2,192,384]{3,2,1,0:T(8,128)(2,1)S(1)}, bf16[2,2,192,384]{3,2,1,0:T(8,128)(2,1)S(1)}, u32[]{:S(2)}, u32[]{:S(2)}) %collective-permute-start.7) | collective-permute-done | bytes 589856 | tf_op jit(solution)/shard_map/ppermute | solution.py:674
  88.0 1.4 collective-permute-start.10
  89.4 6.5 %weight_last.1 = (bf16[2,2,4,192,384]{4,3,2,1,0:T(8,128)(2,1)S(1)}, bf16[4,192,384]{2,1,0:T(8,128)(2,1)S(1)}, bf16[4,192,384]{2,1,0:T(8,128)(2,1)S(1)}, bf16[4,1...) custom-call(s32[6]{0:T(128)S(1)} %stack.24.s, bf16[2,256,768]{2,1,0:T(8,128)(2,1)} %own.3, ...), custom_call_target="tpu_custom_call" | custom-call | flops 2400000 | bytes 10485 | tf_op jit(solution)/shard_map/weight_last/pallas_call | solution.py:755
  96.6 2.3 %collective-permute-done.13.refs_18_ = f32[32,384]{1,0:T(8,128)S(1)} collective-permute-done((f32[32,384]{1,0:T(8,128)S(1)}, f32[32,384]{1,0:T(8,128)S(1)}, u32[]{:S(2)}, u32[]{:S(2)}) %collective-permute-start.13) | collective-permute-done | bytes 49184 | tf_op jit(solution)/shard_map/ppermute | solution.py:664
  101.2 1.6 %collective-permute-start.14 = (bf16[1568,384]{1,0:T(8,128)(2,1)S(1)}, bf16[1568,384]{1,0:T(8,128)(2,1)S(1)}, u32[]{:S(2)}, u32[]{:S(2)}) collective-permute-start(bf16[1568,384]{1,0:T(8,128)(2,1)S(1)} %get-tuple-element.186), channel_id=1, source_target_pairs={{0,4},{1,5},{2,3},{3,2},{4,0},{5,1},{6,7},{7,6},{8,12},{9,13},{10,... | collective-permute-start | bytes 3612680 | tf_op jit(solution)/shard_map/ppermute | solution.py:674
  103.2 1.6 %collective-permute-start.17 = (bf16[384,384]{1,0:T(8,128)(2,1)S(1)}, bf16[384,384]{1,0:T(8,128)(2,1)S(1)}, u32[]{:S(2)}, u32[]{:S(2)}) collective-permute-start(bf16[384,384]{1,0:T(8,128)(2,1)S(1)} %get-tuple-element.191), channel_id=1, source_target_pairs={{0,8},{1,9},{2,10},{3,11},{4,12},{5,13},{6,14},{7,15},{8,0},{9,1},... | collective-permute-start | bytes 884744 | tf_op jit(solution)/shard_map/ppermute | solution.py:674
  104.8 2.6 %collective-permute-start.18 = (bf16[192,384]{1,0:T(8,128)(2,1)S(1)}, bf16[192,384]{1,0:T(8,128)(2,1)S(1)}, u32[]{:S(2)}, u32[]{:S(2)}) collective-permute-start(bf16[192,384]{1,0:T(8,128)(2,1)S(1)} %get-tuple-element.192), channel_id=1, source_target_pairs={{0,16},{1,17},{2,18},{3,19},{4,20},{5,21},{6,22},{7,23},{8,24},{9,... | collective-permute-start | bytes 442376 | tf_op jit(solution)/shard_map/ppermute | solution.py:674
  107.4 5.4 %input_grad.1 = (f32[2,256,768]{2,1,0:T(8,128)}, bf16[256,768]{1,0:T(8,128)(2,1)S(1)}) custom-call(s32[6]{0:T(128)S(1)} %stack.24.s, bf16[512,768]{1,0:T(8,128)(2,1)S(1)} %get-tuple-element.167.dq, bf16[512,768]{1,0:T(8,128)(2,1)S(1)} %get-tuple-element.168.dk, bf16[512,768]{1,0:T(8,128)(2,1)S(1)} %get-tuple-element.169.dv, bf16[768,768]{1,0:T(8,128)(2,1)} %wq.3, ...), custom_call_target="tpu_custom_call" | custom-call | flops 1800000 | bytes 8388 | tf_op jit(solution)/shard_map/input_grad/pallas_call | solution.py:400
  112.8 1.6 %collective-permute-done.18 = bf16[192,384]{1,0:T(8,128)(2,1)S(1)} collective-permute-done((bf16[192,384]{1,0:T(8,128)(2,1)S(1)}, bf16[192,384]{1,0:T(8,128)(2,1)S(1)}, u32[]{:S(2)}, u32[]{:S(2)}) %collective-permute-start.18) | collective-permute-done | bytes 147488 | tf_op jit(solution)/shard_map/ppermute | solution.py:674
  115.3 2.4 %collective-permute-done.14.refs_1_.refs_9_.refs_2_.refs_6_ = bf16[1568,384]{1,0:T(8,128)(2,1)S(1)} collective-permute-done((bf16[1568,384]{1,0:T(8,128)(2,1)S(1)}, bf16[1568,384]{1,0:T(8,128)(2,1)S(1)}, u32[]{:S(2)}, u32[]{:S(2)}) %collective-permute-start.14) | collective-permute-done | bytes 1204256 | tf_op jit(solution)/shard_map/ppermute | solution.py:674
  119.4 2.6 %collective-permute-start.20 = (bf16[192,384]{1,0:T(8,128)(2,1)S(1)}, bf16[192,384]{1,0:T(8,128)(2,1)S(1)}, u32[]{:S(2)}, u32[]{:S(2)}) collective-permute-start(bf16[192,384]{1,0:T(8,128)(2,1)S(1)} %get-tuple-element.202), channel_id=1, source_target_pairs={{0,16},{1,17},{2,18},{3,19},{4,20},{5,21},{6,22},{7,23},{8,24},{9,... | collective-permute-start | bytes 442376 | tf_op jit(solution)/shard_map/ppermute | solution.py:674
  124.1 3.7 %collective-permute-done.20.refs_5_ = bf16[192,384]{1,0:T(8,128)(2,1)S(1)} collective-permute-done((bf16[192,384]{1,0:T(8,128)(2,1)S(1)}, bf16[192,384]{1,0:T(8,128)(2,1)S(1)}, u32[]{:S(2)}, u32[]{:S(2)}) %collective-permute-start.20) | collective-permute-done | bytes 147488 | tf_op jit(solution)/shard_map/ppermute | solution.py:674
  129.5 1.6 %collective-permute-start.21 = (bf16[416,384]{1,0:T(8,128)(2,1)S(1)}, bf16[416,384]{1,0:T(8,128)(2,1)S(1)}, u32[]{:S(2)}, u32[]{:S(2)}) collective-permute-start(bf16[416,384]{1,0:T(8,128)(2,1)S(1)} %get-tuple-element.209), channel_id=1, source_target_pairs={{0,8},{1,9},{2,10},{3,11},{4,12},{5,13},{6,14},{7,15},{8,0},{9,1},... | collective-permute-start | bytes 958472 | tf_op jit(solution)/shard_map/ppermute | solution.py:674
  133.2 3.8 %collective-permute-done.21.refs_4_.refs_6_ = bf16[416,384]{1,0:T(8,128)(2,1)S(1)} collective-permute-done((bf16[416,384]{1,0:T(8,128)(2,1)S(1)}, bf16[416,384]{1,0:T(8,128)(2,1)S(1)}, u32[]{:S(2)}, u32[]{:S(2)}) %collective-permute-start.21) | collective-permute-done | bytes 319520 | tf_op jit(solution)/shard_map/ppermute | solution.py:674
  137.6 2.6 %collective-permute-start.22 = (bf16[224,384]{1,0:T(8,128)(2,1)S(1)}, bf16[224,384]{1,0:T(8,128)(2,1)S(1)}, u32[]{:S(2)}, u32[]{:S(2)}) collective-permute-start(bf16[224,384]{1,0:T(8,128)(2,1)S(1)} %get-tuple-element.211), channel_id=1, source_target_pairs={{0,16},{1,17},{2,18},{3,19},{4,20},{5,21},{6,22},{7,23},{8,24},{9,... | collective-permute-start | bytes 516104 | tf_op jit(solution)/shard_map/ppermute | solution.py:674
  141.3 1.5 finish.4
  142.8 1.4 total_inner.1
  145.9 1.3 combine.9
  (48 shorter events, 22.3 us)
Async XLA Ops:
  0.7 5.2 %copy-start = (s32[2]{0:T(128)S(1)}, s32[2]{0:T(128)}, u32[]{:S(2)}) copy-start(s32[2]{0:T(128)} %param.20) | copy-start | bytes 28
  1.7 13.0 %collective-permute-start = (bf16[256,768]{1,0:T(8,128)(2,1)S(1)}, bf16[256,768]{1,0:T(8,128)(2,1)S(1)}, u32[]{:S(2)}, u32[]{:S(2)}) collective-permute-start(bf16[256,768]{1,0:T(8,128)(2,1)S(1)} %dynamic-slice_bitcast_fusion.1), channel_id=1, source_target_pairs={{0,1},{1,0},{2,3},{3,2},{4,5},{5,4},{6,7},{7,6},{8,9},{9,8},{10,11... | collective-permute-start | bytes 1179656 | tf_op jit(solution)/shard_map/ppermute | solution.py:663
  5.8 21.6 %collective-permute-start.1 = (bf16[256,768]{1,0:T(8,128)(2,1)S(1)}, bf16[256,768]{1,0:T(8,128)(2,1)S(1)}, u32[]{:S(2)}, u32[]{:S(2)}) collective-permute-start(bf16[256,768]{1,0:T(8,128)(2,1)S(1)} %dynamic-slice_bitcast_fusion), channel_id=1, source_target_pairs={{0,1},{1,0},{2,3},{3,2},{4,5},{5,4},{6,7},{7,6},{8,9},{9,8},{10,11... | collective-permute-start | bytes 1179656 | tf_op jit(solution)/shard_map/ppermute | solution.py:663
  40.9 7.1 %collective-permute-start.2 = (bf16[128,768]{1,0:T(8,128)(2,1)S(1)}, bf16[128,768]{1,0:T(8,128)(2,1)S(1)}, u32[]{:S(2)}, u32[]{:S(2)}) collective-permute-start(bf16[128,768]{1,0:T(8,128)(2,1)S(1)} %get-tuple-element.135), channel_id=1, source_target_pairs={{0,1},{1,0},{2,3},{3,2},{4,5},{5,4},{6,7},{7,6},{8,9},{9,8},{10,11... | collective-permute-start | bytes 589832 | tf_op jit(solution)/shard_map/ppermute | solution.py:663
  48.0 5.5 %collective-permute-start.3 = (bf16[2,2,2,2,192,384]{5,4,3,2,1,0:T(8,128)(2,1)S(1)}, bf16[2,2,2,2,192,384]{5,4,3,2,1,0:T(8,128)(2,1)S(1)}, u32[]{:S(2)}, u32[]{:S(2)}) collective-permute-start(bf16[2,2,2,2,192,384]{5,4,3,2,1,0:T(8,128)(2,1)S(1)} %get-tuple-element.136), channel_id=1, source_target_pairs={{0,2},{2,0},{4,6},{6,4},{8,10},{10,8},{12,14},{14,12},{16,18},{18,... | collective-permute-start | bytes 7077896 | tf_op jit(solution)/shard_map/ppermute | solution.py:664
  53.9 16.3 %collective-permute-start.4 = (bf16[2,2,2,192,384]{4,3,2,1,0:T(8,128)(2,1)S(1)}, bf16[2,2,2,192,384]{4,3,2,1,0:T(8,128)(2,1)S(1)}, u32[]{:S(2)}, u32[]{:S(2)}) collective-permute-start(bf16[2,2,2,192,384]{4,3,2,1,0:T(8,128)(2,1)S(1)} %fusion.1), channel_id=1, source_target_pairs={{0,4},{1,5},{2,3},{3,2},{4,0},{5,1},{6,7},{7,6},{8,12},{9,13},{10,... | collective-permute-start | bytes 3538952 | tf_op jit(solution)/shard_map/ppermute | solution.py:674
  60.9 9.3 %collective-permute-start.5 = (bf16[2,4,192,384]{3,2,1,0:T(8,128)(2,1)S(1)}, bf16[2,4,192,384]{3,2,1,0:T(8,128)(2,1)S(1)}, u32[]{:S(2)}, u32[]{:S(2)}) collective-permute-start(bf16[2,4,192,384]{3,2,1,0:T(8,128)(2,1)S(1)} %get-tuple-element.143), channel_id=1, source_target_pairs={{0,2},{2,0},{4,6},{6,4},{8,10},{10,8},{12,14},{14,12},{16,18},{18,... | collective-permute-start | bytes 3538952 | tf_op jit(solution)/shard_map/ppermute | solution.py:664
  60.9 9.3 %collective-permute-start.6 = (bf16[2,4,192,384]{3,2,1,0:T(8,128)(2,1)S(1)}, bf16[2,4,192,384]{3,2,1,0:T(8,128)(2,1)S(1)}, u32[]{:S(2)}, u32[]{:S(2)}) collective-permute-start(bf16[2,4,192,384]{3,2,1,0:T(8,128)(2,1)S(1)} %get-tuple-element.144), channel_id=1, source_target_pairs={{0,2},{2,0},{4,6},{6,4},{8,10},{10,8},{12,14},{14,12},{16,18},{18,... | collective-permute-start | bytes 3538952 | tf_op jit(solution)/shard_map/ppermute | solution.py:664
  70.5 16.3 %collective-permute-start.8 = (bf16[2,4,192,384]{3,2,1,0:T(8,128)(2,1)S(1)}, bf16[2,4,192,384]{3,2,1,0:T(8,128)(2,1)S(1)}, u32[]{:S(2)}, u32[]{:S(2)}) collective-permute-start(bf16[2,4,192,384]{3,2,1,0:T(8,128)(2,1)S(1)} %fusion), channel_id=1, source_target_pairs={{0,4},{1,5},{2,3},{3,2},{4,0},{5,1},{6,7},{7,6},{8,12},{9,13},{10,... | collective-permute-start | bytes 3538952 | tf_op jit(solution)/shard_map/ppermute | solution.py:674
  72.3 13.7 %collective-permute-start.7 = (bf16[2,2,192,384]{3,2,1,0:T(8,128)(2,1)S(1)}, bf16[2,2,192,384]{3,2,1,0:T(8,128)(2,1)S(1)}, u32[]{:S(2)}, u32[]{:S(2)}) collective-permute-start(bf16[2,2,192,384]{3,2,1,0:T(8,128)(2,1)S(1)} %fusion.3), channel_id=1, source_target_pairs={{0,8},{1,9},{2,10},{3,11},{4,12},{5,13},{6,14},{7,15},{8,0},{9,1},... | collective-permute-start | bytes 1769480 | tf_op jit(solution)/shard_map/ppermute | solution.py:674
  87.0 8.9 %collective-permute-start.9 = (bf16[2,192,384]{2,1,0:T(8,128)(2,1)S(1)}, bf16[2,192,384]{2,1,0:T(8,128)(2,1)S(1)}, u32[]{:S(2)}, u32[]{:S(2)}) collective-permute-start(bf16[2,192,384]{2,1,0:T(8,128)(2,1)S(1)} %fusion.4), channel_id=1, source_target_pairs={{0,1},{1,0},{2,6},{3,7},{4,5},{5,4},{6,2},{7,3},{8,9},{9,8},{10,14... | collective-permute-start | bytes 884744 | tf_op jit(solution)/shard_map/ppermute | solution.py:674
  88.0 12.1 %collective-permute-start.10 = (bf16[4,192,384]{2,1,0:T(8,128)(2,1)S(1)}, bf16[4,192,384]{2,1,0:T(8,128)(2,1)S(1)}, u32[]{:S(2)}, u32[]{:S(2)}) collective-permute-start(bf16[4,192,384]{2,1,0:T(8,128)(2,1)S(1)} %fusion.2), channel_id=1, source_target_pairs={{0,1},{1,0},{2,6},{3,7},{4,5},{5,4},{6,2},{7,3},{8,9},{9,8},{10,14... | collective-permute-start | bytes 1769480 | tf_op jit(solution)/shard_map/ppermute | solution.py:674
  95.9 4.2 %collective-permute-start.11 = (bf16[4,192,384]{2,1,0:T(8,128)(2,1)S(1)}, bf16[4,192,384]{2,1,0:T(8,128)(2,1)S(1)}, u32[]{:S(2)}, u32[]{:S(2)}) collective-permute-start(bf16[4,192,384]{2,1,0:T(8,128)(2,1)S(1)} %get-tuple-element.178), channel_id=1, source_target_pairs={{0,2},{2,0},{4,6},{6,4},{8,10},{10,8},{12,14},{14,12},{16,18},{18,... | collective-permute-start | bytes 1769480 | tf_op jit(solution)/shard_map/ppermute | solution.py:664
  96.0 4.1 %collective-permute-start.12 = (bf16[4,192,384]{2,1,0:T(8,128)(2,1)S(1)}, bf16[4,192,384]{2,1,0:T(8,128)(2,1)S(1)}, u32[]{:S(2)}, u32[]{:S(2)}) collective-permute-start(bf16[4,192,384]{2,1,0:T(8,128)(2,1)S(1)} %get-tuple-element.179), channel_id=1, source_target_pairs={{0,2},{2,0},{4,6},{6,4},{8,10},{10,8},{12,14},{14,12},{16,18},{18,... | collective-permute-start | bytes 1769480 | tf_op jit(solution)/shard_map/ppermute | solution.py:664
  96.5 2.4 %collective-permute-start.13 = (f32[32,384]{1,0:T(8,128)S(1)}, f32[32,384]{1,0:T(8,128)S(1)}, u32[]{:S(2)}, u32[]{:S(2)}) collective-permute-start(f32[32,384]{1,0:T(8,128)S(1)} %get-tuple-element.180.refs_17_), channel_id=1, source_target_pairs={{0,2},{2,0},{4,6},{6,4},{8,10},{10,8},{12,14},{14,12},{16,18},{18,... | collective-permute-start | bytes 147464 | tf_op jit(solution)/shard_map/ppermute | solution.py:664
  101.2 16.5 %collective-permute-start.14 = (bf16[1568,384]{1,0:T(8,128)(2,1)S(1)}, bf16[1568,384]{1,0:T(8,128)(2,1)S(1)}, u32[]{:S(2)}, u32[]{:S(2)}) collective-permute-start(bf16[1568,384]{1,0:T(8,128)(2,1)S(1)} %get-tuple-element.186), channel_id=1, source_target_pairs={{0,4},{1,5},{2,3},{3,2},{4,0},{5,1},{6,7},{7,6},{8,12},{9,13},{10,... | collective-permute-start | bytes 3612680 | tf_op jit(solution)/shard_map/ppermute | solution.py:674
  102.7 12.6 %collective-permute-start.15 = (bf16[4,192,384]{2,1,0:T(8,128)(2,1)S(1)}, bf16[4,192,384]{2,1,0:T(8,128)(2,1)S(1)}, u32[]{:S(2)}, u32[]{:S(2)}) collective-permute-start(bf16[4,192,384]{2,1,0:T(8,128)(2,1)S(1)} %get-tuple-element.188), channel_id=1, source_target_pairs={{0,2},{2,0},{4,6},{6,4},{8,10},{10,8},{12,14},{14,12},{16,18},{18,... | collective-permute-start | bytes 1769480 | tf_op jit(solution)/shard_map/ppermute | solution.py:664
  102.7 12.6 %collective-permute-start.16 = (bf16[4,192,384]{2,1,0:T(8,128)(2,1)S(1)}, bf16[4,192,384]{2,1,0:T(8,128)(2,1)S(1)}, u32[]{:S(2)}, u32[]{:S(2)}) collective-permute-start(bf16[4,192,384]{2,1,0:T(8,128)(2,1)S(1)} %get-tuple-element.190), channel_id=1, source_target_pairs={{0,2},{2,0},{4,6},{6,4},{8,10},{10,8},{12,14},{14,12},{16,18},{18,... | collective-permute-start | bytes 1769480 | tf_op jit(solution)/shard_map/ppermute | solution.py:664
  103.2 12.1 %collective-permute-start.17 = (bf16[384,384]{1,0:T(8,128)(2,1)S(1)}, bf16[384,384]{1,0:T(8,128)(2,1)S(1)}, u32[]{:S(2)}, u32[]{:S(2)}) collective-permute-start(bf16[384,384]{1,0:T(8,128)(2,1)S(1)} %get-tuple-element.191), channel_id=1, source_target_pairs={{0,8},{1,9},{2,10},{3,11},{4,12},{5,13},{6,14},{7,15},{8,0},{9,1},... | collective-permute-start | bytes 884744 | tf_op jit(solution)/shard_map/ppermute | solution.py:674
  104.8 9.6 %collective-permute-start.18 = (bf16[192,384]{1,0:T(8,128)(2,1)S(1)}, bf16[192,384]{1,0:T(8,128)(2,1)S(1)}, u32[]{:S(2)}, u32[]{:S(2)}) collective-permute-start(bf16[192,384]{1,0:T(8,128)(2,1)S(1)} %get-tuple-element.192), channel_id=1, source_target_pairs={{0,16},{1,17},{2,18},{3,19},{4,20},{5,21},{6,22},{7,23},{8,24},{9,... | collective-permute-start | bytes 442376 | tf_op jit(solution)/shard_map/ppermute | solution.py:674
  118.6 10.2 %collective-permute-start.19 = (bf16[800,384]{1,0:T(8,128)(2,1)S(1)}, bf16[800,384]{1,0:T(8,128)(2,1)S(1)}, u32[]{:S(2)}, u32[]{:S(2)}) collective-permute-start(bf16[800,384]{1,0:T(8,128)(2,1)S(1)} %get-tuple-element.201), channel_id=1, source_target_pairs={{0,1},{1,0},{2,6},{3,7},{4,5},{5,4},{6,2},{7,3},{8,9},{9,8},{10,14... | collective-permute-start | bytes 1843208 | tf_op jit(solution)/shard_map/ppermute | solution.py:674
  119.4 8.4 %collective-permute-start.20 = (bf16[192,384]{1,0:T(8,128)(2,1)S(1)}, bf16[192,384]{1,0:T(8,128)(2,1)S(1)}, u32[]{:S(2)}, u32[]{:S(2)}) collective-permute-start(bf16[192,384]{1,0:T(8,128)(2,1)S(1)} %get-tuple-element.202), channel_id=1, source_target_pairs={{0,16},{1,17},{2,18},{3,19},{4,20},{5,21},{6,22},{7,23},{8,24},{9,... | collective-permute-start | bytes 442376 | tf_op jit(solution)/shard_map/ppermute | solution.py:674
  129.5 7.5 %collective-permute-start.21 = (bf16[416,384]{1,0:T(8,128)(2,1)S(1)}, bf16[416,384]{1,0:T(8,128)(2,1)S(1)}, u32[]{:S(2)}, u32[]{:S(2)}) collective-permute-start(bf16[416,384]{1,0:T(8,128)(2,1)S(1)} %get-tuple-element.209), channel_id=1, source_target_pairs={{0,8},{1,9},{2,10},{3,11},{4,12},{5,13},{6,14},{7,15},{8,0},{9,1},... | collective-permute-start | bytes 958472 | tf_op jit(solution)/shard_map/ppermute | solution.py:674
  131.1 10.2 %collective-permute-start.23 = (bf16[256,768]{1,0:T(8,128)(2,1)S(1)}, bf16[256,768]{1,0:T(8,128)(2,1)S(1)}, u32[]{:S(2)}, u32[]{:S(2)}) collective-permute-start(bf16[256,768]{1,0:T(8,128)(2,1)S(1)} %get-tuple-element.214), channel_id=1, source_target_pairs={{0,1},{1,0},{2,3},{3,2},{4,5},{5,4},{6,7},{7,6},{8,9},{9,8},{10,11... | collective-permute-start | bytes 1179656 | tf_op jit(solution)/shard_map/ppermute | solution.py:663
  131.9 12.3 %collective-permute-start.24 = (bf16[128,768]{1,0:T(8,128)(2,1)S(1)}, bf16[128,768]{1,0:T(8,128)(2,1)S(1)}, u32[]{:S(2)}, u32[]{:S(2)}) collective-permute-start(bf16[128,768]{1,0:T(8,128)(2,1)S(1)} %get-tuple-element.220), channel_id=1, source_target_pairs={{0,1},{1,0},{2,3},{3,2},{4,5},{5,4},{6,7},{7,6},{8,9},{9,8},{10,11... | collective-permute-start | bytes 589832 | tf_op jit(solution)/shard_map/ppermute | solution.py:663
  137.6 8.2 %collective-permute-start.22 = (bf16[224,384]{1,0:T(8,128)(2,1)S(1)}, bf16[224,384]{1,0:T(8,128)(2,1)S(1)}, u32[]{:S(2)}, u32[]{:S(2)}) collective-permute-start(bf16[224,384]{1,0:T(8,128)(2,1)S(1)} %get-tuple-element.211), channel_id=1, source_target_pairs={{0,16},{1,17},{2,18},{3,19},{4,20},{5,21},{6,22},{7,23},{8,24},{9,... | collective-permute-start | bytes 516104 | tf_op jit(solution)/shard_map/ppermute | solution.py:674

commit v7 on v6

--- a/solution.py
+++ b/solution.py
@@ -806,17 +806,18 @@
     r3.got.append(r3.away(going))
     grad_got = trade(after(grad_rem, going), "y")
     got1 = trade(after(out1, going), "y")
+    inner = total_inner(
+        after(s, going), at(of_z(0, 0), *r2.got[:4]) + at(of_z2(0), r2.got[4]) + at(0, r2.got[5]))
+
+    r3.got[-1], inner = together(r3.got[-1], inner)
 
     going, vec = combine(
         s, [[(192, at(of_z(0, 1), *r3.got[:4]) + at(of_z2(1), r3.got[4]))]], vec, r3.got[-1])
     r3.got.append(r3.away(going))
     grad = finish(after(s, going), grad_got, grad)
-    inner = total_inner(
-        after(s, going, grad), at(of_z(0, 0), *r2.got[:4]) + at(of_z2(0), r2.got[4]) + at(0, r2.got[5]))
-
-    out = finish(after(s, inner), got1, out, 1)
-
-    r3.got[-1], grad, inner, out = together(r3.got[-1], grad, inner, out)
+    out = finish(after(s, grad), got1, out, 1)
+
+    r3.got[-1], grad, out = together(r3.got[-1], grad, out)
     apart = low_n == 1
     sums = combine(
         s, [[(192, at(of_z(0, 0), *r3.got[:4]) + at(of_z2(0), r3.got[4]) + at(0, r3.got[5]))]],

time: 148 us -> 148 us (level)
  transfers between devices with their start and end apart: 25 -> 25, of which waited for: 14 -> 15; matrix products, arithmetic and copies ran while one was open for 2% -> 2% of each run, Pallas kernels for 43% -> 43%
where the time goes in v7:
time: 148 us; the launch traced here: 147 us
  Pallas kernels  81 us (55%)
  waiting for transfers between devices  30.6 us (21%)
  starting transfers between devices  29.2 us (20%)
  local copies, waits for them, and re-layouts  3.37 us (2%)
  other arithmetic  2.11 us (1%)
    ppermute x12, starting transfers between devices, trade_stage(): return lax.ppermute(value, ('dp', 'seq'), pairs)  20.2 us
    ppermute x12, waiting for transfers between devices, trade_stage(): return lax.ppermute(value, ('dp', 'seq'), pairs)  19.1 us
    pallas_call x1, Pallas kernels, mlp_fwd(): call(mlp_fwd_body, (ff // w,), [full((t, d)), cols(d, w), vec(w), rows_of...  13.5 us
    pallas_call x1, Pallas kernels, attn_fwd(): call(attn_fwd_body, (d // 256,), [own_slot(half, d), full((half, d))] + [...  12.7 us
    pallas_call x1, Pallas kernels, attn_bwd(): call(attn_bwd_body, (d // 256,), [full((t, d)), rows_of(256, d), cols(t,...  9.94 us
    ppermute x5, waiting for transfers between devices, trade(): return lax.ppermute(value, 'seq', [(0, 1), (1, 0)])  9.21 us
    ppermute x5, starting transfers between devices, trade(): return lax.ppermute(value, 'seq', [(0, 1), (1, 0)])  7.2 us
    pallas_call x1, Pallas kernels, slope_first(): call(slope_first_body, (ff // w,), [cols(t, w), cols(d, w), full((t, d)),...  6.97 us
  transfers between devices with their start and end apart: 25, of which 15 were waited for; matrix products, arithmetic and copies ran while one was open for 2% of the time, Pallas kernels for 43%

profile of v7, /device:TPU:0, one launch (start us, length us, event | category | flops | bytes accessed | tf_op | source)
XLA Modules:
  0.0 147.4 jit_solution(15573019857286870648)
XLA Ops:
  1.7 3.1 %collective-permute-start = (bf16[256,768]{1,0:T(8,128)(2,1)S(1)}, bf16[256,768]{1,0:T(8,128)(2,1)S(1)}, u32[]{:S(2)}, u32[]{:S(2)}) collective-permute-start(bf16[256,768]{1,0:T(8,128)(2,1)S(1)} %dynamic-slice_bitcast_fusion.1), channel_id=1, source_target_pairs={{0,1},{1,0},{2,3},{3,2},{4,5},{5,4},{6,7},{7,6},{8,9},{9,8},{10,11... | collective-permute-start | bytes 1179656 | tf_op jit(solution)/shard_map/ppermute | solution.py:663
  7.2 7.5 %collective-permute-done.rem = bf16[256,768]{1,0:T(8,128)(2,1)S(1)} collective-permute-done((bf16[256,768]{1,0:T(8,128)(2,1)S(1)}, bf16[256,768]{1,0:T(8,128)(2,1)S(1)}, u32[]{:S(2)}, u32[]{:S(2)}) %collective-permute-start) | collective-permute-done | bytes 393248 | tf_op jit(solution)/shard_map/ppermute | solution.py:663
  14.7 12.7 %attn_fwd.1 = (bf16[512,768]{1,0:T(8,128)(2,1)S(1)}, bf16[768,512]{1,0:T(8,128)(2,1)S(1)}, bf16[512,768]{1,0:T(8,128)(2,1)S(1)}, bf16[12,512,512]{2,1,0:T(8,128)...) custom-call(s32[6]{0:T(128)S(1)} %stack.24.s, ...), custom_call_target="tpu_custom_call" | custom-call | flops 3200000 | bytes 18874 | tf_op jit(solution)/shard_map/attn_fwd/pallas_call | solution.py:137
  27.4 13.5 %mlp_fwd.1 = (bf16[512,3072]{1,0:T(8,128)(2,1)S(1)}, bf16[512,3072]{1,0:T(8,128)(2,1)S(1)}, f32[2,256,768]{2,1,0:T(8,128)}, bf16[128,768]{1,0:T(8,128)(2,1)S(1)}...) custom-call(s32[6]{0:T(128)S(1)} %stack.24.s, ...), custom_call_target="tpu_custom_call" | custom-call | flops 4800000 | bytes 25165 | tf_op jit(solution)/shard_map/mlp_fwd/pallas_call | solution.py:239
  40.9 2.0 %collective-permute-start.2 = (bf16[128,768]{1,0:T(8,128)(2,1)S(1)}, bf16[128,768]{1,0:T(8,128)(2,1)S(1)}, u32[]{:S(2)}, u32[]{:S(2)}) collective-permute-start(bf16[128,768]{1,0:T(8,128)(2,1)S(1)} %get-tuple-element.136), channel_id=1, source_target_pairs={{0,1},{1,0},{2,3},{3,2},{4,5},{5,4},{6,7},{7,6},{8,9},{9,8},{10,11... | collective-permute-start | bytes 589832 | tf_op jit(solution)/shard_map/ppermute | solution.py:663
  42.9 5.1 %weight_outer.1 = (bf16[2,2,2,2,192,384]{5,4,3,2,1,0:T(8,128)(2,1)S(1)}, bf16[2,2,2,2,192,384]{5,4,3,2,1,0:T(8,128)(2,1)S(1)}) custom-call(s32[6]{0:T(128)S(1)} %stack.24.s, bf16[512,3072]{1,0:T(8,128)(2,1)S(1)} %get-tuple-element.132.act, bf16[512,768]{1,0:T(8,128)(2,1)S(1)} %get-tuple-element.133.sl), custom_call_target="tpu_custom_call" | custom-call | flops 2400000 | bytes 10485 | tf_op jit(solution)/shard_map/weight_outer/pallas_call | solution.py:725
  48.1 5.5 %slope_inner.1 = (bf16[512,3072]{1,0:T(8,128)(2,1)S(1)}, f32[1,3072]{1,0:T(1,128)S(1)}) custom-call(s32[6]{0:T(128)S(1)} %stack.24.s, bf16[512,768]{1,0:T(8,128)(2,1)S(1)} %get-tuple-element.133.sl, bf16[3072,768]{1,0:T(8,128)(2,1)} %wo.3, bf16[512,3072]{1,0:T(8,128)(2,1)S(1)} %get-tuple-element.139.dg), custom_call_target="tpu_custom_call" | custom-call | flops 2400000 | bytes 12582 | tf_op jit(solution)/shard_map/slope_inner/pallas_call | solution.py:275
  53.9 1.6 %collective-permute-start.4 = (bf16[2,2,2,192,384]{4,3,2,1,0:T(8,128)(2,1)S(1)}, bf16[2,2,2,192,384]{4,3,2,1,0:T(8,128)(2,1)S(1)}, u32[]{:S(2)}, u32[]{:S(2)}) collective-permute-start(bf16[2,2,2,192,384]{4,3,2,1,0:T(8,128)(2,1)S(1)} %fusion.1), channel_id=1, source_target_pairs={{0,4},{1,5},{2,3},{3,2},{4,0},{5,1},{6,7},{7,6},{8,12},{9,13},{10,... | collective-permute-start | bytes 3538952 | tf_op jit(solution)/shard_map/ppermute | solution.py:674
  55.5 5.4 %weight_inner.1 = (bf16[2,2,4,192,384]{4,3,2,1,0:T(8,128)(2,1)S(1)}, bf16[2,4,192,384]{3,2,1,0:T(8,128)(2,1)S(1)}, bf16[2,4,192,384]{3,2,1,0:T(8,128)(2,1)S(1)}) custom-call(s32[6]{0:T(128)S(1)} %stack.24.s, bf16[512,768]{1,0:T(8,128)(2,1)S(1)} %get-tuple-element.130.nl, bf16[512,3072]{1,0:T(8,128)(2,1)S(1)} %get-tuple-element.143.si0.si1.si, ...), custom_call_target="tpu_custom_call" | custom-call | flops 2400000 | bytes 10485 | tf_op jit(solution)/shard_map/weight_inner/pallas_call | solution.py:734
  61.4 7.0 %slope_first.1 = (f32[512,768]{1,0:T(8,128)S(1)}, bf16[512,768]{1,0:T(8,128)(2,1)S(1)}, f32[3,768]{1,0:T(4,128)S(1)}) custom-call(s32[6]{0:T(128)S(1)} %stack.24.s, bf16[512,3072]{1,0:T(8,128)(2,1)S(1)} %get-tuple-element.143.si0.si1.si, bf16[768,3072]{1,0:T(8,128)(2,1)} %wi.3, f32[512,768]{1,0:T(8,128)S(1)} %get-tuple-element.147.ss, ...), custom_call_target="tpu_custom_call" | custom-call | flops 2400000 | bytes 14680 | tf_op jit(solution)/shard_map/slope_first/pallas_call | solution.py:324
  68.4 1.8 %collective-permute-done.4 = bf16[2,2,2,192,384]{4,3,2,1,0:T(8,128)(2,1)S(1)} collective-permute-done((bf16[2,2,2,192,384]{4,3,2,1,0:T(8,128)(2,1)S(1)}, bf16[2,2,2,192,384]{4,3,2,1,0:T(8,128)(2,1)S(1)}, u32[]{:S(2)}, u32[]{:S(2)}) %collective-permute-start.4) | collective-permute-done | bytes 1179680 | tf_op jit(solution)/shard_map/ppermute | solution.py:674
  70.5 1.6 %collective-permute-start.8 = (bf16[2,4,192,384]{3,2,1,0:T(8,128)(2,1)S(1)}, bf16[2,4,192,384]{3,2,1,0:T(8,128)(2,1)S(1)}, u32[]{:S(2)}, u32[]{:S(2)}) collective-permute-start(bf16[2,4,192,384]{3,2,1,0:T(8,128)(2,1)S(1)} %fusion), channel_id=1, source_target_pairs={{0,4},{1,5},{2,3},{3,2},{4,0},{5,1},{6,7},{7,6},{8,12},{9,13},{10,... | collective-permute-start | bytes 3538952 | tf_op jit(solution)/shard_map/ppermute | solution.py:674
  72.3 1.6 %collective-permute-start.7 = (bf16[2,2,192,384]{3,2,1,0:T(8,128)(2,1)S(1)}, bf16[2,2,192,384]{3,2,1,0:T(8,128)(2,1)S(1)}, u32[]{:S(2)}, u32[]{:S(2)}) collective-permute-start(bf16[2,2,192,384]{3,2,1,0:T(8,128)(2,1)S(1)} %fusion.3), channel_id=1, source_target_pairs={{0,8},{1,9},{2,10},{3,11},{4,12},{5,13},{6,14},{7,15},{8,0},{9,1},... | collective-permute-start | bytes 1769480 | tf_op jit(solution)/shard_map/ppermute | solution.py:674
  74.0 9.9 %attn_bwd.1 = (bf16[512,768]{1,0:T(8,128)(2,1)S(1)}, bf16[512,768]{1,0:T(8,128)(2,1)S(1)}, bf16[512,768]{1,0:T(8,128)(2,1)S(1)}) custom-call(s32[6]{0:T(128)S(1)} %stack.24.s, bf16[512,768]{1,0:T(8,128)(2,1)S(1)} %get-tuple-element.154.ml, bf16[768,768]{1,0:T(8,128)(2,1)} %wm.3, bf16[512,768]{1,0:T(8,128)(2,1)S(1)} %get-tuple-element.155.q, ...), custom_call_target="tpu_custom_call" | custom-call | flops 3600000 | bytes 15728 | tf_op jit(solution)/shard_map/attn_bwd/pallas_call | solution.py:368
  83.9 2.1 %collective-permute-done.7 = bf16[2,2,192,384]{3,2,1,0:T(8,128)(2,1)S(1)} collective-permute-done((bf16[2,2,192,384]{3,2,1,0:T(8,128)(2,1)S(1)}, bf16[2,2,192,384]{3,2,1,0:T(8,128)(2,1)S(1)}, u32[]{:S(2)}, u32[]{:S(2)}) %collective-permute-start.7) | collective-permute-done | bytes 589856 | tf_op jit(solution)/shard_map/ppermute | solution.py:674
  88.0 1.4 collective-permute-start.10
  89.4 6.5 %weight_last.1 = (bf16[2,2,4,192,384]{4,3,2,1,0:T(8,128)(2,1)S(1)}, bf16[4,192,384]{2,1,0:T(8,128)(2,1)S(1)}, bf16[4,192,384]{2,1,0:T(8,128)(2,1)S(1)}, bf16[4,1...) custom-call(s32[6]{0:T(128)S(1)} %stack.24.s, bf16[2,256,768]{2,1,0:T(8,128)(2,1)} %own.3, ...), custom_call_target="tpu_custom_call" | custom-call | flops 2400000 | bytes 10485 | tf_op jit(solution)/shard_map/weight_last/pallas_call | solution.py:755
  96.6 2.3 %collective-permute-done.13.refs_18_ = f32[32,384]{1,0:T(8,128)S(1)} collective-permute-done((f32[32,384]{1,0:T(8,128)S(1)}, f32[32,384]{1,0:T(8,128)S(1)}, u32[]{:S(2)}, u32[]{:S(2)}) %collective-permute-start.13) | collective-permute-done | bytes 49184 | tf_op jit(solution)/shard_map/ppermute | solution.py:664
  101.2 1.6 %collective-permute-start.14 = (bf16[1568,384]{1,0:T(8,128)(2,1)S(1)}, bf16[1568,384]{1,0:T(8,128)(2,1)S(1)}, u32[]{:S(2)}, u32[]{:S(2)}) collective-permute-start(bf16[1568,384]{1,0:T(8,128)(2,1)S(1)} %get-tuple-element.187), channel_id=1, source_target_pairs={{0,4},{1,5},{2,3},{3,2},{4,0},{5,1},{6,7},{7,6},{8,12},{9,13},{10,... | collective-permute-start | bytes 3612680 | tf_op jit(solution)/shard_map/ppermute | solution.py:674
  103.2 1.6 %collective-permute-start.17 = (bf16[384,384]{1,0:T(8,128)(2,1)S(1)}, bf16[384,384]{1,0:T(8,128)(2,1)S(1)}, u32[]{:S(2)}, u32[]{:S(2)}) collective-permute-start(bf16[384,384]{1,0:T(8,128)(2,1)S(1)} %get-tuple-element.192), channel_id=1, source_target_pairs={{0,8},{1,9},{2,10},{3,11},{4,12},{5,13},{6,14},{7,15},{8,0},{9,1},... | collective-permute-start | bytes 884744 | tf_op jit(solution)/shard_map/ppermute | solution.py:674
  104.8 2.6 %collective-permute-start.18 = (bf16[192,384]{1,0:T(8,128)(2,1)S(1)}, bf16[192,384]{1,0:T(8,128)(2,1)S(1)}, u32[]{:S(2)}, u32[]{:S(2)}) collective-permute-start(bf16[192,384]{1,0:T(8,128)(2,1)S(1)} %get-tuple-element.193), channel_id=1, source_target_pairs={{0,16},{1,17},{2,18},{3,19},{4,20},{5,21},{6,22},{7,23},{8,24},{9,... | collective-permute-start | bytes 442376 | tf_op jit(solution)/shard_map/ppermute | solution.py:674
  107.4 5.4 %input_grad.1 = (f32[2,256,768]{2,1,0:T(8,128)}, bf16[256,768]{1,0:T(8,128)(2,1)S(1)}) custom-call(s32[6]{0:T(128)S(1)} %stack.24.s, bf16[512,768]{1,0:T(8,128)(2,1)S(1)} %get-tuple-element.168.dq, bf16[512,768]{1,0:T(8,128)(2,1)S(1)} %get-tuple-element.169.dk, bf16[512,768]{1,0:T(8,128)(2,1)S(1)} %get-tuple-element.170.dv, bf16[768,768]{1,0:T(8,128)(2,1)} %wq.3, ...), custom_call_target="tpu_custom_call" | custom-call | flops 1800000 | bytes 8388 | tf_op jit(solution)/shard_map/input_grad/pallas_call | solution.py:400
  112.8 1.6 %collective-permute-done.18 = bf16[192,384]{1,0:T(8,128)(2,1)S(1)} collective-permute-done((bf16[192,384]{1,0:T(8,128)(2,1)S(1)}, bf16[192,384]{1,0:T(8,128)(2,1)S(1)}, u32[]{:S(2)}, u32[]{:S(2)}) %collective-permute-start.18) | collective-permute-done | bytes 147488 | tf_op jit(solution)/shard_map/ppermute | solution.py:674
  115.3 2.4 %collective-permute-done.14.refs_1_.refs_9_.refs_2_.refs_6_ = bf16[1568,384]{1,0:T(8,128)(2,1)S(1)} collective-permute-done((bf16[1568,384]{1,0:T(8,128)(2,1)S(1)}, bf16[1568,384]{1,0:T(8,128)(2,1)S(1)}, u32[]{:S(2)}, u32[]{:S(2)}) %collective-permute-start.14) | collective-permute-done | bytes 1204256 | tf_op jit(solution)/shard_map/ppermute | solution.py:674
  119.4 2.6 %collective-permute-start.20 = (bf16[192,384]{1,0:T(8,128)(2,1)S(1)}, bf16[192,384]{1,0:T(8,128)(2,1)S(1)}, u32[]{:S(2)}, u32[]{:S(2)}) collective-permute-start(bf16[192,384]{1,0:T(8,128)(2,1)S(1)} %get-tuple-element.203), channel_id=1, source_target_pairs={{0,16},{1,17},{2,18},{3,19},{4,20},{5,21},{6,22},{7,23},{8,24},{9,... | collective-permute-start | bytes 442376 | tf_op jit(solution)/shard_map/ppermute | solution.py:674
  124.1 3.7 %collective-permute-done.20.refs_5_ = bf16[192,384]{1,0:T(8,128)(2,1)S(1)} collective-permute-done((bf16[192,384]{1,0:T(8,128)(2,1)S(1)}, bf16[192,384]{1,0:T(8,128)(2,1)S(1)}, u32[]{:S(2)}, u32[]{:S(2)}) %collective-permute-start.20) | collective-permute-done | bytes 147488 | tf_op jit(solution)/shard_map/ppermute | solution.py:674
  129.5 1.6 %collective-permute-start.21 = (bf16[416,384]{1,0:T(8,128)(2,1)S(1)}, bf16[416,384]{1,0:T(8,128)(2,1)S(1)}, u32[]{:S(2)}, u32[]{:S(2)}) collective-permute-start(bf16[416,384]{1,0:T(8,128)(2,1)S(1)} %get-tuple-element.210), channel_id=1, source_target_pairs={{0,8},{1,9},{2,10},{3,11},{4,12},{5,13},{6,14},{7,15},{8,0},{9,1},... | collective-permute-start | bytes 958472 | tf_op jit(solution)/shard_map/ppermute | solution.py:674
  133.2 1.4 total_inner.1
  134.5 2.4 %collective-permute-done.21.refs_4_.refs_6_ = bf16[416,384]{1,0:T(8,128)(2,1)S(1)} collective-permute-done((bf16[416,384]{1,0:T(8,128)(2,1)S(1)}, bf16[416,384]{1,0:T(8,128)(2,1)S(1)}, u32[]{:S(2)}, u32[]{:S(2)}) %collective-permute-start.21) | collective-permute-done | bytes 319520 | tf_op jit(solution)/shard_map/ppermute | solution.py:674
  137.6 2.6 %collective-permute-start.22 = (bf16[224,384]{1,0:T(8,128)(2,1)S(1)}, bf16[224,384]{1,0:T(8,128)(2,1)S(1)}, u32[]{:S(2)}, u32[]{:S(2)}) collective-permute-start(bf16[224,384]{1,0:T(8,128)(2,1)S(1)} %get-tuple-element.215), channel_id=1, source_target_pairs={{0,16},{1,17},{2,18},{3,19},{4,20},{5,21},{6,22},{7,23},{8,24},{9,... | collective-permute-start | bytes 516104 | tf_op jit(solution)/shard_map/ppermute | solution.py:674
  141.3 1.5 finish.4
  145.9 1.3 combine.9
  (48 shorter events, 23.7 us)
Async XLA Ops:
  0.7 5.2 %copy-start = (s32[2]{0:T(128)S(1)}, s32[2]{0:T(128)}, u32[]{:S(2)}) copy-start(s32[2]{0:T(128)} %param.20) | copy-start | bytes 28
  1.7 13.0 %collective-permute-start = (bf16[256,768]{1,0:T(8,128)(2,1)S(1)}, bf16[256,768]{1,0:T(8,128)(2,1)S(1)}, u32[]{:S(2)}, u32[]{:S(2)}) collective-permute-start(bf16[256,768]{1,0:T(8,128)(2,1)S(1)} %dynamic-slice_bitcast_fusion.1), channel_id=1, source_target_pairs={{0,1},{1,0},{2,3},{3,2},{4,5},{5,4},{6,7},{7,6},{8,9},{9,8},{10,11... | collective-permute-start | bytes 1179656 | tf_op jit(solution)/shard_map/ppermute | solution.py:663
  5.8 21.6 %collective-permute-start.1 = (bf16[256,768]{1,0:T(8,128)(2,1)S(1)}, bf16[256,768]{1,0:T(8,128)(2,1)S(1)}, u32[]{:S(2)}, u32[]{:S(2)}) collective-permute-start(bf16[256,768]{1,0:T(8,128)(2,1)S(1)} %dynamic-slice_bitcast_fusion), channel_id=1, source_target_pairs={{0,1},{1,0},{2,3},{3,2},{4,5},{5,4},{6,7},{7,6},{8,9},{9,8},{10,11... | collective-permute-start | bytes 1179656 | tf_op jit(solution)/shard_map/ppermute | solution.py:663
  40.9 7.1 %collective-permute-start.2 = (bf16[128,768]{1,0:T(8,128)(2,1)S(1)}, bf16[128,768]{1,0:T(8,128)(2,1)S(1)}, u32[]{:S(2)}, u32[]{:S(2)}) collective-permute-start(bf16[128,768]{1,0:T(8,128)(2,1)S(1)} %get-tuple-element.136), channel_id=1, source_target_pairs={{0,1},{1,0},{2,3},{3,2},{4,5},{5,4},{6,7},{7,6},{8,9},{9,8},{10,11... | collective-permute-start | bytes 589832 | tf_op jit(solution)/shard_map/ppermute | solution.py:663
  48.0 5.5 %collective-permute-start.3 = (bf16[2,2,2,2,192,384]{5,4,3,2,1,0:T(8,128)(2,1)S(1)}, bf16[2,2,2,2,192,384]{5,4,3,2,1,0:T(8,128)(2,1)S(1)}, u32[]{:S(2)}, u32[]{:S(2)}) collective-permute-start(bf16[2,2,2,2,192,384]{5,4,3,2,1,0:T(8,128)(2,1)S(1)} %get-tuple-element.137), channel_id=1, source_target_pairs={{0,2},{2,0},{4,6},{6,4},{8,10},{10,8},{12,14},{14,12},{16,18},{18,... | collective-permute-start | bytes 7077896 | tf_op jit(solution)/shard_map/ppermute | solution.py:664
  53.9 16.3 %collective-permute-start.4 = (bf16[2,2,2,192,384]{4,3,2,1,0:T(8,128)(2,1)S(1)}, bf16[2,2,2,192,384]{4,3,2,1,0:T(8,128)(2,1)S(1)}, u32[]{:S(2)}, u32[]{:S(2)}) collective-permute-start(bf16[2,2,2,192,384]{4,3,2,1,0:T(8,128)(2,1)S(1)} %fusion.1), channel_id=1, source_target_pairs={{0,4},{1,5},{2,3},{3,2},{4,0},{5,1},{6,7},{7,6},{8,12},{9,13},{10,... | collective-permute-start | bytes 3538952 | tf_op jit(solution)/shard_map/ppermute | solution.py:674
  60.9 9.3 %collective-permute-start.5 = (bf16[2,4,192,384]{3,2,1,0:T(8,128)(2,1)S(1)}, bf16[2,4,192,384]{3,2,1,0:T(8,128)(2,1)S(1)}, u32[]{:S(2)}, u32[]{:S(2)}) collective-permute-start(bf16[2,4,192,384]{3,2,1,0:T(8,128)(2,1)S(1)} %get-tuple-element.144), channel_id=1, source_target_pairs={{0,2},{2,0},{4,6},{6,4},{8,10},{10,8},{12,14},{14,12},{16,18},{18,... | collective-permute-start | bytes 3538952 | tf_op jit(solution)/shard_map/ppermute | solution.py:664
  60.9 9.3 %collective-permute-start.6 = (bf16[2,4,192,384]{3,2,1,0:T(8,128)(2,1)S(1)}, bf16[2,4,192,384]{3,2,1,0:T(8,128)(2,1)S(1)}, u32[]{:S(2)}, u32[]{:S(2)}) collective-permute-start(bf16[2,4,192,384]{3,2,1,0:T(8,128)(2,1)S(1)} %get-tuple-element.145), channel_id=1, source_target_pairs={{0,2},{2,0},{4,6},{6,4},{8,10},{10,8},{12,14},{14,12},{16,18},{18,... | collective-permute-start | bytes 3538952 | tf_op jit(solution)/shard_map/ppermute | solution.py:664
  70.5 16.3 %collective-permute-start.8 = (bf16[2,4,192,384]{3,2,1,0:T(8,128)(2,1)S(1)}, bf16[2,4,192,384]{3,2,1,0:T(8,128)(2,1)S(1)}, u32[]{:S(2)}, u32[]{:S(2)}) collective-permute-start(bf16[2,4,192,384]{3,2,1,0:T(8,128)(2,1)S(1)} %fusion), channel_id=1, source_target_pairs={{0,4},{1,5},{2,3},{3,2},{4,0},{5,1},{6,7},{7,6},{8,12},{9,13},{10,... | collective-permute-start | bytes 3538952 | tf_op jit(solution)/shard_map/ppermute | solution.py:674
  72.3 13.7 %collective-permute-start.7 = (bf16[2,2,192,384]{3,2,1,0:T(8,128)(2,1)S(1)}, bf16[2,2,192,384]{3,2,1,0:T(8,128)(2,1)S(1)}, u32[]{:S(2)}, u32[]{:S(2)}) collective-permute-start(bf16[2,2,192,384]{3,2,1,0:T(8,128)(2,1)S(1)} %fusion.3), channel_id=1, source_target_pairs={{0,8},{1,9},{2,10},{3,11},{4,12},{5,13},{6,14},{7,15},{8,0},{9,1},... | collective-permute-start | bytes 1769480 | tf_op jit(solution)/shard_map/ppermute | solution.py:674
  87.0 8.9 %collective-permute-start.9 = (bf16[2,192,384]{2,1,0:T(8,128)(2,1)S(1)}, bf16[2,192,384]{2,1,0:T(8,128)(2,1)S(1)}, u32[]{:S(2)}, u32[]{:S(2)}) collective-permute-start(bf16[2,192,384]{2,1,0:T(8,128)(2,1)S(1)} %fusion.4), channel_id=1, source_target_pairs={{0,1},{1,0},{2,6},{3,7},{4,5},{5,4},{6,2},{7,3},{8,9},{9,8},{10,14... | collective-permute-start | bytes 884744 | tf_op jit(solution)/shard_map/ppermute | solution.py:674
  88.0 12.1 %collective-permute-start.10 = (bf16[4,192,384]{2,1,0:T(8,128)(2,1)S(1)}, bf16[4,192,384]{2,1,0:T(8,128)(2,1)S(1)}, u32[]{:S(2)}, u32[]{:S(2)}) collective-permute-start(bf16[4,192,384]{2,1,0:T(8,128)(2,1)S(1)} %fusion.2), channel_id=1, source_target_pairs={{0,1},{1,0},{2,6},{3,7},{4,5},{5,4},{6,2},{7,3},{8,9},{9,8},{10,14... | collective-permute-start | bytes 1769480 | tf_op jit(solution)/shard_map/ppermute | solution.py:674
  95.9 4.2 %collective-permute-start.11 = (bf16[4,192,384]{2,1,0:T(8,128)(2,1)S(1)}, bf16[4,192,384]{2,1,0:T(8,128)(2,1)S(1)}, u32[]{:S(2)}, u32[]{:S(2)}) collective-permute-start(bf16[4,192,384]{2,1,0:T(8,128)(2,1)S(1)} %get-tuple-element.179), channel_id=1, source_target_pairs={{0,2},{2,0},{4,6},{6,4},{8,10},{10,8},{12,14},{14,12},{16,18},{18,... | collective-permute-start | bytes 1769480 | tf_op jit(solution)/shard_map/ppermute | solution.py:664
  96.0 4.1 %collective-permute-start.12 = (bf16[4,192,384]{2,1,0:T(8,128)(2,1)S(1)}, bf16[4,192,384]{2,1,0:T(8,128)(2,1)S(1)}, u32[]{:S(2)}, u32[]{:S(2)}) collective-permute-start(bf16[4,192,384]{2,1,0:T(8,128)(2,1)S(1)} %get-tuple-element.180), channel_id=1, source_target_pairs={{0,2},{2,0},{4,6},{6,4},{8,10},{10,8},{12,14},{14,12},{16,18},{18,... | collective-permute-start | bytes 1769480 | tf_op jit(solution)/shard_map/ppermute | solution.py:664
  96.5 2.4 %collective-permute-start.13 = (f32[32,384]{1,0:T(8,128)S(1)}, f32[32,384]{1,0:T(8,128)S(1)}, u32[]{:S(2)}, u32[]{:S(2)}) collective-permute-start(f32[32,384]{1,0:T(8,128)S(1)} %get-tuple-element.181.refs_17_), channel_id=1, source_target_pairs={{0,2},{2,0},{4,6},{6,4},{8,10},{10,8},{12,14},{14,12},{16,18},{18,... | collective-permute-start | bytes 147464 | tf_op jit(solution)/shard_map/ppermute | solution.py:664
  101.2 16.5 %collective-permute-start.14 = (bf16[1568,384]{1,0:T(8,128)(2,1)S(1)}, bf16[1568,384]{1,0:T(8,128)(2,1)S(1)}, u32[]{:S(2)}, u32[]{:S(2)}) collective-permute-start(bf16[1568,384]{1,0:T(8,128)(2,1)S(1)} %get-tuple-element.187), channel_id=1, source_target_pairs={{0,4},{1,5},{2,3},{3,2},{4,0},{5,1},{6,7},{7,6},{8,12},{9,13},{10,... | collective-permute-start | bytes 3612680 | tf_op jit(solution)/shard_map/ppermute | solution.py:674
  102.7 12.6 %collective-permute-start.15 = (bf16[4,192,384]{2,1,0:T(8,128)(2,1)S(1)}, bf16[4,192,384]{2,1,0:T(8,128)(2,1)S(1)}, u32[]{:S(2)}, u32[]{:S(2)}) collective-permute-start(bf16[4,192,384]{2,1,0:T(8,128)(2,1)S(1)} %get-tuple-element.189), channel_id=1, source_target_pairs={{0,2},{2,0},{4,6},{6,4},{8,10},{10,8},{12,14},{14,12},{16,18},{18,... | collective-permute-start | bytes 1769480 | tf_op jit(solution)/shard_map/ppermute | solution.py:664
  102.7 12.6 %collective-permute-start.16 = (bf16[4,192,384]{2,1,0:T(8,128)(2,1)S(1)}, bf16[4,192,384]{2,1,0:T(8,128)(2,1)S(1)}, u32[]{:S(2)}, u32[]{:S(2)}) collective-permute-start(bf16[4,192,384]{2,1,0:T(8,128)(2,1)S(1)} %get-tuple-element.191), channel_id=1, source_target_pairs={{0,2},{2,0},{4,6},{6,4},{8,10},{10,8},{12,14},{14,12},{16,18},{18,... | collective-permute-start | bytes 1769480 | tf_op jit(solution)/shard_map/ppermute | solution.py:664
  103.2 12.1 %collective-permute-start.17 = (bf16[384,384]{1,0:T(8,128)(2,1)S(1)}, bf16[384,384]{1,0:T(8,128)(2,1)S(1)}, u32[]{:S(2)}, u32[]{:S(2)}) collective-permute-start(bf16[384,384]{1,0:T(8,128)(2,1)S(1)} %get-tuple-element.192), channel_id=1, source_target_pairs={{0,8},{1,9},{2,10},{3,11},{4,12},{5,13},{6,14},{7,15},{8,0},{9,1},... | collective-permute-start | bytes 884744 | tf_op jit(solution)/shard_map/ppermute | solution.py:674
  104.8 9.6 %collective-permute-start.18 = (bf16[192,384]{1,0:T(8,128)(2,1)S(1)}, bf16[192,384]{1,0:T(8,128)(2,1)S(1)}, u32[]{:S(2)}, u32[]{:S(2)}) collective-permute-start(bf16[192,384]{1,0:T(8,128)(2,1)S(1)} %get-tuple-element.193), channel_id=1, source_target_pairs={{0,16},{1,17},{2,18},{3,19},{4,20},{5,21},{6,22},{7,23},{8,24},{9,... | collective-permute-start | bytes 442376 | tf_op jit(solution)/shard_map/ppermute | solution.py:674
  118.6 10.2 %collective-permute-start.19 = (bf16[800,384]{1,0:T(8,128)(2,1)S(1)}, bf16[800,384]{1,0:T(8,128)(2,1)S(1)}, u32[]{:S(2)}, u32[]{:S(2)}) collective-permute-start(bf16[800,384]{1,0:T(8,128)(2,1)S(1)} %get-tuple-element.202), channel_id=1, source_target_pairs={{0,1},{1,0},{2,6},{3,7},{4,5},{5,4},{6,2},{7,3},{8,9},{9,8},{10,14... | collective-permute-start | bytes 1843208 | tf_op jit(solution)/shard_map/ppermute | solution.py:674
  119.4 8.4 %collective-permute-start.20 = (bf16[192,384]{1,0:T(8,128)(2,1)S(1)}, bf16[192,384]{1,0:T(8,128)(2,1)S(1)}, u32[]{:S(2)}, u32[]{:S(2)}) collective-permute-start(bf16[192,384]{1,0:T(8,128)(2,1)S(1)} %get-tuple-element.203), channel_id=1, source_target_pairs={{0,16},{1,17},{2,18},{3,19},{4,20},{5,21},{6,22},{7,23},{8,24},{9,... | collective-permute-start | bytes 442376 | tf_op jit(solution)/shard_map/ppermute | solution.py:674
  129.5 7.5 %collective-permute-start.21 = (bf16[416,384]{1,0:T(8,128)(2,1)S(1)}, bf16[416,384]{1,0:T(8,128)(2,1)S(1)}, u32[]{:S(2)}, u32[]{:S(2)}) collective-permute-start(bf16[416,384]{1,0:T(8,128)(2,1)S(1)} %get-tuple-element.210), channel_id=1, source_target_pairs={{0,8},{1,9},{2,10},{3,11},{4,12},{5,13},{6,14},{7,15},{8,0},{9,1},... | collective-permute-start | bytes 958472 | tf_op jit(solution)/shard_map/ppermute | solution.py:674
  131.1 10.2 %collective-permute-start.23 = (bf16[256,768]{1,0:T(8,128)(2,1)S(1)}, bf16[256,768]{1,0:T(8,128)(2,1)S(1)}, u32[]{:S(2)}, u32[]{:S(2)}) collective-permute-start(bf16[256,768]{1,0:T(8,128)(2,1)S(1)} %get-tuple-element.218), channel_id=1, source_target_pairs={{0,1},{1,0},{2,3},{3,2},{4,5},{5,4},{6,7},{7,6},{8,9},{9,8},{10,11... | collective-permute-start | bytes 1179656 | tf_op jit(solution)/shard_map/ppermute | solution.py:663
  131.9 11.5 %collective-permute-start.24 = (bf16[128,768]{1,0:T(8,128)(2,1)S(1)}, bf16[128,768]{1,0:T(8,128)(2,1)S(1)}, u32[]{:S(2)}, u32[]{:S(2)}) collective-permute-start(bf16[128,768]{1,0:T(8,128)(2,1)S(1)} %get-tuple-element.222), channel_id=1, source_target_pairs={{0,1},{1,0},{2,3},{3,2},{4,5},{5,4},{6,7},{7,6},{8,9},{9,8},{10,11... | collective-permute-start | bytes 589832 | tf_op jit(solution)/shard_map/ppermute | solution.py:663
  137.6 8.2 %collective-permute-start.22 = (bf16[224,384]{1,0:T(8,128)(2,1)S(1)}, bf16[224,384]{1,0:T(8,128)(2,1)S(1)}, u32[]{:S(2)}, u32[]{:S(2)}) collective-permute-start(bf16[224,384]{1,0:T(8,128)(2,1)S(1)} %get-tuple-element.215), channel_id=1, source_target_pairs={{0,16},{1,17},{2,18},{3,19},{4,20},{5,21},{6,22},{7,23},{8,24},{9,... | collective-permute-start | bytes 516104 | tf_op jit(solution)/shard_map/ppermute | solution.py:674
